TPU v7x, 32 devices: a whole 2x2x4 slice. The times are simulated.
32 devices in a mesh: dp: 4 (over x, core), seq: 8 (over z, y).
Axes of the slice: x: 2, y: 2, z: 4, core: 2. Of those that a mesh axis runs over, the one named last changes fastest.
Arguments:
- hidden_in: bfloat16 [4, 1024, 2048], P('dp', 'seq'), may hold values from -6 to 6
- segment_ids: int32 [4, 1024], P('dp'), may hold values from 0 to 3, never falling along the last dimension, each value on 1 to 512 neighbouring positions
- routes: int32 [4, 1024, 8], P('dp', 'seq'), may hold values from 0 to 15, all different within a row; in each aligned block of 128 rows (0 to 127, 128 to 255, ..., all dimensions but the last counted through in order) at most 96 rows name the same one
- w_query: bfloat16 [2048, 2048], P(('dp', 'seq')), may hold values from -0.125 to 0.125
- w_key: bfloat16 [2048, 2048], P(('dp', 'seq')), may hold values from -0.125 to 0.125
- w_value: bfloat16 [2048, 2048], P(('dp', 'seq')), may hold values from -0.125 to 0.125
- w_out: bfloat16 [2048, 2048], P(('dp', 'seq')), may hold values from -0.5 to 0.5
- gain_attn: bfloat16 [2048], P(('dp', 'seq')), may hold values from 0.099609375 to 1.8984375
- gain_query: bfloat16 [2048], P(('dp', 'seq')), may hold values from 0.796875 to 2
- gain_key: bfloat16 [2048], P(('dp', 'seq')), may hold values from 0.796875 to 2
- gain_ffn: bfloat16 [2048], P(('dp', 'seq')), may hold values from 0.099609375 to 1.8984375
- w_router: bfloat16 [2048, 16], P(('dp', 'seq')), may hold values from -0.0625 to 0.0625
- w_gate: bfloat16 [16, 2048, 1024], P('seq', 'dp'), may hold values from -0.125 to 0.125
- w_up: bfloat16 [16, 2048, 1024], P('seq', 'dp'), may hold values from -0.125 to 0.125
- w_down: bfloat16 [16, 1024, 2048], P('seq', None, 'dp'), may hold values from -6 to 6
- cotangent: bfloat16 [4, 1024, 2048], P('dp', 'seq'), may hold values from -6 to 6
Outputs:
- block_out: bfloat16 [4, 1024, 2048], P('dp', 'seq')
- grad_hidden: float32 [4, 1024, 2048], P('dp', 'seq')
- grad_query: float32 [2048, 2048], P(('dp', 'seq'))
- grad_key: float32 [2048, 2048], P(('dp', 'seq'))
- grad_value: float32 [2048, 2048], P(('dp', 'seq'))
- grad_out_proj: float32 [2048, 2048], P(('dp', 'seq'))
- grad_gain_attn: float32 [2048], P(('dp', 'seq'))
- grad_gain_query: float32 [2048], P(('dp', 'seq'))
- grad_gain_key: float32 [2048], P(('dp', 'seq'))
- grad_gain_ffn: float32 [2048], P(('dp', 'seq'))
- grad_router: float32 [2048, 16], P(('dp', 'seq'))
- grad_gate: float32 [16, 2048, 1024], P('seq', 'dp')
- grad_up: float32 [16, 2048, 1024], P('seq', 'dp')
- grad_down: float32 [16, 1024, 2048], P('seq', None, 'dp')
Inputs may be any that keep to these rules, and one draw needn't show every extreme that they name: `routes`: within the rows of one device (aligned blocks of 128 tokens of the flattened rows), each expert is named by at most 96 token choices; a token's 8 experts are distinct. `segment_ids`: file numbers never fall along a row; each file is a run of 1 to 512 positions.
All inputs are finite; a program needn't handle non-finite values.
Results may differ from a plain program's by a relative error of at most 0.02.
Values may be sent and summed in bfloat16 or wider, within the bound.
No kernel may reach another device: no remote copies, remote signals or barrier semaphores. Data moves between devices by JAX's collectives and lax.ppermute only.
A program may use at most 448 MiB of HBM per device.

v0:
```python
import math

import jax
import jax.numpy as jnp
from jax import lax
from jax.sharding import PartitionSpec as P

HEAD = 128


epsilon = 1e-05
masked_score = -1e30
rope_base = 10000.0


def normalize(values, gain_vec):
    return (
        values * lax.rsqrt(jnp.mean(values * values, axis=-1, keepdims=True) + epsilon) * gain_vec
    )


def rotary(values, positions):
    half_dim = values.shape[-1] // 2
    frequency = jnp.exp(
        jnp.arange(half_dim, dtype=jnp.float32) * (-2.0 * math.log(rope_base) / values.shape[-1])
    )
    angles = positions.astype(jnp.float32)[:, None] * frequency[None, :]
    cosine = jnp.cos(angles)[:, None, :]
    sine_table = jnp.sin(angles)[:, None, :]
    first_half = values[..., :half_dim]
    second = values[..., half_dim:]
    return jnp.concatenate(
        [first_half * cosine - second * sine_table, second * cosine + first_half * sine_table],
        axis=-1,
    )


def softmax_rows(values):
    peak_value = jnp.max(values, axis=-1, keepdims=True)
    raised = jnp.exp(values - peak_value)
    return raised / jnp.sum(raised, axis=-1, keepdims=True)


def rotate_normed(projection, gain_vec, positions):
    tokens, model_width = projection.shape
    return rotary(
        normalize(projection, gain_vec).reshape(tokens, model_width // HEAD, HEAD), positions
    )


def masked_scores(queries, key_block, query_pos, query_seg, key_pos, key_seg, scaling):
    raw_scores = jnp.einsum("qhd,khd->hqk", queries, key_block, preferred_element_type=jnp.float32)
    allowed = (query_pos[:, None] >= key_pos[None, :]) & (query_seg[:, None] == key_seg[None, :])
    return jnp.where(allowed[None], raw_scores * scaling, masked_score)


def key_window(keys_all, values_all, row_seg, begin_at, span):
    key_block = lax.dynamic_slice_in_dim(keys_all, begin_at, span)
    value_block = lax.dynamic_slice_in_dim(values_all, begin_at, span)
    key_pos = begin_at + lax.iota(jnp.int32, span)
    key_seg = lax.dynamic_slice_in_dim(row_seg, begin_at, span)
    return (key_block, value_block, key_pos, key_seg)


def project_front(hidden, layer_full, positions):
    tokens, model_width = hidden.shape
    normed = normalize(hidden, layer_full[5].astype(jnp.float32)).astype(jnp.bfloat16)
    query = jnp.dot(normed, layer_full[0], preferred_element_type=jnp.float32)
    key_proj = jnp.dot(normed, layer_full[1], preferred_element_type=jnp.float32)
    value_proj = jnp.dot(normed, layer_full[2], preferred_element_type=jnp.float32)
    query_rot = rotate_normed(query, layer_full[6].astype(jnp.float32), positions).astype(
        jnp.bfloat16
    )
    key_rot = rotate_normed(key_proj, layer_full[7].astype(jnp.float32), positions).astype(
        jnp.bfloat16
    )
    value_in = value_proj.astype(jnp.bfloat16).reshape(tokens, model_width // HEAD, HEAD)
    return (normed, query, key_proj, query_rot, key_rot, value_in)


def attend_local(query_rot, keys_all, values_all, row_seg, offset, span):
    tokens, head_count, head_dim = query_rot.shape
    scaling = head_dim ** (-0.5)
    query_pos = offset + lax.iota(jnp.int32, tokens)
    query_seg = lax.dynamic_slice_in_dim(row_seg, offset, tokens)
    reach_blocks = (offset + tokens + span - 1) // span

    def block_scores(block_index):
        begin_at = block_index * span
        key_block, value_block, key_pos, key_seg = key_window(
            keys_all, values_all, row_seg, begin_at, span
        )
        return (
            masked_scores(query_rot, key_block, query_pos, query_seg, key_pos, key_seg, scaling),
            value_block,
        )

    def first_pass(block_index, state_pair):
        peak_value, denominator = state_pair
        scores, unused_values = block_scores(block_index)
        new_peak = jnp.maximum(peak_value, jnp.max(scores, axis=-1))
        denominator = denominator * jnp.exp(peak_value - new_peak) + jnp.sum(
            jnp.exp(scores - new_peak[..., None]), axis=-1
        )
        return (new_peak, denominator)

    start_state = (
        jnp.full((head_count, tokens), masked_score, jnp.float32),
        jnp.zeros((head_count, tokens), jnp.float32),
    )
    peak_value, denominator = lax.fori_loop(0, reach_blocks, first_pass, start_state)
    log_total = peak_value + jnp.log(denominator)

    def second_pass(block_index, running):
        scores, value_block = block_scores(block_index)
        weights = jnp.exp(scores - log_total[..., None]).astype(jnp.bfloat16)
        return running + jnp.einsum(
            "hqk,khd->qhd", weights, value_block, preferred_element_type=jnp.float32
        )

    attention = lax.fori_loop(
        0, reach_blocks, second_pass, jnp.zeros((tokens, head_count, head_dim), jnp.float32)
    )
    return (attention, log_total)


def query_grads(query_rot, keys_all, values_all, row_seg, offset, span, log_total, grad_attended):
    tokens, head_count, head_dim = query_rot.shape
    scaling = head_dim ** (-0.5)
    query_pos = offset + lax.iota(jnp.int32, tokens)
    query_seg = lax.dynamic_slice_in_dim(row_seg, offset, tokens)
    reach_blocks = (offset + tokens + span - 1) // span

    def block_terms(block_index):
        begin_at = block_index * span
        key_block, value_block, key_pos, key_seg = key_window(
            keys_all, values_all, row_seg, begin_at, span
        )
        scores = masked_scores(
            query_rot, key_block, query_pos, query_seg, key_pos, key_seg, scaling
        )
        weights = jnp.exp(scores - log_total[..., None])
        grad_weights = jnp.einsum(
            "qhd,khd->hqk", grad_attended, value_block, preferred_element_type=jnp.float32
        )
        return (key_block, weights, grad_weights)

    def delta_pass(block_index, running):
        unused_keys, weights, grad_weights = block_terms(block_index)
        return running + jnp.sum(weights * grad_weights, axis=-1)

    delta = lax.fori_loop(0, reach_blocks, delta_pass, jnp.zeros((head_count, tokens), jnp.float32))

    def query_pass(block_index, running):
        key_block, weights, grad_weights = block_terms(block_index)
        grad_scores = (weights * (grad_weights - delta[..., None]) * scaling).astype(jnp.bfloat16)
        return running + jnp.einsum(
            "hqk,khd->qhd", grad_scores, key_block, preferred_element_type=jnp.float32
        )

    grad_query_rot = lax.fori_loop(
        0, reach_blocks, query_pass, jnp.zeros((tokens, head_count, head_dim), jnp.float32)
    )
    return (delta, grad_query_rot)


def route_tokens(hidden_mid, layer_full, choice_rows):
    tokens, pick_count = choice_rows.shape
    normed_ffn = normalize(hidden_mid, layer_full[8].astype(jnp.float32)).astype(jnp.bfloat16)
    logits = jnp.dot(normed_ffn, layer_full[4], preferred_element_type=jnp.float32)
    expert_count = logits.shape[1]
    capacity = 3 * tokens * pick_count // (2 * expert_count)
    chances = softmax_rows(logits)
    picks = choice_rows[:, :, None] == lax.iota(jnp.int32, expert_count)[None, None, :]
    gate_values = jnp.sum(jnp.where(picks, chances[:, None, :], 0.0), axis=-1)
    flat_hits = picks.reshape(tokens * pick_count, expert_count).astype(jnp.int32)
    earlier = jnp.cumsum(flat_hits, axis=0) - flat_hits
    slot_ids = choice_rows.reshape(-1) * capacity + jnp.sum(earlier * flat_hits, axis=1)
    pair_table = lax.iota(jnp.int32, expert_count * capacity)[:, None] == slot_ids[None, :]
    spread = jnp.sum(
        pair_table.reshape(expert_count * capacity, tokens, pick_count).astype(jnp.int32), axis=2
    ).astype(jnp.bfloat16)
    send_rows = jnp.dot(spread, normed_ffn, preferred_element_type=jnp.float32).astype(jnp.bfloat16)
    send_rows = send_rows.reshape(expert_count, capacity, hidden_mid.shape[1])
    return (normed_ffn, chances, picks, gate_values, slot_ids, pair_table, spread, send_rows)


def group_rows(row_block, held_experts):
    sources = row_block.shape[0] // held_experts
    grouped = row_block.reshape(
        sources, held_experts, row_block.shape[1], row_block.shape[2]
    ).transpose(1, 0, 2, 3)
    return grouped.reshape(held_experts, sources * row_block.shape[1], row_block.shape[2])


def ungroup_rows(grouped, whole_shape):
    held_experts = grouped.shape[0]
    sources = whole_shape[0] // held_experts
    spread_out = grouped.reshape(held_experts, sources, whole_shape[1], whole_shape[2]).transpose(
        1, 0, 2, 3
    )
    return spread_out.reshape(whole_shape)


def expert_forward(row_block, gate_full, up_full, down_full):
    inputs = group_rows(row_block, gate_full.shape[0])
    gate_pre = jnp.einsum("erd,edf->erf", inputs, gate_full, preferred_element_type=jnp.float32)
    up_pre = jnp.einsum("erd,edf->erf", inputs, up_full, preferred_element_type=jnp.float32)
    activated = (gate_pre * lax.logistic(gate_pre) * up_pre).astype(jnp.bfloat16)
    result = jnp.einsum(
        "erf,efd->erd", activated, down_full, preferred_element_type=jnp.float32
    ).astype(jnp.bfloat16)
    return ungroup_rows(result, row_block.shape)


def expert_backward(row_block, grad_block, gate_full, up_full, down_full):
    inputs = group_rows(row_block, gate_full.shape[0])
    grad_outputs = group_rows(grad_block, gate_full.shape[0])
    gate_pre = jnp.einsum("erd,edf->erf", inputs, gate_full, preferred_element_type=jnp.float32)
    up_pre = jnp.einsum("erd,edf->erf", inputs, up_full, preferred_element_type=jnp.float32)
    sigmoid_gate = lax.logistic(gate_pre)
    activated = (gate_pre * sigmoid_gate * up_pre).astype(jnp.bfloat16)
    grad_act = jnp.einsum(
        "erd,efd->erf", grad_outputs, down_full, preferred_element_type=jnp.float32
    )
    grad_down = jnp.einsum(
        "erf,erd->efd", activated, grad_outputs, preferred_element_type=jnp.float32
    )
    grad_gate_pre = (
        grad_act * up_pre * sigmoid_gate * (1.0 + gate_pre * (1.0 - sigmoid_gate))
    ).astype(jnp.bfloat16)
    grad_up_pre = (grad_act * gate_pre * sigmoid_gate).astype(jnp.bfloat16)
    grad_gate_w = jnp.einsum(
        "erd,erf->edf", inputs, grad_gate_pre, preferred_element_type=jnp.float32
    )
    grad_up_w = jnp.einsum("erd,erf->edf", inputs, grad_up_pre, preferred_element_type=jnp.float32)
    grad_inputs = jnp.einsum(
        "erf,edf->erd", grad_gate_pre, gate_full, preferred_element_type=jnp.float32
    )
    grad_inputs = grad_inputs + jnp.einsum(
        "erf,edf->erd", grad_up_pre, up_full, preferred_element_type=jnp.float32
    )
    return (
        ungroup_rows(grad_inputs.astype(jnp.bfloat16), row_block.shape),
        grad_gate_w,
        grad_up_w,
        grad_down,
    )


def contract_rows(left, right):
    return lax.dot_general(
        left, right, (((0,), (0,)), ((), ())), preferred_element_type=jnp.float32
    )


def contract_cols(left, right):
    return lax.dot_general(
        left, right, (((1,), (1,)), ((), ())), preferred_element_type=jnp.float32
    )


def on_device(
    hidden_in,
    segment_ids,
    routes,
    w_query,
    w_key,
    w_value,
    w_out,
    gain_attn,
    gain_query,
    gain_key,
    gain_ffn,
    w_router,
    w_gate,
    w_up,
    w_down,
    cotangent,
):
    hidden = hidden_in[0].astype(jnp.float32)
    tokens, model_width = hidden.shape
    head_count = model_width // HEAD
    row_seg = segment_ids[0]
    choice_rows = routes[0]
    offset = lax.axis_index("seq") * tokens
    positions = offset + lax.iota(jnp.int32, tokens)
    span = min(512, row_seg.shape[0])
    layer_full = (
        lax.all_gather(w_query, ("dp", "seq"), axis=0, tiled=True),
        lax.all_gather(w_key, ("dp", "seq"), axis=0, tiled=True),
        lax.all_gather(w_value, ("dp", "seq"), axis=0, tiled=True),
        lax.all_gather(w_out, ("dp", "seq"), axis=0, tiled=True),
        lax.all_gather(w_router, ("dp", "seq"), axis=0, tiled=True),
        lax.all_gather(gain_attn, ("dp", "seq"), axis=0, tiled=True),
        lax.all_gather(gain_query, ("dp", "seq"), axis=0, tiled=True),
        lax.all_gather(gain_key, ("dp", "seq"), axis=0, tiled=True),
        lax.all_gather(gain_ffn, ("dp", "seq"), axis=0, tiled=True),
    )
    expert_full = (
        lax.all_gather(w_gate, "dp", axis=1, tiled=True),
        lax.all_gather(w_up, "dp", axis=1, tiled=True),
        lax.all_gather(w_down, "dp", axis=2, tiled=True),
    )
    projected = project_front(hidden, layer_full, positions)
    keys_all, values_all = (
        lax.all_gather(projected[4], "seq", axis=0, tiled=True),
        lax.all_gather(projected[5], "seq", axis=0, tiled=True),
    )
    attention, log_total = attend_local(projected[3], keys_all, values_all, row_seg, offset, span)
    attended = attention.reshape(tokens, model_width).astype(jnp.bfloat16)
    hidden_mid = hidden + jnp.dot(attended, layer_full[3], preferred_element_type=jnp.float32)
    routing = route_tokens(hidden_mid, layer_full, choice_rows)
    expert_count, capacity = (routing[7].shape[0], routing[7].shape[1])
    expert_out = expert_forward(
        lax.all_to_all(routing[7], "seq", split_axis=0, concat_axis=0, tiled=True),
        expert_full[0],
        expert_full[1],
        expert_full[2],
    )
    returned = lax.all_to_all(expert_out, "seq", split_axis=0, concat_axis=0, tiled=True)
    picked = jnp.take(returned.reshape(expert_count * capacity, model_width), routing[4], axis=0)
    picked = picked.reshape(tokens, choice_rows.shape[1], model_width)
    mixture = jnp.sum(routing[3][:, :, None] * picked.astype(jnp.float32), axis=1)
    block_out = (hidden_mid + mixture).astype(jnp.bfloat16)
    layer_full = (
        lax.all_gather(w_query, ("dp", "seq"), axis=0, tiled=True),
        lax.all_gather(w_key, ("dp", "seq"), axis=0, tiled=True),
        lax.all_gather(w_value, ("dp", "seq"), axis=0, tiled=True),
        lax.all_gather(w_out, ("dp", "seq"), axis=0, tiled=True),
        lax.all_gather(w_router, ("dp", "seq"), axis=0, tiled=True),
        lax.all_gather(gain_attn, ("dp", "seq"), axis=0, tiled=True),
        lax.all_gather(gain_query, ("dp", "seq"), axis=0, tiled=True),
        lax.all_gather(gain_key, ("dp", "seq"), axis=0, tiled=True),
        lax.all_gather(gain_ffn, ("dp", "seq"), axis=0, tiled=True),
    )
    expert_full = (
        lax.all_gather(w_gate, "dp", axis=1, tiled=True),
        lax.all_gather(w_up, "dp", axis=1, tiled=True),
        lax.all_gather(w_down, "dp", axis=2, tiled=True),
    )
    projected = project_front(hidden, layer_full, positions)
    keys_all, values_all = (
        lax.all_gather(projected[4], "seq", axis=0, tiled=True),
        lax.all_gather(projected[5], "seq", axis=0, tiled=True),
    )
    attention, log_total = attend_local(projected[3], keys_all, values_all, row_seg, offset, span)
    attended = attention.reshape(tokens, model_width).astype(jnp.bfloat16)
    hidden_mid = hidden + jnp.dot(attended, layer_full[3], preferred_element_type=jnp.float32)
    routing = route_tokens(hidden_mid, layer_full, choice_rows)
    normed_ffn, chances, picks, gate_values, slot_ids, pair_table, spread, send_rows = routing
    grad_out = cotangent[0].astype(jnp.float32)
    grad_gates = jnp.sum(grad_out[:, None, :] * picked.astype(jnp.float32), axis=-1)
    slot_gates = jnp.sum(jnp.where(pair_table, gate_values.reshape(-1)[None, :], 0.0), axis=1)
    grad_rows_in = jnp.dot(spread, cotangent[0], preferred_element_type=jnp.float32)
    grad_slots = (
        (slot_gates[:, None] * grad_rows_in)
        .astype(jnp.bfloat16)
        .reshape(expert_count, capacity, model_width)
    )
    arrived_rows, arrived_grads = (
        lax.all_to_all(send_rows, "seq", split_axis=0, concat_axis=0, tiled=True),
        lax.all_to_all(grad_slots, "seq", split_axis=0, concat_axis=0, tiled=True),
    )
    grad_inputs, grad_gate_w, grad_up_w, grad_down_w = expert_backward(
        arrived_rows, arrived_grads, expert_full[0], expert_full[1], expert_full[2]
    )
    grad_back = lax.all_to_all(grad_inputs, "seq", split_axis=0, concat_axis=0, tiled=True)
    grad_normed_ffn = contract_rows(spread, grad_back.reshape(expert_count * capacity, model_width))
    grad_chances = jnp.sum(jnp.where(picks, grad_gates[:, :, None], 0.0), axis=1)
    grad_logits = (
        chances * (grad_chances - jnp.sum(chances * grad_chances, axis=-1, keepdims=True))
    ).astype(jnp.bfloat16)
    grad_router_w = contract_rows(normed_ffn, grad_logits)
    grad_normed_ffn = grad_normed_ffn + contract_cols(grad_logits, layer_full[4])
    unused_ffn, pull_ffn = jax.vjp(normalize, hidden_mid, layer_full[8].astype(jnp.float32))
    grad_mid_norm, grad_gain_ffn_w = pull_ffn(grad_normed_ffn)
    grad_mid = grad_out + grad_mid_norm
    grad_mid_low = grad_mid.astype(jnp.bfloat16)
    grad_w_out = contract_rows(attended, grad_mid_low)
    grad_attended = (
        contract_cols(grad_mid_low, layer_full[3])
        .astype(jnp.bfloat16)
        .reshape(tokens, head_count, HEAD)
    )
    query_rot = projected[3]
    delta, grad_query_rot = query_grads(
        query_rot, keys_all, values_all, row_seg, offset, span, log_total, grad_attended
    )
    scaling = HEAD ** (-0.5)
    query_seg = lax.dynamic_slice_in_dim(row_seg, offset, tokens)
    row_count = lax.axis_size("seq") * tokens
    step_rows = math.gcd(row_count, 512)

    def one_window(window_index, running):
        window_start = window_index * step_rows
        key_block, value_block, key_pos, key_seg = key_window(
            keys_all, values_all, row_seg, window_start, step_rows
        )
        scores = masked_scores(
            query_rot, key_block, positions, query_seg, key_pos, key_seg, scaling
        )
        weights = jnp.exp(scores - log_total[..., None])
        grad_weights = jnp.einsum(
            "qhd,khd->hqk", grad_attended, value_block, preferred_element_type=jnp.float32
        )
        grad_scores = (weights * (grad_weights - delta[..., None]) * scaling).astype(jnp.bfloat16)
        grad_key_part = jnp.einsum(
            "hqk,qhd->khd", grad_scores, query_rot, preferred_element_type=jnp.float32
        )
        grad_value_part = jnp.einsum(
            "hqk,qhd->khd",
            weights.astype(jnp.bfloat16),
            grad_attended,
            preferred_element_type=jnp.float32,
        )
        term = jnp.concatenate(
            [
                grad_key_part.reshape(step_rows, model_width),
                grad_value_part.reshape(step_rows, model_width),
            ],
            axis=1,
        )
        return lax.dynamic_update_slice_in_dim(running, term, window_index * step_rows, 0)

    key_sums = lax.psum_scatter(
        lax.fori_loop(
            0,
            row_count // step_rows,
            one_window,
            jnp.zeros((row_count, 2 * model_width), jnp.float32),
        ).astype(jnp.bfloat16),
        "seq",
        scatter_dimension=0,
        tiled=True,
    ).astype(jnp.float32)
    grad_key_rot = key_sums[:, :model_width].reshape(tokens, head_count, HEAD)
    grad_v_low = key_sums[:, model_width:].astype(jnp.bfloat16)

    def query_chain(projection, gain_vec):
        return rotate_normed(projection, gain_vec, positions)

    unused_query, pull_query = jax.vjp(query_chain, projected[1], layer_full[6].astype(jnp.float32))
    grad_query_pre, grad_gain_query_w = pull_query(grad_query_rot)
    unused_key, pull_key = jax.vjp(query_chain, projected[2], layer_full[7].astype(jnp.float32))
    grad_key_pre, grad_gain_key_w = pull_key(grad_key_rot)
    grad_q_low = grad_query_pre.astype(jnp.bfloat16)
    grad_k_low = grad_key_pre.astype(jnp.bfloat16)
    normed = projected[0]
    grad_w_query = contract_rows(normed, grad_q_low)
    grad_w_key = contract_rows(normed, grad_k_low)
    grad_w_value = contract_rows(normed, grad_v_low)
    grad_normed = (
        contract_cols(grad_q_low, layer_full[0])
        + contract_cols(grad_k_low, layer_full[1])
        + contract_cols(grad_v_low, layer_full[2])
    )
    unused_attn, pull_attn = jax.vjp(normalize, hidden, layer_full[5].astype(jnp.float32))
    grad_hidden_norm, grad_gain_attn_w = pull_attn(grad_normed)
    grad_hidden = grad_mid + grad_hidden_norm
    shares = (
        lax.psum_scatter(grad_w_query, ("dp", "seq"), scatter_dimension=0, tiled=True),
        lax.psum_scatter(grad_w_key, ("dp", "seq"), scatter_dimension=0, tiled=True),
        lax.psum_scatter(grad_w_value, ("dp", "seq"), scatter_dimension=0, tiled=True),
        lax.psum_scatter(grad_w_out, ("dp", "seq"), scatter_dimension=0, tiled=True),
        lax.psum_scatter(grad_router_w, ("dp", "seq"), scatter_dimension=0, tiled=True),
        lax.psum_scatter(grad_gain_attn_w, ("dp", "seq"), scatter_dimension=0, tiled=True),
        lax.psum_scatter(grad_gain_query_w, ("dp", "seq"), scatter_dimension=0, tiled=True),
        lax.psum_scatter(grad_gain_key_w, ("dp", "seq"), scatter_dimension=0, tiled=True),
        lax.psum_scatter(grad_gain_ffn_w, ("dp", "seq"), scatter_dimension=0, tiled=True),
    )
    expert_shares = (
        lax.psum_scatter(
            grad_gate_w.astype(jnp.bfloat16), "dp", scatter_dimension=1, tiled=True
        ).astype(jnp.float32),
        lax.psum_scatter(
            grad_up_w.astype(jnp.bfloat16), "dp", scatter_dimension=1, tiled=True
        ).astype(jnp.float32),
        lax.psum_scatter(
            grad_down_w.astype(jnp.bfloat16), "dp", scatter_dimension=2, tiled=True
        ).astype(jnp.float32),
    )
    return (
        block_out[None],
        grad_hidden[None],
        shares[0],
        shares[1],
        shares[2],
        shares[3],
        shares[5],
        shares[6],
        shares[7],
        shares[8],
        shares[4],
        expert_shares[0],
        expert_shares[1],
        expert_shares[2],
    )


def solution(mesh):
    return jax.shard_map(
        on_device,
        mesh=mesh,
        in_specs=(
            P("dp", "seq", None),
            P("dp", None),
            P("dp", "seq", None),
            P(("dp", "seq"), None),
            P(("dp", "seq"), None),
            P(("dp", "seq"), None),
            P(("dp", "seq"), None),
            P(("dp", "seq")),
            P(("dp", "seq")),
            P(("dp", "seq")),
            P(("dp", "seq")),
            P(("dp", "seq"), None),
            P("seq", "dp", None),
            P("seq", "dp", None),
            P("seq", None, "dp"),
            P("dp", "seq", None),
        ),
        out_specs=(
            P("dp", "seq", None),
            P("dp", "seq", None),
            P(("dp", "seq"), None),
            P(("dp", "seq"), None),
            P(("dp", "seq"), None),
            P(("dp", "seq"), None),
            P(("dp", "seq")),
            P(("dp", "seq")),
            P(("dp", "seq")),
            P(("dp", "seq")),
            P(("dp", "seq"), None),
            P("seq", "dp", None),
            P("seq", "dp", None),
            P("seq", None, "dp"),
        ),
        check_vma=False,
    )
```

profile of v0, /device:TPU:0, one launch (start us, length us, event | category | flops | bytes accessed | tf_op | source)
XLA Modules:
  0.0 3253.8 jit_solution(7342092540080103934)
XLA Ops:
  12.9 42.6 %all-reduce.13 = (bf16[2048]{0:T(1024)(128)(2,1)S(1)}, bf16[2048]{0:T(1024)(128)(2,1)S(1)}, bf16[2048]{0:T(1024)(128)(2,1)S(1)}, bf16[2048]{0:T(1024)(128)(2,1)S(1)}) all-reduce(bf16[2048]{0:T(1024)(128)(2,1)S(1)} %dynamic-update-slice, bf16[2048]{0:T(1024)(128)(2,1)S(1)} %dynamic-update-slice.1, ...), channel_id=1, replica_groups=mesh['dp'=4,'seq'=8] {'dp','seq'}, use_global_device_ids=true, to_apply=%add.4 | all-reduce | flops 8192 | bytes 32768
  57.0 34.4 %all-gather.15.cloned.1.call-done = bf16[2048,2048]{1,0:T(8,128)(2,1)} async-done(((bf16[64,2048]{1,0:T(8,128)(2,1)}), bf16[2048,2048]{1,0:T(8,128)(2,1)}) %all-gather.15.cloned.1.call-update) | async-done | bytes 8388624 | tf_op jit(solution)/shard_map/all_gather | solution.py:291
  97.9 72.5 %all-gather.19.cloned.1.call-done = bf16[2048,2048]{1,0:T(8,128)(2,1)} async-done(((bf16[64,2048]{1,0:T(8,128)(2,1)}), bf16[2048,2048]{1,0:T(8,128)(2,1)}) %all-gather.19.cloned.1.call-update) | async-done | bytes 8388624 | tf_op jit(solution)/shard_map/all_gather | solution.py:290
  180.1 69.2 %all-gather.11.cloned.1.call-done = bf16[2048,2048]{1,0:T(8,128)(2,1)} async-done(((bf16[64,2048]{1,0:T(8,128)(2,1)}), bf16[2048,2048]{1,0:T(8,128)(2,1)}) %all-gather.11.cloned.1.call-update) | async-done | bytes 8388624 | tf_op jit(solution)/shard_map/all_gather | solution.py:292
  271.7 53.7 %all-gather.17.cloned.1.call-done = bf16[1024,16,128]{0,2,1:T(8,128)(2,1)} async-done(((bf16[128,16,128]{0,2,1:T(8,128)(2,1)}), bf16[1024,16,128]{0,2,1:T(8,128)(2,1)}) %all-gather.17.cloned.1.call-update) | async-done | bytes 4194320 | tf_op jit(solution)/shard_map/all_gather | solution.py:307
  335.7 63.8 %all-gather.13.cloned.1.call-done = bf16[1024,16,128]{2,1,0:T(8,128)(2,1)} async-done(((bf16[128,16,128]{2,1,0:T(8,128)(2,1)}), bf16[1024,16,128]{2,1,0:T(8,128)(2,1)}) %all-gather.13.cloned.1.call-update) | async-done | bytes 4194320 | tf_op jit(solution)/shard_map/all_gather | solution.py:308
  411.5 66.5 %all-gather.21.cloned.1.call-done = bf16[2048,2048]{1,0:T(8,128)(2,1)} async-done(((bf16[64,2048]{1,0:T(8,128)(2,1)}), bf16[2048,2048]{1,0:T(8,128)(2,1)}) %all-gather.21.cloned.1.call-update) | async-done | bytes 8388624 | tf_op jit(solution)/shard_map/all_gather | solution.py:293
  493.4 138.1 %all-to-all-done = bf16[16,96,2048]{2,1,0:T(8,128)(2,1)} async-done(((bf16[16,96,2048]{2,1,0:T(8,128)(2,1)}), bf16[16,96,2048]{2,1,0:T(8,128)(2,1)}, u32[]{:S(2)}, u32[]{:S(2)}) %all-to-all-start) | async-done | bytes 6291488 | tf_op jit(solution)/shard_map/all_to_all | solution.py:316
  651.0 14.8 multiply_convert_fusion.3
  684.8 193.7 %all-gather = bf16[32,64,16]{1,2,0:T(8,128)(2,1)S(1)} all-gather(bf16[1,64,16]{1,2,0:T(8,128)(2,1)S(1)} %bitcast.323), channel_id=1, replica_groups=mesh['dp'=4,'seq'=8] {'dp','seq'}, dimensions={0}, use_global_device_ids=true | all-gather | bytes 67584 | tf_op jit(solution)/shard_map/all_gather | solution.py:294
  899.2 139.6 %all_to_all.21 = bf16[16,96,2048]{2,1,0:T(8,128)(2,1)S(1)} all-to-all(bf16[16,96,2048]{2,1,0:T(8,128)(2,1)S(1)} %bitcast.295), channel_id=1, replica_groups=mesh['dp'=4,'seq'=8] {'seq'}, dimensions={0} | all-to-all | bytes 12582912 | tf_op jit(solution)/shard_map/all_to_all | solution.py:363
  1042.0 16.2 multiply_convert_fusion.1
  1107.9 126.5 %all-to-all-done.3 = bf16[16,96,2048]{2,1,0:T(8,128)(2,1)} async-done(((bf16[16,96,2048]{2,1,0:T(8,128)(2,1)}), bf16[16,96,2048]{2,1,0:T(8,128)(2,1)}, u32[]{:S(2)}, u32[]{:S(2)}) %all-to-all-start.3) | async-done | bytes 6291488 | tf_op jit(solution)/shard_map/all_to_all | solution.py:368
  1253.8 31.7 while.73
  1357.4 90.6 %reduce-scatter.28.cloned.1.call-done = bf16[128,4096]{1,0:T(8,128)(2,1)} async-done(((bf16[1024,4096]{1,0:T(8,128)(2,1)}), bf16[128,4096]{1,0:T(8,128)(2,1)}) %reduce-scatter.28.cloned.1.call-update) | async-done | bytes 1048592
  1489.2 95.3 %reduce-scatter.30.cloned.1.call-done = f32[64,16]{1,0:T(8,128)} async-done(((f32[2048,16]{1,0:T(8,128)}), f32[64,16]{1,0:T(8,128)}) %reduce-scatter.30.cloned.1.call-update) | async-done | bytes 4112
  1585.9 69.2 %reduce-scatter.26.cloned.1.call-done = bf16[2,1024,512]{2,1,0:T(8,128)(2,1)} async-done(((bf16[2,1024,2048]{2,1,0:T(8,128)(2,1)}), bf16[2,1024,512]{2,1,0:T(8,128)(2,1)}) %reduce-scatter.26.cloned.1.call-update) | async-done | bytes 2097168 | tf_op jit(solution)/shard_map/reduce_scatter | solution.py:479
  1659.4 70.3 %reduce-scatter.22.cloned.1.call-done = bf16[2,512,1024]{2,1,0:T(8,128)(2,1)} async-done(((bf16[2,2048,1024]{2,1,0:T(8,128)(2,1)}), bf16[2,512,1024]{2,1,0:T(8,128)(2,1)}) %reduce-scatter.22.cloned.1.call-update) | async-done | bytes 2097168 | tf_op jit(solution)/shard_map/reduce_scatter | solution.py:473
  1733.7 70.1 %reduce-scatter.24.cloned.1.call-done = bf16[2,512,1024]{2,1,0:T(8,128)(2,1)} async-done(((bf16[2,2048,1024]{2,1,0:T(8,128)(2,1)}), bf16[2,512,1024]{2,1,0:T(8,128)(2,1)}) %reduce-scatter.24.cloned.1.call-update) | async-done | bytes 2097168 | tf_op jit(solution)/shard_map/reduce_scatter | solution.py:476
  1820.6 46.6 %all-reduce.12 = (f32[2048]{0:T(1024)S(1)}, f32[2048]{0:T(1024)S(1)}, f32[2048]{0:T(1024)S(1)}, f32[2048]{0:T(1024)S(1)}) all-reduce(f32[2048]{0:T(1024)S(1)} %get-tuple-element.808, f32[2048]{0:T(1024)S(1)} %get-tuple-element.806, f32[2048]{0:T(1024)S(1)} %get-tuple-element.804, ...), channel_id=7, replica_groups=mesh['dp'=4,'seq'=8] {'dp','seq'}, use_global_device_ids=true, to_apply=%region_39.40.clone | all-reduce | flops 8192 | bytes 65536
  1870.9 295.4 %reduce-scatter.20.cloned.1.call-done = f32[64,2048]{1,0:T(8,128)} async-done(((f32[2048,2048]{1,0:T(8,128)}), f32[64,2048]{1,0:T(8,128)}) %reduce-scatter.20.cloned.1.call-update) | async-done | bytes 524304 | tf_op jit(solution)/shard_map/reduce_scatter | solution.py:465
  2166.2 360.2 %reduce-scatter.16.cloned.1.call-done = f32[64,2048]{1,0:T(8,128)} async-done(((f32[2048,2048]{1,0:T(8,128)}), f32[64,2048]{1,0:T(8,128)}) %reduce-scatter.16.cloned.1.call-update) | async-done | bytes 524304 | tf_op jit(solution)/shard_map/reduce_scatter | solution.py:463
  2526.4 360.2 %reduce-scatter.14.cloned.1.call-done = f32[64,2048]{1,0:T(8,128)} async-done(((f32[2048,2048]{1,0:T(8,128)}), f32[64,2048]{1,0:T(8,128)}) %reduce-scatter.14.cloned.1.call-update) | async-done | bytes 524304 | tf_op jit(solution)/shard_map/reduce_scatter | solution.py:462
  2886.6 360.2 %reduce-scatter.18.cloned.1.call-done = f32[64,2048]{1,0:T(8,128)} async-done(((f32[2048,2048]{1,0:T(8,128)}), f32[64,2048]{1,0:T(8,128)}) %reduce-scatter.18.cloned.1.call-update) | async-done | bytes 524304 | tf_op jit(solution)/shard_map/reduce_scatter | solution.py:464
  (364 shorter events, 414.2 us)
Async XLA Ops:
  7.2 84.2 %all-gather.15.cloned.1.call-start = ((), (), s32[]{:S(2)}) async-start(), calls=%async_computation.15 | async-start | bytes 8650752 | tf_op jit(solution)/shard_map/all_gather | solution.py:291
  7.9 162.5 %all-gather.19.cloned.1.call-start = ((), (), s32[]{:S(2)}) async-start(), calls=%async_computation.17 | async-start | bytes 8650752 | tf_op jit(solution)/shard_map/all_gather | solution.py:290
  8.7 240.6 %all-gather.11.cloned.1.call-start = ((), (), s32[]{:S(2)}) async-start(), calls=%async_computation.13 | async-start | bytes 8650752 | tf_op jit(solution)/shard_map/all_gather | solution.py:292
  9.4 316.0 %all-gather.17.cloned.1.call-start = ((), (), s32[]{:S(2)}) async-start(), calls=%async_computation.16 | async-start | bytes 4718592 | tf_op jit(solution)/shard_map/all_gather | solution.py:307
  55.5 193.8 %copy-start.24 = (f32[2048]{0:T(1024)}, f32[2048]{0:T(1024)S(1)}, u32[]{:S(2)}) copy-start(f32[2048]{0:T(1024)S(1)} %convert_element_type.180) | copy-start | bytes 24580
  180.1 219.5 %all-gather.13.cloned.1.call-start = ((), (), s32[]{:S(2)}) async-start(), calls=%async_computation.14 | async-start | bytes 4718592 | tf_op jit(solution)/shard_map/all_gather | solution.py:308
  254.9 223.0 %all-gather.21.cloned.1.call-start = ((), (), s32[]{:S(2)}) async-start(), calls=%async_computation.18 | async-start | bytes 8650752 | tf_op jit(solution)/shard_map/all_gather | solution.py:293
  255.5 382.7 %all-gather.23.cloned.1.call-start = ((), (), s32[]{:S(2)}) async-start(), calls=%async_computation.19 | async-start | bytes 10485760 | tf_op jit(solution)/shard_map/all_gather | solution.py:301
  256.3 394.8 %all-gather.25.cloned.1.call-start = ((), (), s32[]{:S(2)}) async-start(), calls=%async_computation.20 | async-start | bytes 10485760 | tf_op jit(solution)/shard_map/all_gather | solution.py:302
  483.0 397.2 %copy-start.14 = (bf16[128,2048]{1,0:T(8,128)(2,1)}, bf16[128,2048]{1,0:T(8,128)(2,1)S(1)}, u32[]{:S(2)}) copy-start(bf16[128,2048]{1,0:T(8,128)(2,1)S(1)} %multiply_convert_fusion.4) | copy-start | bytes 1572868
  487.9 143.7 %all-to-all-start = ((bf16[16,96,2048]{2,1,0:T(8,128)(2,1)}), bf16[16,96,2048]{2,1,0:T(8,128)(2,1)}, u32[]{:S(2)}, u32[]{:S(2)}) async-start(bf16[16,96,2048]{2,1,0:T(8,128)(2,1)} %bitcast.294), calls=%async_computation | async-start | bytes 12582912 | tf_op jit(solution)/shard_map/all_to_all | solution.py:316
  492.7 173.1 %all-gather.27.cloned.1.call-start = ((), (), s32[]{:S(2)}) async-start(), calls=%async_computation.21 | async-start | bytes 10485760 | tf_op jit(solution)/shard_map/all_gather | solution.py:303
  680.0 199.2 %copy-start.18 = (bf16[1,128,2048]{2,1,0:T(8,128)(2,1)S(1)}, bf16[1,128,2048]{2,1,0:T(8,128)(2,1)}, u32[]{:S(2)}) copy-start(bf16[1,128,2048]{2,1,0:T(8,128)(2,1)} %param.41) | copy-start | bytes 1572868
  680.0 200.5 %all-to-all-start.1 = ((bf16[16,96,2048]{2,1,0:T(8,128)(2,1)}), bf16[16,96,2048]{2,1,0:T(8,128)(2,1)}, u32[]{:S(2)}, u32[]{:S(2)}) async-start(bf16[16,96,2048]{2,1,0:T(8,128)(2,1)} %bitcast.296), calls=%async_computation.1 | async-start | bytes 12582912 | tf_op jit(solution)/shard_map/all_to_all | solution.py:321
  1092.6 141.8 %all-to-all-start.3 = ((bf16[16,96,2048]{2,1,0:T(8,128)(2,1)}), bf16[16,96,2048]{2,1,0:T(8,128)(2,1)}, u32[]{:S(2)}, u32[]{:S(2)}) async-start(bf16[16,96,2048]{2,1,0:T(8,128)(2,1)} %bitcast.297), calls=%async_computation.3 | async-start | bytes 12582912 | tf_op jit(solution)/shard_map/all_to_all | solution.py:368
  1097.3 350.7 %reduce-scatter.28.cloned.1.call-start = ((), (), s32[]{:S(2)}) async-start(), calls=%async_computation.29 | async-start | bytes 9437184
  1296.8 287.8 %reduce-scatter.30.cloned.1.call-start = ((), (), s32[]{:S(2)}) async-start(), calls=%async_computation.30 | async-start | bytes 1081344
  1299.1 356.0 %reduce-scatter.26.cloned.1.call-start = ((), (), s32[]{:S(2)}) async-start(), calls=%async_computation.28 | async-start | bytes 10485760 | tf_op jit(solution)/shard_map/reduce_scatter | solution.py:479
  1311.5 418.2 %reduce-scatter.22.cloned.1.call-start = ((), (), s32[]{:S(2)}) async-start(), calls=%async_computation.26 | async-start | bytes 10485760 | tf_op jit(solution)/shard_map/reduce_scatter | solution.py:473
  1323.8 480.0 %reduce-scatter.24.cloned.1.call-start = ((), (), s32[]{:S(2)}) async-start(), calls=%async_computation.27 | async-start | bytes 10485760 | tf_op jit(solution)/shard_map/reduce_scatter | solution.py:476
  1335.8 830.4 %reduce-scatter.20.cloned.1.call-start = ((), (), s32[]{:S(2)}) async-start(), calls=%async_computation.25 | async-start | bytes 17301504 | tf_op jit(solution)/shard_map/reduce_scatter | solution.py:465
  1345.7 1180.7 %reduce-scatter.16.cloned.1.call-start = ((), (), s32[]{:S(2)}) async-start(), calls=%async_computation.23 | async-start | bytes 17301504 | tf_op jit(solution)/shard_map/reduce_scatter | solution.py:463
  1465.9 1420.6 %reduce-scatter.14.cloned.1.call-start = ((), (), s32[]{:S(2)}) async-start(), calls=%async_computation.22 | async-start | bytes 17301504 | tf_op jit(solution)/shard_map/reduce_scatter | solution.py:462
  1479.8 1766.9 %reduce-scatter.18.cloned.1.call-start = ((), (), s32[]{:S(2)}) async-start(), calls=%async_computation.24 | async-start | bytes 17301504 | tf_op jit(solution)/shard_map/reduce_scatter | solution.py:464
  (63 other events, 1529.4 us)
Sparse Core Ops, SparseCore 0:
  11.0 80.3 all-gather.14
  94.4 75.9 all-gather.18
  173.4 75.8 all-gather.10
  251.8 73.5 all-gather.16
  327.9 71.5 all-gather.12
  402.4 75.5 all-gather.20
  479.5 56.9 all-gather.22
  538.0 58.2 all-gather.24
  597.9 58.2 all-gather.26
  1296.9 151.1 reduce-scatter.27
  1450.4 134.0 reduce-scatter.29
  1587.0 68.1 reduce-scatter.25
  1657.9 71.6 reduce-scatter.21
  1732.1 71.7 reduce-scatter.23
  1806.7 359.4 reduce-scatter.19
  2169.0 357.3 reduce-scatter.15
  2529.2 357.3 reduce-scatter.13
  2889.4 357.3 reduce-scatter.17
where the time goes:
time: 3260 us; the launch traced here: 3250 us
  waiting for transfers between devices  2400 us (74%)
  blocking collectives  423 us (13%)
  matrix products  247 us (8%)
  local copies, waits for them, and re-layouts  91.9 us (3%)
  other arithmetic  58.9 us (2%)
    reduce_scatter x1, waiting for transfers between devices, on_device(): lax.psum_scatter(grad_w_key, ('dp', 'seq'), scatter_dimension=0, tiled=True)  360 us
    reduce_scatter x1, waiting for transfers between devices, on_device(): lax.psum_scatter(grad_w_value, ('dp', 'seq'), scatter_dimension=0, tiled=...  360 us
    reduce_scatter x1, waiting for transfers between devices, on_device(): lax.psum_scatter(grad_w_query, ('dp', 'seq'), scatter_dimension=0, tiled=...  360 us
    reduce_scatter x1, waiting for transfers between devices, on_device(): lax.psum_scatter(grad_w_out, ('dp', 'seq'), scatter_dimension=0, tiled=True)  295 us
    all_gather x1, blocking collectives, on_device(): lax.all_gather(w_router, ('dp', 'seq'), axis=0, tiled=True)  194 us
    unnamed x20, waiting for transfers between devices  191 us
    all_to_all x1, blocking collectives, on_device(): lax.all_to_all(grad_slots, 'seq', split_axis=0, concat_axis=0, tiled=True)  140 us
    all_to_all x1, waiting for transfers between devices, on_device(): lax.all_to_all(routing[7], 'seq', split_axis=0, concat_axis=0, tiled=True)  138 us
  transfers between devices with their start and end apart: 21, of which 17 were waited for; matrix products, arithmetic and copies ran while one was open for 7% of the time, Pallas kernels for 0%

commit v1 on v0

--- a/solution.py
+++ b/solution.py
@@ -498,9 +498,332 @@
     )
 
 
+def rope_tables(row_count, head_dim):
+    half_dim = head_dim // 2
+    frequency = jnp.exp(
+        jnp.arange(half_dim, dtype=jnp.float32) * (-2.0 * math.log(rope_base) / head_dim)
+    )
+    angles = jnp.arange(row_count, dtype=jnp.float32)[:, None] * frequency[None, :]
+    return (jnp.cos(angles), jnp.sin(angles))
+
+
+def rotate(values, cosine, sine):
+    half_dim = values.shape[-1] // 2
+    first, second = (values[:, :half_dim], values[:, half_dim:])
+    return jnp.concatenate(
+        [first * cosine - second * sine, second * cosine + first * sine], axis=-1
+    )
+
+
+def mm(left, right, dims):
+    return lax.dot_general(left, right, (dims, ((), ())), preferred_element_type=jnp.float32)
+
+
+def swap(values, bits, size):
+    return lax.ppermute(values, "dp", [(i, i ^ bits) for i in range(size)])
+
+
+def gather_pieces(shard):
+    across = swap(shard, 2, 4)
+    return (shard, swap(shard, 1, 4), across, swap(across, 1, 4))
+
+
+def sum_pieces(pieces):
+    arrived_own, arrived_across = (swap(pieces[1], 1, 4), swap(pieces[3], 1, 4))
+    kept = pieces[0].astype(jnp.float32) + arrived_own.astype(jnp.float32)
+    passed = (pieces[2].astype(jnp.float32) + arrived_across.astype(jnp.float32)).astype(
+        jnp.bfloat16
+    )
+    return kept + swap(passed, 2, 4).astype(jnp.float32)
+
+
+def reorder(values, dp_index, pieces):
+    width = values.shape[1] // pieces
+    return jnp.concatenate(
+        [
+            lax.dynamic_slice_in_dim(values, (dp_index ^ k) * width, width, axis=1)
+            for k in range(pieces)
+        ],
+        axis=1,
+    )
+
+
+def on_device_heads(
+    hidden_in,
+    segment_ids,
+    routes,
+    w_query,
+    w_key,
+    w_value,
+    w_out,
+    gain_attn,
+    gain_query,
+    gain_key,
+    gain_ffn,
+    w_router,
+    w_gate,
+    w_up,
+    w_down,
+    cotangent,
+):
+    low, full = (jnp.bfloat16, jnp.float32)
+    both = ("dp", "seq")
+    shards, parts = (lax.axis_size("seq"), lax.axis_size("dp"))
+    seq_index, dp_index = (lax.axis_index("seq"), lax.axis_index("dp"))
+    tokens, width = hidden_in.shape[1:]
+    rows = shards * tokens
+    cols = width // shards
+    heads = cols // HEAD
+    held = w_gate.shape[0]
+    ff = w_gate.shape[2]
+    expert_count = held * shards
+    block_rows = w_query.shape[0]
+    row_seg = segment_ids[0]
+    first_col = seq_index * cols
+    first_row = seq_index * tokens
+
+    def own_cols(values, count=cols):
+        return lax.dynamic_slice_in_dim(values, seq_index * count, count, axis=values.ndim - 1)
+
+    x_row = lax.all_gather(hidden_in[0], "seq", axis=0, tiled=True)
+    small = lax.all_gather(
+        jnp.concatenate(
+            [
+                w_router,
+                gain_attn[:, None],
+                gain_query[:, None],
+                gain_key[:, None],
+                gain_ffn[:, None],
+            ],
+            axis=1,
+        ).T,
+        both,
+        axis=1,
+        tiled=True,
+    )
+    router_t = small[:expert_count]
+    gains = small[expert_count:].astype(full)
+    qkv_blocks = jnp.stack([w_query, w_key, w_value], axis=1)
+    qkv_blocks = qkv_blocks.reshape(block_rows, 3, shards, cols).transpose(2, 0, 1, 3)
+    w_qkv = lax.all_to_all(qkv_blocks, "seq", 0, 0, tiled=True)
+    w_qkv = lax.all_gather(
+        w_qkv.reshape(shards * block_rows, 3 * cols), "dp", axis=0, tiled=True
+    )
+    out_full = lax.all_gather(w_out, both, axis=0, tiled=True)
+    dy_shard = reorder(cotangent[0], dp_index, parts)
+    routes_low = jnp.pad(routes[0].astype(low), ((0, 0), (0, 128 - routes.shape[2])))
+    dy_ext = lax.all_gather(
+        jnp.concatenate([dy_shard, routes_low], axis=1), "seq", axis=0, tiled=True
+    )
+    dy_row = dy_ext[:, :width]
+    routes_row = dy_ext[:, width : width + routes.shape[2]].astype(jnp.int32)
+    gate_full = jnp.concatenate(gather_pieces(w_gate), axis=1)
+    up_full = jnp.concatenate(gather_pieces(w_up), axis=1)
+    down_full = jnp.concatenate(gather_pieces(w_down), axis=2)
+
+    x_wide = x_row.astype(full)
+    r_attn = lax.rsqrt(jnp.mean(x_wide * x_wide, axis=-1, keepdims=True) + epsilon)
+    normed = (x_wide * r_attn * gains[0]).astype(low)
+    qkv = mm(normed, w_qkv, ((1,), (0,)))
+    query, key_proj = (qkv[:, :cols], qkv[:, cols : 2 * cols])
+    value_in = qkv[:, 2 * cols :].astype(low)
+    sums = lax.psum(
+        jnp.stack([jnp.sum(query * query, axis=-1), jnp.sum(key_proj * key_proj, axis=-1)]), "seq"
+    )
+    r_query, r_key = (
+        lax.rsqrt(sums[i] / width + epsilon)[:, None] for i in range(2)
+    )
+    g_query, g_key = (own_cols(gains[1]), own_cols(gains[2]))
+    cosine, sine = rope_tables(rows, HEAD)
+    q_normed, k_normed = (query * r_query * g_query, key_proj * r_key * g_key)
+    position = lax.iota(jnp.int32, rows)
+    allowed = (position[:, None] >= position[None, :]) & (row_seg[:, None] == row_seg[None, :])
+    scaling = HEAD ** (-0.5)
+
+    def head(values, h):
+        return values[:, h * HEAD : (h + 1) * HEAD]
+
+    q_rot, k_rot, log_total, attended = ([], [], [], [])
+    for h in range(heads):
+        q_rot.append(rotate(head(q_normed, h), cosine, sine).astype(low))
+        k_rot.append(rotate(head(k_normed, h), cosine, sine).astype(low))
+        scores = jnp.where(
+            allowed, mm(q_rot[h], k_rot[h], ((1,), (1,))) * scaling, masked_score
+        )
+        peak = jnp.max(scores, axis=-1, keepdims=True)
+        log_total.append(peak + jnp.log(jnp.sum(jnp.exp(scores - peak), axis=-1, keepdims=True)))
+        weights = jnp.exp(scores - log_total[h]).astype(low)
+        attended.append(mm(weights, head(value_in, h), ((1,), (0,))).astype(low))
+    attended = jnp.concatenate(attended, axis=1)
+    attended_row = lax.all_gather(attended, "seq", axis=0)
+    hidden_mid = x_wide + jnp.einsum(
+        "src,scn->rn",
+        attended_row,
+        out_full.reshape(shards, cols, width),
+        preferred_element_type=full,
+    )
+
+    r_ffn = lax.rsqrt(jnp.mean(hidden_mid * hidden_mid, axis=-1, keepdims=True) + epsilon)
+    normed_ffn = (hidden_mid * r_ffn * gains[3]).astype(low)
+    chances = softmax_rows(mm(normed_ffn, router_t, ((1,), (1,))))
+    expert_ids = lax.iota(jnp.int32, expert_count)
+    chosen = jnp.any(routes_row[:, :, None] == expert_ids[None, None, :], axis=1)
+    mine = own_cols(jnp.where(chosen, chances, 0.0), held)
+    mine_chosen = own_cols(chosen, held)
+    nf_parts = reorder(normed_ffn, dp_index, parts)
+    scaled, gate_grads, up_grads, gate_sums = ([], [], [], [])
+    for e in range(held):
+        gate_pre = mm(nf_parts, gate_full[e], ((1,), (0,)))
+        up_pre = mm(nf_parts, up_full[e], ((1,), (0,)))
+        grad_act = mm(dy_row, down_full[e], ((1,), (1,)))
+        weight = mine[:, e : e + 1]
+        sig = lax.logistic(gate_pre)
+        act = gate_pre * sig * up_pre
+        gate_sums.append(jnp.sum(act * grad_act, axis=-1))
+        scaled.append((weight * act).astype(low))
+        grad_act = weight * grad_act
+        gate_grads.append(
+            (grad_act * up_pre * sig * (1.0 + gate_pre * (1.0 - sig))).astype(low)
+        )
+        up_grads.append((grad_act * gate_pre * sig).astype(low))
+    mixture = sum(mm(scaled[e], down_full[e], ((1,), (0,))) for e in range(held)).astype(low)
+    mixture_own = lax.psum_scatter(mixture, "seq", scatter_dimension=0, tiled=True)
+    nf_grad = sum(
+        mm(gate_grads[e], gate_full[e], ((1,), (1,))) + mm(up_grads[e], up_full[e], ((1,), (1,)))
+        for e in range(held)
+    )
+
+    my_gates = jnp.where(mine_chosen, jnp.stack(gate_sums, axis=1), 0.0)
+    my_chances = own_cols(chances, held)
+    placed = lax.dynamic_update_slice_in_dim(
+        jnp.zeros_like(chances), my_gates, seq_index * held, axis=1
+    )
+    grad_logits = (
+        chances * (placed - jnp.sum(my_gates * my_chances, axis=1, keepdims=True))
+    ).astype(low)
+    router_grad = mm(grad_logits, normed_ffn, ((0,), (0,)))
+    nf_grad = nf_grad + mm(grad_logits, reorder(router_t, dp_index, parts), ((1,), (0,)))
+    nf_grad = lax.psum_scatter(nf_grad.astype(low), "seq", scatter_dimension=0, tiled=True)
+
+    mid_own = lax.dynamic_slice_in_dim(hidden_mid, first_row, tokens)
+    block_out = (mid_own + reorder(mixture_own, dp_index, parts).astype(full)).astype(low)
+    nf_own = reorder(nf_grad, dp_index, parts).astype(full)
+    r_own = lax.dynamic_slice_in_dim(r_ffn, first_row, tokens)
+    gain_ffn_grad = jnp.sum(nf_own * mid_own * r_own, axis=0)
+    scaled_grad = nf_own * gains[3]
+    grad_mid = (
+        cotangent[0].astype(full)
+        + r_own * scaled_grad
+        - mid_own * (r_own**3) * jnp.mean(scaled_grad * mid_own, axis=-1, keepdims=True)
+    )
+    mid_row = lax.all_gather(grad_mid.astype(low), "seq", axis=0, tiled=True)
+
+    def expert_grad(left, right):
+        return [mm(left[e], right[e], ((0,), (0,))).astype(low) for e in range(held)]
+
+    down_grad = jnp.stack(expert_grad(scaled, [dy_row] * held))
+    gate_grad = jnp.stack(expert_grad([nf_parts] * held, gate_grads))
+    up_grad = jnp.stack(expert_grad([nf_parts] * held, up_grads))
+    grad_w_down = sum_pieces(jnp.split(down_grad, parts, axis=2))
+    grad_w_gate = sum_pieces(jnp.split(gate_grad, parts, axis=1))
+    grad_w_up = sum_pieces(jnp.split(up_grad, parts, axis=1))
+
+    out_rows = lax.dynamic_slice_in_dim(out_full, first_col, cols)
+    grad_attended = mm(mid_row, out_rows, ((1,), (1,))).astype(low)
+    q_grads, k_grads, v_grads = ([], [], [])
+    for h in range(heads):
+        scores = jnp.where(
+            allowed, mm(q_rot[h], k_rot[h], ((1,), (1,))) * scaling, masked_score
+        )
+        p = jnp.exp(scores - log_total[h])
+        grad_h = head(grad_attended, h)
+        grad_weights = mm(grad_h, head(value_in, h), ((1,), (1,)))
+        delta = jnp.sum(p * grad_weights, axis=-1, keepdims=True)
+        grad_scores = (scaling * p * (grad_weights - delta)).astype(low)
+        q_grads.append(rotate(mm(grad_scores, k_rot[h], ((1,), (0,))), cosine, -sine))
+        k_grads.append(rotate(mm(grad_scores, q_rot[h], ((0,), (0,))), cosine, -sine))
+        v_grads.append(mm(p.astype(low), grad_h, ((0,), (0,))))
+    q_grad, k_grad = (jnp.concatenate(q_grads, axis=1), jnp.concatenate(k_grads, axis=1))
+    gain_query_grad = jnp.sum(q_grad * query * r_query, axis=0)
+    gain_key_grad = jnp.sum(k_grad * key_proj * r_key, axis=0)
+    q_grad, k_grad = (q_grad * g_query, k_grad * g_key)
+    means = lax.psum(
+        jnp.stack([jnp.sum(q_grad * query, axis=-1), jnp.sum(k_grad * key_proj, axis=-1)]), "seq"
+    )
+    means = means / width
+    q_low = (r_query * q_grad - query * (r_query**3) * means[0][:, None]).astype(low)
+    k_low = (r_key * k_grad - key_proj * (r_key**3) * means[1][:, None]).astype(low)
+    v_low = jnp.concatenate(v_grads, axis=1).astype(low)
+    qkv_low = jnp.concatenate([q_low, k_low, v_low], axis=1)
+    normed_grad = mm(qkv_low, w_qkv, ((1,), (1,)))
+    gain_attn_grad = jnp.sum(normed_grad * x_wide * r_attn, axis=0)
+    normed_grad = lax.psum_scatter(
+        normed_grad.astype(low), "seq", scatter_dimension=0, tiled=True
+    ).astype(full)
+
+    out_grad = jnp.einsum(
+        "src,rn->scn", attended_row, own_cols(mid_row), preferred_element_type=full
+    ).reshape(width, cols)
+    proj_grad = jnp.concatenate([mm(normed, qkv_low, ((0,), (0,))), out_grad], axis=1).astype(low)
+    proj_grad = lax.psum_scatter(proj_grad, "dp", scatter_dimension=0, tiled=True)
+    proj_grad = lax.all_to_all(
+        proj_grad.reshape(shards, block_rows, 4, cols), "seq", 0, 0, tiled=True
+    )
+    proj_grad = proj_grad.transpose(2, 1, 0, 3).reshape(4, block_rows, width).astype(full)
+
+    x_own = hidden_in[0].astype(full)
+    r_here = lax.rsqrt(jnp.mean(x_own * x_own, axis=-1, keepdims=True) + epsilon)
+    scaled_grad = normed_grad * gains[0]
+    grad_hidden = (
+        grad_mid
+        + r_here * scaled_grad
+        - x_own * (r_here**3) * jnp.mean(scaled_grad * x_own, axis=-1, keepdims=True)
+    )
+
+    def place(values):
+        return lax.dynamic_update_slice_in_dim(jnp.zeros((width,), full), values, first_col, 0)
+
+    vectors = jnp.concatenate(
+        [
+            router_grad,
+            gain_attn_grad[None],
+            place(gain_query_grad)[None],
+            place(gain_key_grad)[None],
+            gain_ffn_grad[None],
+        ]
+    )
+    count = vectors.shape[0]
+    vectors = vectors.reshape(count, parts * shards, block_rows).transpose(1, 0, 2)
+    vectors = lax.psum_scatter(
+        vectors.reshape(parts * shards, count * block_rows), both, scatter_dimension=0, tiled=True
+    ).reshape(count, block_rows)
+    return (
+        block_out[None],
+        grad_hidden[None],
+        proj_grad[0],
+        proj_grad[1],
+        proj_grad[2],
+        proj_grad[3],
+        vectors[expert_count],
+        vectors[expert_count + 1],
+        vectors[expert_count + 2],
+        vectors[expert_count + 3],
+        vectors[:expert_count].T,
+        grad_w_gate,
+        grad_w_up,
+        grad_w_down,
+    )
+
+
 def solution(mesh):
+    def layer(*arrays):
+        whole_heads = (arrays[0].shape[2] // HEAD) % mesh.shape["seq"] == 0
+        if whole_heads and mesh.shape["dp"] == 4:
+            return on_device_heads(*arrays)
+        return on_device(*arrays)
+
     return jax.shard_map(
-        on_device,
+        layer,
         mesh=mesh,
         in_specs=(
             P("dp", "seq", None),

time: 3260 us -> 1100 us (0.34)
  waiting for transfers between devices: 2400 us -> 526 us
  blocking collectives: 423 us -> 153 us
    reduce_scatter x7 -> x4, waiting for transfers between devices: 1590 us -> 196 us  [the longest x1 89 us: on_device_heads(): lax.psum_scatter(mixture, 'seq', scatter_dimension=0, tiled=True)]
    all_gather x9 -> x6, waiting for transfers between devices: 360 us -> 83.9 us  [the longest x1 72.8 us: on_device_heads(): mid_row = lax.all_gather(grad_mid.astype(low), 'seq', axis=0, tiled=True)]
    all_to_all x3 -> x1, waiting for transfers between devices: 265 us -> 0.01 us  [on_device_heads(): lax.all_to_all(proj_grad.reshape(shards, block_rows, 4, cols), 'seq', 0,...]
    ppermute x0 -> x18, waiting for transfers between devices: none -> 245 us  [swap(): return lax.ppermute(values, 'dp', [(i, i ^ bits) for i in range(size)])]
    unnamed x20 -> x12, waiting for transfers between devices: 191 us -> 1.36 us
    all_gather x1, blocking collectives: 194 us -> 67.6 us  [on_device_heads(): lax.all_gather(jnp.concatenate([w_router, gain_attn[:, None], gain_query[...]
    all_to_all x1, blocking collectives: 140 us -> 43.6 us  [on_device_heads(): w_qkv = lax.all_to_all(qkv_blocks, 'seq', 0, 0, tiled=True)]
    unnamed x2 -> x0, blocking collectives: 89.2 us -> none
  transfers between devices with their start and end apart: 21 -> 30, of which waited for: 17 -> 13; matrix products, arithmetic and copies ran while one was open for 7% -> 19% of each run, Pallas kernels for 0% -> 0%
where the time goes in v1:
time: 1100 us
  waiting for transfers between devices  526 us (48%)
  matrix products  244 us (22%)
  blocking collectives  153 us (14%)
  local copies, waits for them, and re-layouts  80.9 us (7%)
  other arithmetic  63.2 us (6%)
  between operations  15.9 us (1%)
  starting transfers between devices  12.9 us (1%)
    ppermute x18, waiting for transfers between devices, swap(): return lax.ppermute(values, 'dp', [(i, i ^ bits) for i in range(size)])  245 us
    dot_general x37, matrix products, mm(): lax.dot_general(left, right, (dims, ((), ())), preferred_element_type=jnp...  226 us
    reduce_scatter x1, waiting for transfers between devices, on_device_heads(): lax.psum_scatter(mixture, 'seq', scatter_dimension=0, tiled=True)  89 us
    all_gather x1, waiting for transfers between devices, on_device_heads(): mid_row = lax.all_gather(grad_mid.astype(low), 'seq', axis=0, tiled=True)  72.8 us
    all_gather x1, blocking collectives, on_device_heads(): lax.all_gather(jnp.concatenate([w_router, gain_attn[:, None], gain_query[...  67.6 us
    reduce_scatter x1, waiting for transfers between devices, on_device_heads(): lax.psum_scatter(nf_grad.astype(low), 'seq', scatter_dimension=0, tiled=T...  66.3 us
    unnamed x255, local copies, waits for them, and re-layouts  51.8 us
    all_to_all x1, blocking collectives, on_device_heads(): w_qkv = lax.all_to_all(qkv_blocks, 'seq', 0, 0, tiled=True)  43.6 us
  transfers between devices with their start and end apart: 30, of which 13 were waited for; matrix products, arithmetic and copies ran while one was open for 19% of the time, Pallas kernels for 0%

profile of v1, /device:TPU:0, one launch (start us, length us, event | category | flops | bytes accessed | tf_op | source)
XLA Modules:
  0.0 1096.2 jit_solution(9835236042166773127)
XLA Ops:
  11.3 43.6 %all_to_all.10 = bf16[8,64,3,256]{3,1,2,0:T(8,128)(2,1)S(1)} all-to-all(bf16[8,64,3,256]{3,1,2,0:T(8,128)(2,1)S(1)} %copy.128), channel_id=1, replica_groups=mesh['dp'=4,'seq'=8] {'seq'}, dimensions={0} | all-to-all | bytes 1572864 | tf_op jit(solution)/shard_map/all_to_all | solution.py:608
  58.4 67.6 %all-gather.2 = bf16[32,64,20]{1,2,0:T(8,128)(2,1)S(1)} all-gather(bf16[1,64,20]{1,2,0:T(8,128)(2,1)S(1)} %bitcast.221), channel_id=1, replica_groups=mesh['dp'=4,'seq'=8] {'dp','seq'}, dimensions={0}, use_global_device_ids=true | all-gather | bytes 84480 | tf_op jit(solution)/shard_map/all_gather | solution.py:589
  139.1 22.7 %psum.14 = f32[2,1024]{1,0:T(2,128)S(1)} all-reduce(f32[2,1024]{1,0:T(2,128)S(1)} %pad_maximum_fusion.24), channel_id=1, replica_groups=mesh['dp'=4,'seq'=8] {'seq'}, use_global_device_ids=true, to_apply=%region_3.4 | all-reduce | flops 2048 | bytes 16384 | tf_op jit(solution)/shard_map/psum | solution.py:630
  178.4 44.3 %collective-permute-done.1 = bf16[2,512,1024]{2,1,0:T(8,128)(2,1)} collective-permute-done((bf16[2,512,1024]{2,1,0:T(8,128)(2,1)S(1)}, bf16[2,512,1024]{2,1,0:T(8,128)(2,1)}, u32[]{:S(2)}, u32[]{:S(2)}) %collective-permute-start.1) | collective-permute-done | bytes 2097184 | tf_op jit(solution)/shard_map/ppermute | solution.py:523
  222.7 44.9 %collective-permute-done.4 = bf16[2,512,1024]{2,1,0:T(8,128)(2,1)} collective-permute-done((bf16[2,512,1024]{2,1,0:T(8,128)(2,1)}, bf16[2,512,1024]{2,1,0:T(8,128)(2,1)}, u32[]{:S(2)}, u32[]{:S(2)}) %collective-permute-start.4) | collective-permute-done | bytes 2097184 | tf_op jit(solution)/shard_map/ppermute | solution.py:523
  267.6 46.4 %collective-permute-done.7 = bf16[2,1024,512]{2,1,0:T(8,128)(2,1)} collective-permute-done((bf16[2,1024,512]{2,1,0:T(8,128)(2,1)}, bf16[2,1024,512]{2,1,0:T(8,128)(2,1)}, u32[]{:S(2)}, u32[]{:S(2)}) %collective-permute-start.7) | collective-permute-done | bytes 2097184 | tf_op jit(solution)/shard_map/ppermute | solution.py:523
  356.3 10.3 all-gather.12.cloned.1.call-done
  366.7 15.1 %multiply_reduce_fusion = (f32[1024]{0:T(1024)S(1)}, f32[1024,2048]{1,0:T(8,128)S(1)}) fusion(bf16[8,1024,256]{1,0,2:T(8,128)(2,1)} %bitcast.185, bf16[8,256,2048]{2,1,0:T(8,128)(2,1)} %bitcast.251, bf16[1,1024,2048]{2,1,0:T(8,128)(2,1)} %all-gather.18.cloned.1.call-done), kind=kOutput, calls=%fused_computation.32 | convolution fusion | flops 8598322176 | bytes 25169920 | tf_op jit(solution)/shard_map/src,scn->rn/dot_general | solution.py:659
  387.1 10.4 fusion.18
  425.1 10.2 multiply_convert_fusion.6
  435.3 10.8 fusion.15
  454.3 10.5 fusion.19
  478.5 16.1 %add_convert_fusion = bf16[1024,2048]{1,0:T(8,128)(2,1)} fusion(f32[1024,2048]{1,0:T(8,128)} %fusion.83, f32[1024,2048]{1,0:T(8,128)} %fusion.19, f32[1024,2048]{1,0:T(8,128)} %fusion.13, f32[1024,2048]{1,0:T(8,128)} %fusion.15, bf16[1024,1024]{0,1:T(8,128)(2,1)S(1)} %get-tuple-element.28, bf16[2,2048,1024]{2,1,0:T(8,128)(2,1)} %constant_dynamic-update-slice_fusion.5), kind=kOutput, calls=%fused_computation.29 | convolution fusion | flops 4305453056 | bytes 44040192 | tf_op jit(solution)/shard_map/dot_general | solution.py:519
  503.5 10.7 add_convert_fusion.1
  515.1 66.3 %reduce-scatter.7.cloned.1.call-done = bf16[128,2048]{1,0:T(8,128)(2,1)} async-done(((bf16[1024,2048]{1,0:T(8,128)(2,1)}), bf16[128,2048]{1,0:T(8,128)(2,1)}) %reduce-scatter.7.cloned.1.call-update) | async-done | bytes 524304 | tf_op jit(solution)/shard_map/reduce_scatter | solution.py:706
  584.1 89.0 %reduce-scatter.5.cloned.1.call-done = bf16[128,2048]{1,0:T(8,128)(2,1)} async-done(((bf16[1024,2048]{1,0:T(8,128)(2,1)}), bf16[128,2048]{1,0:T(8,128)(2,1)}) %reduce-scatter.5.cloned.1.call-update) | async-done | bytes 524304 | tf_op jit(solution)/shard_map/reduce_scatter | solution.py:690
  677.8 72.8 %all-gather.16.cloned.1.call-done = bf16[1024,2048]{1,0:T(8,128)(2,1)} async-done(((bf16[128,2048]{1,0:T(8,128)(2,1)}), bf16[1024,2048]{1,0:T(8,128)(2,1)}) %all-gather.16.cloned.1.call-update) | async-done | bytes 4194320 | tf_op jit(solution)/shard_map/all_gather | solution.py:719
  780.2 19.1 %psum.15 = f32[2,1024]{1,0:T(2,128)S(1)} all-reduce(f32[2,1024]{1,0:T(2,128)S(1)} %pad_maximum_fusion.25), channel_id=1, replica_groups=mesh['dp'=4,'seq'=8] {'seq'}, use_global_device_ids=true, to_apply=%region_23.24 | all-reduce | flops 2048 | bytes 16384 | tf_op jit(solution)/shard_map/psum | solution.py:750
  811.7 12.8 %convert_bitcast_fusion = bf16[1,1024,2048]{2,1,0:T(8,128)(2,1)} fusion(bf16[1024,2176]{0,1:T(8,128)(2,1)} %all-gather.14.cloned.1.call-done, f32[1024]{0:T(1024)S(1)} %bitcast.242, f32[1024,1024]{0,1:T(8,128)} %fusion.20, f32[1024,1024]{0,1:T(8,128)} %fusion.18), kind=kOutput, calls=%fused_computation.46 | convolution fusion | flops 4304404480 | bytes 16781312 | tf_op jit(solution)/shard_map/dot_general | solution.py:519
  835.5 10.2 fusion.4
  903.1 37.4 %collective-permute-done.17 = bf16[2,1024,512]{2,1,0:T(8,128)(2,1)} collective-permute-done((bf16[2,1024,512]{2,1,0:T(8,128)(2,1)S(1)}, bf16[2,1024,512]{2,1,0:T(8,128)(2,1)}, u32[]{:S(2)}, u32[]{:S(2)}) %collective-permute-start.17) | collective-permute-done | bytes 2097184 | tf_op jit(solution)/shard_map/ppermute | solution.py:523
  952.9 33.1 %collective-permute-done.14 = bf16[2,512,1024]{2,1,0:T(8,128)(2,1)} collective-permute-done((bf16[2,512,1024]{2,1,0:T(8,128)(2,1)}, bf16[2,512,1024]{2,1,0:T(8,128)(2,1)}, u32[]{:S(2)}, u32[]{:S(2)}) %collective-permute-start.14) | collective-permute-done | bytes 2097184 | tf_op jit(solution)/shard_map/ppermute | solution.py:523
  992.2 37.5 %collective-permute-done.11 = bf16[2,512,1024]{2,1,0:T(8,128)(2,1)} collective-permute-done((bf16[2,512,1024]{2,1,0:T(8,128)(2,1)}, bf16[2,512,1024]{2,1,0:T(8,128)(2,1)}, u32[]{:S(2)}, u32[]{:S(2)}) %collective-permute-start.11) | collective-permute-done | bytes 2097184 | tf_op jit(solution)/shard_map/ppermute | solution.py:523
  1038.2 40.3 %reduce-scatter.9.cloned.1.call-done = bf16[128,2048]{1,0:T(8,128)(2,1)} async-done(((bf16[1024,2048]{1,0:T(8,128)(2,1)}), bf16[128,2048]{1,0:T(8,128)(2,1)}) %reduce-scatter.9.cloned.1.call-update) | async-done | bytes 524304 | tf_op jit(solution)/shard_map/reduce_scatter | solution.py:760
  (447 shorter events, 298.5 us)
Async XLA Ops:
  7.2 119.8 %all-gather.18.cloned.1.call-start = ((), (), s32[]{:S(2)}) async-start(), calls=%async_computation.14 | async-start | bytes 4718592 | tf_op jit(solution)/shard_map/all_gather | solution.py:588
  7.9 123.0 %all-gather.10.cloned.1.call-start = ((), (), s32[]{:S(2)}) async-start(), calls=%async_computation.6 | async-start | bytes 3932160 | tf_op jit(solution)/shard_map/all_gather | solution.py:609
  56.6 289.8 %all-gather.14.cloned.1.call-start = ((), (), s32[]{:S(2)}) async-start(), calls=%async_computation.8 | async-start | bytes 5013504 | tf_op jit(solution)/shard_map/all_gather | solution.py:615
  58.3 289.6 %all-gather.20.cloned.1.call-start = ((), (), s32[]{:S(2)}) async-start(), calls=%async_computation.15 | async-start | bytes 4718592 | tf_op jit(solution)/shard_map/all_gather | solution.py:658
  172.8 193.8 %all-gather.12.cloned.1.call-start = ((), (), s32[]{:S(2)}) async-start(), calls=%async_computation.7 | async-start | bytes 8650752 | tf_op jit(solution)/shard_map/all_gather | solution.py:612
  173.4 408.0 %reduce-scatter.7.cloned.1.call-start = ((), (), s32[]{:S(2)}) async-start(), calls=%async_computation.10 | async-start | bytes 4718592 | tf_op jit(solution)/shard_map/reduce_scatter | solution.py:706
  174.1 48.6 %collective-permute-start.1 = (bf16[2,512,1024]{2,1,0:T(8,128)(2,1)S(1)}, bf16[2,512,1024]{2,1,0:T(8,128)(2,1)}, u32[]{:S(2)}, u32[]{:S(2)}) collective-permute-start(bf16[2,512,1024]{2,1,0:T(8,128)(2,1)S(1)} %copy-done.30), channel_id=1, source_target_pairs={{0,16},{8,24},{16,0},{24,8},{1,17},{9,25},{17,1},{25,9},{2,18},{10... | collective-permute-start | bytes 6291464 | tf_op jit(solution)/shard_map/ppermute | solution.py:523
  174.8 92.9 %collective-permute-start.4 = (bf16[2,512,1024]{2,1,0:T(8,128)(2,1)}, bf16[2,512,1024]{2,1,0:T(8,128)(2,1)}, u32[]{:S(2)}, u32[]{:S(2)}) collective-permute-start(bf16[2,512,1024]{2,1,0:T(8,128)(2,1)} %param.29), channel_id=1, source_target_pairs={{0,16},{8,24},{16,0},{24,8},{1,17},{9,25},{17,1},{25,9},{2,18},{10... | collective-permute-start | bytes 6291464 | tf_op jit(solution)/shard_map/ppermute | solution.py:523
  176.2 137.8 %collective-permute-start.7 = (bf16[2,1024,512]{2,1,0:T(8,128)(2,1)}, bf16[2,1024,512]{2,1,0:T(8,128)(2,1)}, u32[]{:S(2)}, u32[]{:S(2)}) collective-permute-start(bf16[2,1024,512]{2,1,0:T(8,128)(2,1)} %param.30), channel_id=1, source_target_pairs={{0,16},{8,24},{16,0},{24,8},{1,17},{9,25},{17,1},{25,9},{2,18},{10... | collective-permute-start | bytes 6291464 | tf_op jit(solution)/shard_map/ppermute | solution.py:523
  176.8 147.0 %collective-permute-start.3 = (bf16[2,512,1024]{2,1,0:T(8,128)(2,1)}, bf16[2,512,1024]{2,1,0:T(8,128)(2,1)}, u32[]{:S(2)}, u32[]{:S(2)}) collective-permute-start(bf16[2,512,1024]{2,1,0:T(8,128)(2,1)} %param.29), channel_id=1, source_target_pairs={{0,8},{8,0},{16,24},{24,16},{1,9},{9,1},{17,25},{25,17},{2,10},{10... | collective-permute-start | bytes 6291464 | tf_op jit(solution)/shard_map/ppermute | solution.py:523
  178.2 151.8 %collective-permute-start.6 = (bf16[2,1024,512]{2,1,0:T(8,128)(2,1)}, bf16[2,1024,512]{2,1,0:T(8,128)(2,1)}, u32[]{:S(2)}, u32[]{:S(2)}) collective-permute-start(bf16[2,1024,512]{2,1,0:T(8,128)(2,1)} %param.30), channel_id=1, source_target_pairs={{0,8},{8,0},{16,24},{24,16},{1,9},{9,1},{17,25},{25,17},{2,10},{10... | collective-permute-start | bytes 6291464 | tf_op jit(solution)/shard_map/ppermute | solution.py:523
  222.7 113.6 %collective-permute-start.2 = (bf16[2,512,1024]{2,1,0:T(8,128)(2,1)}, bf16[2,512,1024]{2,1,0:T(8,128)(2,1)}, u32[]{:S(2)}, u32[]{:S(2)}) collective-permute-start(bf16[2,512,1024]{2,1,0:T(8,128)(2,1)} %collective-permute-done.1), channel_id=1, source_target_pairs={{0,8},{8,0},{16,24},{24,16},{1,9},{9,1},{17,25},{25,17},{2,10},{10... | collective-permute-start | bytes 6291464 | tf_op jit(solution)/shard_map/ppermute | solution.py:523
  267.6 72.4 %collective-permute-start.5 = (bf16[2,512,1024]{2,1,0:T(8,128)(2,1)}, bf16[2,512,1024]{2,1,0:T(8,128)(2,1)}, u32[]{:S(2)}, u32[]{:S(2)}) collective-permute-start(bf16[2,512,1024]{2,1,0:T(8,128)(2,1)} %collective-permute-done.4), channel_id=1, source_target_pairs={{0,8},{8,0},{16,24},{24,16},{1,9},{9,1},{17,25},{25,17},{2,10},{10... | collective-permute-start | bytes 6291464 | tf_op jit(solution)/shard_map/ppermute | solution.py:523
  494.6 178.6 %reduce-scatter.5.cloned.1.call-start = ((), (), s32[]{:S(2)}) async-start(), calls=%async_computation.9 | async-start | bytes 4718592 | tf_op jit(solution)/shard_map/reduce_scatter | solution.py:690
  514.2 236.4 %all-gather.16.cloned.1.call-start = ((), (), s32[]{:S(2)}) async-start(), calls=%async_computation.11 | async-start | bytes 4718592 | tf_op jit(solution)/shard_map/all_gather | solution.py:719
  677.3 268.9 %reduce-scatter.11.cloned.1.call-start = ((), (), s32[]{:S(2)}) async-start(), calls=%async_computation.13 | async-start | bytes 5242880 | tf_op jit(solution)/shard_map/reduce_scatter | solution.py:768
  808.5 226.9 %all-reduce.4.cloned.1.call-start = ((), (), s32[]{:S(2)}) async-start(), calls=%async_computation.16 | async-start | bytes 327680
  846.7 231.7 %reduce-scatter.9.cloned.1.call-start = ((), (), s32[]{:S(2)}) async-start(), calls=%async_computation.12 | async-start | bytes 4718592 | tf_op jit(solution)/shard_map/reduce_scatter | solution.py:760
  891.5 49.0 %collective-permute-start.17 = (bf16[2,1024,512]{2,1,0:T(8,128)(2,1)S(1)}, bf16[2,1024,512]{2,1,0:T(8,128)(2,1)}, u32[]{:S(2)}, u32[]{:S(2)}) collective-permute-start(bf16[2,1024,512]{2,1,0:T(8,128)(2,1)S(1)} %add_convert_fusion.2), channel_id=1, source_target_pairs={{0,16},{8,24},{16,0},{24,8},{1,17},{9,25},{17,1},{25,9},{2,18},{10... | collective-permute-start | bytes 6291464 | tf_op jit(solution)/shard_map/ppermute | solution.py:523
  893.3 59.6 %collective-permute-start.12 = (bf16[2,512,1024]{2,1,0:T(8,128)(2,1)}, bf16[2,512,1024]{2,1,0:T(8,128)(2,1)}, u32[]{:S(2)}, u32[]{:S(2)}) collective-permute-start(bf16[2,512,1024]{2,1,0:T(8,128)(2,1)} %get-tuple-element.36), channel_id=1, source_target_pairs={{0,8},{8,0},{16,24},{24,16},{1,9},{9,1},{17,25},{25,17},{2,10},{10... | collective-permute-start | bytes 6291464 | tf_op jit(solution)/shard_map/ppermute | solution.py:523
  897.3 88.7 %collective-permute-start.14 = (bf16[2,512,1024]{2,1,0:T(8,128)(2,1)}, bf16[2,512,1024]{2,1,0:T(8,128)(2,1)}, u32[]{:S(2)}, u32[]{:S(2)}) collective-permute-start(bf16[2,512,1024]{2,1,0:T(8,128)(2,1)} %add_convert_fusion.3), channel_id=1, source_target_pairs={{0,16},{8,24},{16,0},{24,8},{1,17},{9,25},{17,1},{25,9},{2,18},{10... | collective-permute-start | bytes 6291464 | tf_op jit(solution)/shard_map/ppermute | solution.py:523
  897.5 94.7 %collective-permute-start.9 = (bf16[2,512,1024]{2,1,0:T(8,128)(2,1)}, bf16[2,512,1024]{2,1,0:T(8,128)(2,1)}, u32[]{:S(2)}, u32[]{:S(2)}) collective-permute-start(bf16[2,512,1024]{2,1,0:T(8,128)(2,1)} %get-tuple-element.38), channel_id=1, source_target_pairs={{0,8},{8,0},{16,24},{24,16},{1,9},{9,1},{17,25},{25,17},{2,10},{10... | collective-permute-start | bytes 6291464 | tf_op jit(solution)/shard_map/ppermute | solution.py:523
  901.4 128.3 %collective-permute-start.11 = (bf16[2,512,1024]{2,1,0:T(8,128)(2,1)}, bf16[2,512,1024]{2,1,0:T(8,128)(2,1)}, u32[]{:S(2)}, u32[]{:S(2)}) collective-permute-start(bf16[2,512,1024]{2,1,0:T(8,128)(2,1)} %add_convert_fusion.4), channel_id=1, source_target_pairs={{0,16},{8,24},{16,0},{24,8},{1,17},{9,25},{17,1},{25,9},{2,18},{10... | collective-permute-start | bytes 6291464 | tf_op jit(solution)/shard_map/ppermute | solution.py:523
  949.3 132.9 %all-to-all-start.1 = ((bf16[8,64,4,256]{3,2,1,0:T(4,128)(2,1)}), bf16[8,64,4,256]{3,2,1,0:T(4,128)(2,1)S(1)}, u32[]{:S(2)}, u32[]{:S(2)}) async-start(bf16[8,64,4,256]{3,2,1,0:T(4,128)(2,1)} %reshape.220), calls=%async_computation.5 | async-start | bytes 2097152 | tf_op jit(solution)/shard_map/all_to_all | solution.py:769
  (122 other events, 2062.5 us)
Sparse Core Ops, SparseCore 0:
  10.1 91.5 all-gather.17
  103.9 26.9 all-gather.9
  133.5 78.7 all-gather.13
  215.0 71.5 all-gather.19
  289.4 77.2 all-gather.11
  494.7 86.6 reduce-scatter.6
  585.4 87.6 reduce-scatter.4
  677.4 73.1 all-gather.15
  808.6 41.7 reduce-scatter.10
  857.3 127.0 all-reduce.3
  988.4 90.0 reduce-scatter.8

commit v2 on v0

--- a/solution.py
+++ b/solution.py
@@ -3,6 +3,8 @@
 import jax
 import jax.numpy as jnp
 from jax import lax
+from jax.experimental import pallas as pl
+from jax.experimental.pallas import tpu as pltpu
 from jax.sharding import PartitionSpec as P
 
 HEAD = 128
@@ -498,9 +500,697 @@
     )
 
 
+VMEM_GRANT = 56 * 1024 * 1024
+
+
+def mm(left, right, dims):
+    return lax.dot_general(left, right, (dims, ((), ())), preferred_element_type=jnp.float32)
+
+
+def cost(flops, transcendentals, *arrays):
+    moved = sum(math.prod(a.shape) * a.dtype.itemsize for a in arrays)
+    return pl.CostEstimate(flops=flops, transcendentals=transcendentals, bytes_accessed=moved)
+
+
+def grid_call(body, grid, in_specs, out_specs, outs, flops, transcendentals, *args):
+    return pl.pallas_call(
+        body,
+        grid=grid,
+        in_specs=in_specs,
+        out_specs=out_specs,
+        out_shape=outs,
+        compiler_params=pltpu.CompilerParams(vmem_limit_bytes=VMEM_GRANT),
+        cost_estimate=cost(flops, transcendentals, *args, *jax.tree.leaves(outs)),
+    )(*args)
+
+
+def row_tiles(rows):
+    return math.gcd(rows, 512)
+
+
+def finish_attention(order, attended, out_pieces, x_row, gain, router, chosen, own, expert_count):
+    shards, rows, cols = attended.shape
+    width = x_row.shape[1]
+    held = own.shape[0]
+    chunk = width // 4
+    per_chunk = chunk // cols
+    tm = math.gcd(rows, 256)
+
+    def body(order_ref, att_ref, p0, p1, p2, p3, x_ref, gain_ref, router_ref, chosen_ref, own_ref, *outs):
+        mid_ref, normed_ref, r_ref, chance_ref, gate_ref, att_all = outs
+        for h in range(shards):
+            source = order_ref[h // per_chunk] * per_chunk + h % per_chunk
+            att_all[:, h * cols : (h + 1) * cols] = att_ref[source]
+        squares = jnp.zeros((tm, 1), jnp.float32)
+        for n in range(4):
+            at = slice(n * chunk, (n + 1) * chunk)
+            total = x_ref[:, at].astype(jnp.float32)
+            for j, piece in enumerate((p0, p1, p2, p3)):
+                k = n ^ j
+                total = total + mm(
+                    att_all[:, j * chunk : (j + 1) * chunk],
+                    piece[:, k * chunk : (k + 1) * chunk],
+                    ((1,), (0,)),
+                )
+            mid_ref[:, at] = total
+            squares = squares + jnp.sum(total * total, axis=-1, keepdims=True)
+        r = lax.rsqrt(squares / width + epsilon)
+        r_ref[...] = r
+        logits = jnp.zeros((tm, 128), jnp.float32)
+        for n in range(4):
+            at = slice(n * chunk, (n + 1) * chunk)
+            normed = (mid_ref[:, at] * r * gain_ref[:, at]).astype(jnp.bfloat16)
+            normed_ref[:, at] = normed
+            logits = logits + mm(normed, router_ref[at, :], ((1,), (0,)))
+        lane = lax.broadcasted_iota(jnp.int32, (tm, 128), 1)
+        logits = jnp.where(lane < expert_count, logits, masked_score)
+        raised = jnp.exp(logits - jnp.max(logits, axis=-1, keepdims=True))
+        chances = raised / jnp.sum(raised, axis=-1, keepdims=True)
+        chance_ref[...] = chances
+        taken = chances * chosen_ref[...]
+        for e in range(held):
+            gate_ref[e] = jnp.sum(taken * own_ref[e : e + 1, :], axis=-1, keepdims=True)
+
+    full = jnp.float32
+    piece_spec = pl.BlockSpec((chunk, width), lambda i, o: (0, 0))
+    wide = pl.BlockSpec((tm, width), lambda i, o: (i, 0))
+    lanes = pl.BlockSpec((tm, 128), lambda i, o: (i, 0))
+    outs = [
+        jax.ShapeDtypeStruct((rows, width), full),
+        jax.ShapeDtypeStruct((rows, width), jnp.bfloat16),
+        jax.ShapeDtypeStruct((rows, 1), full),
+        jax.ShapeDtypeStruct((rows, 128), full),
+        jax.ShapeDtypeStruct((held, rows, 1), full),
+    ]
+    return pl.pallas_call(
+        body,
+        grid_spec=pltpu.PrefetchScalarGridSpec(
+            num_scalar_prefetch=1,
+            grid=(rows // tm,),
+            in_specs=[
+                pl.BlockSpec((shards, tm, cols), lambda i, o: (0, i, 0)),
+                piece_spec,
+                piece_spec,
+                piece_spec,
+                piece_spec,
+                wide,
+                pl.BlockSpec((1, width), lambda i, o: (0, 0)),
+                pl.BlockSpec((width, 128), lambda i, o: (0, 0)),
+                lanes,
+                pl.BlockSpec((held, 128), lambda i, o: (0, 0)),
+            ],
+            out_specs=[
+                wide,
+                wide,
+                pl.BlockSpec((tm, 1), lambda i, o: (i, 0)),
+                lanes,
+                pl.BlockSpec((held, tm, 1), lambda i, o: (0, i, 0)),
+            ],
+            scratch_shapes=[pltpu.VMEM((tm, width), jnp.bfloat16)],
+        ),
+        out_shape=outs,
+        compiler_params=pltpu.CompilerParams(vmem_limit_bytes=VMEM_GRANT),
+        cost_estimate=cost(2 * rows * width * width, rows * 128, attended, *out_pieces, *outs),
+    )(order, attended, *out_pieces, x_row, gain, router, chosen, own)
+
+
+def expert_activations(normed, gate, up):
+    held, width, ff = gate.shape
+    rows = normed.shape[0]
+    tile, tm = (math.gcd(ff, 512), row_tiles(rows))
+
+    def body(x_ref, gate_ref, up_ref, act_ref, dgate_ref, dup_ref):
+        @pl.loop(0, rows // tm)
+        def _(i):
+            at = pl.ds(pl.multiple_of(i * tm, tm), tm)
+            gate_pre = mm(x_ref[at, :], gate_ref[0], ((1,), (0,)))
+            up_pre = mm(x_ref[at, :], up_ref[0], ((1,), (0,)))
+            sig = lax.logistic(gate_pre)
+            silu = gate_pre * sig
+            act_ref[0, at, :] = (silu * up_pre).astype(jnp.bfloat16)
+            dgate_ref[0, at, :] = (up_pre * (sig + silu * (1.0 - sig))).astype(jnp.bfloat16)
+            dup_ref[0, at, :] = silu.astype(jnp.bfloat16)
+
+    tiled = pl.BlockSpec((1, rows, tile), lambda e, f: (e, 0, f))
+    low = jax.ShapeDtypeStruct((held, rows, ff), jnp.bfloat16)
+    return grid_call(
+        body,
+        (held, ff // tile),
+        [
+            pl.BlockSpec((rows, width), lambda e, f: (0, 0)),
+            pl.BlockSpec((1, width, tile), lambda e, f: (e, 0, f)),
+            pl.BlockSpec((1, width, tile), lambda e, f: (e, 0, f)),
+        ],
+        [tiled, tiled, tiled],
+        [low, low, low],
+        4 * held * rows * ff * width,
+        held * rows * ff,
+        normed,
+        gate,
+        up,
+    )
+
+
+def expert_gradients(dy, down, act, dgate_factor, dup_factor, weight):
+    held, ff, width = down.shape
+    rows = dy.shape[0]
+    tile, tm = (math.gcd(ff, 512), row_tiles(rows))
+
+    def body(dy_ref, down_ref, act_ref, a_ref, b_ref, weight_ref, out_ref, dgate_ref, dup_ref, sum_ref):
+        first = pl.program_id(1) == 0
+
+        @pl.loop(0, rows // tm)
+        def _(i):
+            at = pl.ds(pl.multiple_of(i * tm, tm), tm)
+            grad = mm(dy_ref[at, :], down_ref[0], ((1,), (1,)))
+            scale = weight_ref[0, at, :]
+            act = act_ref[0, at, :].astype(jnp.float32)
+            product = act * grad
+            partial = product[:, :128]
+            for j in range(1, tile // 128):
+                partial = partial + product[:, j * 128 : (j + 1) * 128]
+
+            @pl.when(first)
+            def _():
+                sum_ref[0, at, :] = partial
+
+            @pl.when(jnp.logical_not(first))
+            def _():
+                sum_ref[0, at, :] = sum_ref[0, at, :] + partial
+
+            out_ref[0, at, :] = (scale * act).astype(jnp.bfloat16)
+            grad = scale * grad
+            dgate_ref[0, at, :] = (grad * a_ref[0, at, :].astype(jnp.float32)).astype(jnp.bfloat16)
+            dup_ref[0, at, :] = (grad * b_ref[0, at, :].astype(jnp.float32)).astype(jnp.bfloat16)
+
+    tiled = pl.BlockSpec((1, rows, tile), lambda e, f: (e, 0, f))
+    low = jax.ShapeDtypeStruct((held, rows, ff), jnp.bfloat16)
+    return grid_call(
+        body,
+        (held, ff // tile),
+        [
+            pl.BlockSpec((rows, width), lambda e, f: (0, 0)),
+            pl.BlockSpec((1, tile, width), lambda e, f: (e, f, 0)),
+            tiled,
+            tiled,
+            tiled,
+            pl.BlockSpec((1, rows, 1), lambda e, f: (e, 0, 0)),
+        ],
+        [tiled, tiled, tiled, pl.BlockSpec((1, rows, 128), lambda e, f: (e, 0, 0))],
+        [low, low, low, jax.ShapeDtypeStruct((held, rows, 128), jnp.float32)],
+        2 * held * rows * ff * width,
+        0,
+        dy,
+        down,
+        act,
+        dgate_factor,
+        dup_factor,
+        weight,
+    )
+
+
+def input_gradient(dgate, dup, gate, up, gate_sums, chances, chosen, own, router):
+    held, width, ff = gate.shape
+    rows = dgate.shape[1]
+    tile, tm = (math.gcd(width, 512), row_tiles(rows))
+
+    def body(dgate_ref, dup_ref, gate_ref, up_ref, sum_ref, chance_ref, chosen_ref, own_ref, router_ref, out_ref, logits_ref):
+        @pl.loop(0, rows // tm)
+        def _(i):
+            at = pl.ds(pl.multiple_of(i * tm, tm), tm)
+            chances = chance_ref[at, :]
+            placed = jnp.zeros((tm, 128), jnp.float32)
+            for e in range(held):
+                got = jnp.sum(sum_ref[e, at, :], axis=-1, keepdims=True)
+                placed = placed + own_ref[e : e + 1, :] * got
+            placed = placed * chosen_ref[at, :]
+            inner = jnp.sum(chances * placed, axis=-1, keepdims=True)
+            logits = (chances * (placed - inner)).astype(jnp.bfloat16)
+            logits_ref[at, :] = logits
+            total = mm(logits, router_ref[...], ((1,), (1,)))
+            for e in range(held):
+                total = total + mm(dgate_ref[e, at, :], gate_ref[e], ((1,), (1,)))
+                total = total + mm(dup_ref[e, at, :], up_ref[e], ((1,), (1,)))
+            out_ref[at, :] = total.astype(jnp.bfloat16)
+
+    whole = pl.BlockSpec((held, rows, ff), lambda n: (0, 0, 0))
+    weights = pl.BlockSpec((held, tile, ff), lambda n: (0, n, 0))
+    lanes = pl.BlockSpec((rows, 128), lambda n: (0, 0))
+    return grid_call(
+        body,
+        (width // tile,),
+        [
+            whole,
+            whole,
+            weights,
+            weights,
+            pl.BlockSpec((held, rows, 128), lambda n: (0, 0, 0)),
+            lanes,
+            lanes,
+            pl.BlockSpec((held, 128), lambda n: (0, 0)),
+            pl.BlockSpec((tile, 128), lambda n: (n, 0)),
+        ],
+        [pl.BlockSpec((rows, tile), lambda n: (0, n)), lanes],
+        [jax.ShapeDtypeStruct((rows, width), jnp.bfloat16), jax.ShapeDtypeStruct((rows, 128), jnp.bfloat16)],
+        4 * held * rows * ff * width,
+        0,
+        dgate,
+        dup,
+        gate,
+        up,
+        gate_sums,
+        chances,
+        chosen,
+        own,
+        router,
+    )
+
+
+def combine_experts(act, down, weight):
+    held, ff, width = down.shape
+    rows = act.shape[1]
+    tile, tm = (math.gcd(width, 512), row_tiles(rows))
+
+    def body(act_ref, down_ref, weight_ref, out_ref):
+        @pl.loop(0, rows // tm)
+        def _(i):
+            at = pl.ds(pl.multiple_of(i * tm, tm), tm)
+            total = weight_ref[0, at, :] * mm(act_ref[0, at, :], down_ref[0], ((1,), (0,)))
+            for e in range(1, held):
+                term = mm(act_ref[e, at, :], down_ref[e], ((1,), (0,)))
+                total = total + weight_ref[e, at, :] * term
+            out_ref[at, :] = total.astype(jnp.bfloat16)
+
+    return grid_call(
+        body,
+        (width // tile,),
+        [
+            pl.BlockSpec((held, rows, ff), lambda n: (0, 0, 0)),
+            pl.BlockSpec((held, ff, tile), lambda n: (0, 0, n)),
+            pl.BlockSpec((held, rows, 1), lambda n: (0, 0, 0)),
+        ],
+        pl.BlockSpec((rows, tile), lambda n: (0, n)),
+        jax.ShapeDtypeStruct((rows, width), jnp.bfloat16),
+        2 * held * rows * ff * width,
+        0,
+        act,
+        down,
+        weight,
+    )
+
+
+def weight_pieces(left, right, parts, split_left):
+    flat, stacked = (left, right) if split_left else (right, left)
+    held, rows, ff = stacked.shape
+    piece = flat.shape[1] // parts
+    shape = (held, piece, ff) if split_left else (held, ff, piece)
+    tm = math.gcd(shape[1], 512)
+
+    def body(flat_ref, stacked_ref, *outs):
+        step = pl.program_id(0)
+        for j in range(parts):
+
+            @pl.when(step == j)
+            def _(j=j):
+                @pl.loop(0, shape[1] // tm)
+                def _(i):
+                    at = pl.ds(pl.multiple_of(i * tm, tm), tm)
+                    if split_left:
+                        value = mm(flat_ref[:, at], stacked_ref[0], ((0,), (0,)))
+                    else:
+                        value = mm(stacked_ref[0, :, at], flat_ref[...], ((0,), (0,)))
+                    outs[j][0, at, :] = value.astype(jnp.bfloat16)
+
+    def place(j):
+        return lambda k, e: (jnp.where(k < j, 0, jnp.where(k > j, held - 1, e)), 0, 0)
+
+    return grid_call(
+        body,
+        (parts, held),
+        [
+            pl.BlockSpec((rows, piece), lambda k, e: (0, k)),
+            pl.BlockSpec((1, rows, ff), lambda k, e: (e, 0, 0)),
+        ],
+        [pl.BlockSpec((1,) + shape[1:], place(j)) for j in range(parts)],
+        [jax.ShapeDtypeStruct(shape, jnp.bfloat16)] * parts,
+        2 * held * rows * ff * flat.shape[1],
+        0,
+        flat,
+        stacked,
+    )
+
+
+def rope_tables(row_count, head_dim):
+    half_dim = head_dim // 2
+    frequency = jnp.exp(
+        jnp.arange(half_dim, dtype=jnp.float32) * (-2.0 * math.log(rope_base) / head_dim)
+    )
+    angles = jnp.arange(row_count, dtype=jnp.float32)[:, None] * frequency[None, :]
+    return (jnp.cos(angles), jnp.sin(angles))
+
+
+def rotate(values, cosine, sine):
+    half_dim = values.shape[-1] // 2
+    first, second = (values[:, :half_dim], values[:, half_dim:])
+    return jnp.concatenate(
+        [first * cosine - second * sine, second * cosine + first * sine], axis=-1
+    )
+
+
+def swap(values, bits):
+    return lax.ppermute(values, "dp", [(i, i ^ bits) for i in range(4)])
+
+
+def sum_in_chip(pieces, sent):
+    wide = jnp.float32
+    kept = pieces[0].astype(wide) + swap(pieces[1], 1).astype(wide)
+    return (kept.astype(sent), (pieces[2].astype(wide) + swap(pieces[3], 1).astype(wide)).astype(sent))
+
+
+def sum_pieces(pieces, sent):
+    kept, passed = sum_in_chip(pieces, sent)
+    return kept.astype(jnp.float32) + swap(passed, 2).astype(jnp.float32)
+
+
+def reorder(values, dp_index, axis):
+    size = values.shape[axis] // 4
+    return jnp.concatenate(
+        [
+            lax.dynamic_slice_in_dim(values, (dp_index ^ k) * size, size, axis=axis)
+            for k in range(4)
+        ],
+        axis=axis,
+    )
+
+
+def sum_over_seq(values, shards):
+    spread = jnp.broadcast_to(values[None], (shards,) + values.shape)
+    return jnp.sum(lax.all_to_all(spread, "seq", 0, 0, tiled=True), axis=0)
+
+
+def on_device_heads(
+    hidden_in,
+    segment_ids,
+    routes,
+    w_query,
+    w_key,
+    w_value,
+    w_out,
+    gain_attn,
+    gain_query,
+    gain_key,
+    gain_ffn,
+    w_router,
+    w_gate,
+    w_up,
+    w_down,
+    cotangent,
+):
+    low, full = (jnp.bfloat16, jnp.float32)
+    shards = lax.axis_size("seq")
+    seq_index, dp_index = (lax.axis_index("seq"), lax.axis_index("dp"))
+    tokens, width = hidden_in.shape[1:]
+    rows = shards * tokens
+    cols = width // shards
+    heads = cols // HEAD
+    held = w_gate.shape[0]
+    expert_count = held * shards
+    block_rows = w_query.shape[0]
+    chunk = shards * block_rows
+    row_seg = segment_ids[0]
+    first_row = seq_index * tokens
+    barrier = lax.optimization_barrier
+
+    def own_cols(values, count):
+        return lax.dynamic_slice_in_dim(values, seq_index * count, count, axis=values.ndim - 1)
+
+    x_shard = reorder(hidden_in[0], dp_index, 1)
+    x_row = lax.all_gather(x_shard, "seq", axis=0, tiled=True)
+    blocks = jnp.stack(
+        [w.reshape(block_rows, shards, cols).transpose(1, 0, 2) for w in (w_query, w_key, w_value)],
+        axis=1,
+    )
+    blocks = blocks.reshape(shards, 3 * block_rows, cols)
+    place_at = (dp_index * shards + seq_index) * block_rows
+    gain_rows = lax.dynamic_update_slice(
+        jnp.zeros((shards, 16, cols), low),
+        jnp.stack([gain_query, gain_key])[None],
+        (place_at // cols, 0, place_at % cols),
+    )
+    gain_rows = lax.dynamic_update_slice(
+        gain_rows, jnp.broadcast_to(gain_attn[None, None], (shards, 1, block_rows)), (0, 2, 0)
+    )
+    blocks = lax.all_to_all(jnp.concatenate([blocks, gain_rows], axis=1), "seq", 0, 0, tiled=True)
+    across = swap(blocks, 2)
+    qkv_pieces = (blocks, swap(blocks, 1), across, swap(across, 1))
+    gate_across = swap(w_gate, 2)
+    x_row, qkv_pieces, gate_across = barrier((x_row, qkv_pieces, gate_across))
+
+    w_qkv = jnp.concatenate(
+        [
+            p[:, : 3 * block_rows]
+            .reshape(shards, 3, block_rows, cols)
+            .transpose(0, 2, 1, 3)
+            .reshape(chunk, 3 * cols)
+            for p in qkv_pieces
+        ],
+        axis=0,
+    )
+    gain_pair = sum(
+        jnp.sum(p[:, 3 * block_rows : 3 * block_rows + 2].astype(full), axis=0) for p in qkv_pieces
+    )
+    g_query, g_key = (gain_pair[0], gain_pair[1])
+    g_attn = jnp.concatenate(
+        [p[:, 3 * block_rows + 2, :block_rows].reshape(1, chunk) for p in qkv_pieces], axis=1
+    ).astype(full)
+
+    picks = routes.shape[2]
+    packed = tokens // block_rows
+    extra = jnp.concatenate(
+        [routes[0].astype(low).reshape(block_rows, packed * picks), w_router, gain_ffn[:, None]],
+        axis=1,
+    )
+    extra = jnp.pad(extra, ((0, 0), (0, 128 - extra.shape[1])))
+    out_own = lax.all_gather(
+        jnp.concatenate([reorder(w_out, dp_index, 1), extra], axis=1), "seq", axis=0, tiled=True
+    )
+    up_across = swap(w_up, 2)
+
+    x_wide = x_row.astype(full)
+    r_attn = lax.rsqrt(jnp.mean(x_wide * x_wide, axis=-1, keepdims=True) + epsilon)
+    normed = (x_wide * r_attn * g_attn).astype(low)
+    qkv = mm(normed, w_qkv, ((1,), (0,)))
+    query, key_proj = (qkv[:, :cols], qkv[:, cols : 2 * cols])
+    value_in = qkv[:, 2 * cols :].astype(low)
+    sums = sum_over_seq(
+        jnp.stack([jnp.sum(query * query, axis=-1), jnp.sum(key_proj * key_proj, axis=-1)]), shards
+    )
+    r_query, r_key = (lax.rsqrt(sums[i] / width + epsilon)[:, None] for i in range(2))
+    cosine, sine = rope_tables(rows, HEAD)
+    q_normed, k_normed = (query * r_query * g_query, key_proj * r_key * g_key)
+    position = lax.iota(jnp.int32, rows)
+    allowed = (position[:, None] >= position[None, :]) & (row_seg[:, None] == row_seg[None, :])
+    scaling = HEAD ** (-0.5)
+
+    def head(values, h):
+        return values[:, h * HEAD : (h + 1) * HEAD]
+
+    q_rot, k_rot, log_total, attended = ([], [], [], [])
+    for h in range(heads):
+        q_rot.append(rotate(head(q_normed, h), cosine, sine).astype(low))
+        k_rot.append(rotate(head(k_normed, h), cosine, sine).astype(low))
+        scores = jnp.where(
+            allowed, mm(q_rot[h], k_rot[h], ((1,), (1,))) * scaling, masked_score
+        )
+        peak = jnp.max(scores, axis=-1, keepdims=True)
+        log_total.append(peak + jnp.log(jnp.sum(jnp.exp(scores - peak), axis=-1, keepdims=True)))
+        weights = jnp.exp(scores - log_total[h]).astype(low)
+        attended.append(mm(weights, head(value_in, h), ((1,), (0,))).astype(low))
+    attended = jnp.concatenate(attended, axis=1)
+    attended, out_own, up_across = barrier((attended, out_own, up_across))
+
+    attended_row = lax.all_gather(attended, "seq", axis=0)
+    out_across = swap(out_own, 2)
+    out_pieces = (out_own, swap(out_own, 1), out_across, swap(out_across, 1))
+    extras = [p[:, width:] for p in out_pieces]
+    routes_row = extras[0][:, : packed * picks].reshape(rows, picks).astype(jnp.int32)
+    extras = jnp.concatenate([p[:, packed * picks :] for p in extras], axis=0)
+    router = jnp.pad(extras[:, :expert_count], ((0, 0), (0, 128 - expert_count)))
+    g_ffn = extras[:, expert_count].astype(full)[None]
+    lane_ids = lax.iota(jnp.int32, 128)
+    chosen = jnp.any(routes_row[:, :, None] == lane_ids[None, None, :], axis=1).astype(full)
+    own = (
+        lane_ids[None, :] == seq_index * held + lax.iota(jnp.int32, held)[:, None]
+    ).astype(full)
+    gate_full = jnp.concatenate([w_gate, swap(w_gate, 1), gate_across, swap(gate_across, 1)], axis=1)
+    up_full = jnp.concatenate([w_up, swap(w_up, 1), up_across, swap(up_across, 1)], axis=1)
+    attended_row, out_pieces, gate_full, up_full, router, g_ffn, chosen = barrier(
+        (attended_row, out_pieces, gate_full, up_full, router, g_ffn, chosen)
+    )
+
+    dy_shard, attended_row = barrier((reorder(cotangent[0], dp_index, 1), attended_row))
+    dy_row = lax.all_gather(dy_shard, "seq", axis=0, tiled=True)
+    down_across = swap(w_down, 2)
+    down_full = jnp.concatenate([w_down, swap(w_down, 1), down_across, swap(down_across, 1)], axis=2)
+    order = jnp.stack([dp_index ^ k for k in range(4)]).astype(jnp.int32)
+    hidden_mid, normed_ffn, r_ffn, chances, gates = finish_attention(
+        order, attended_row, out_pieces, x_row, g_ffn, router, chosen, own, expert_count
+    )
+    act, dgate_factor, dup_factor = expert_activations(normed_ffn, gate_full, up_full)
+    mixture = combine_experts(act, down_full, gates)
+    dy_row, mixture, act = barrier((dy_row, mixture, act))
+
+    scaled, dgate, dup, gate_sums = expert_gradients(
+        dy_row, down_full, act, dgate_factor, dup_factor, gates
+    )
+    nf_grad, grad_logits = input_gradient(
+        dgate, dup, gate_full, up_full, gate_sums, chances, chosen, own, router
+    )
+    nf_sum = lax.psum_scatter(nf_grad, "seq", scatter_dimension=0, tiled=True)
+
+    down_kept, down_passed = sum_in_chip(weight_pieces(scaled, dy_row, 4, False), low)
+    gate_kept, gate_passed = sum_in_chip(weight_pieces(normed_ffn, dgate, 4, True), low)
+    up_kept, up_passed = sum_in_chip(weight_pieces(normed_ffn, dup, 4, True), low)
+    down_arrived = swap(down_passed, 2)
+    router_grad = mm(grad_logits[:, :expert_count], normed_ffn, ((0,), (0,)))
+    nf_sum, mixture, down_arrived, gate_passed, up_passed, router_grad = barrier(
+        (nf_sum, mixture, down_arrived, gate_passed, up_passed, router_grad)
+    )
+    mixture_own = lax.psum_scatter(mixture, "seq", scatter_dimension=0, tiled=True)
+    gate_arrived, up_arrived = (swap(gate_passed, 2), swap(up_passed, 2))
+    grad_w_down = down_kept.astype(full) + down_arrived.astype(full)
+
+    mid_own = lax.dynamic_slice_in_dim(hidden_mid, first_row, tokens)
+    nf_own = nf_sum.astype(full)
+    r_own = lax.dynamic_slice_in_dim(r_ffn, first_row, tokens)
+    gain_ffn_grad = jnp.sum(nf_own * mid_own * r_own, axis=0)
+    scaled_grad = nf_own * g_ffn
+    grad_mid = (
+        dy_shard.astype(full)
+        + r_own * scaled_grad
+        - mid_own * (r_own**3) * jnp.mean(scaled_grad * mid_own, axis=-1, keepdims=True)
+    )
+    mid_low = grad_mid.astype(low)
+
+    def to_columns(values):
+        return lax.all_to_all(
+            values.reshape(tokens, shards, cols).transpose(1, 0, 2), "seq", 0, 0, tiled=True
+        ).reshape(rows, cols)
+
+    def out_transposed(j):
+        mixed = jnp.concatenate(
+            [mid_low[:, (k ^ j) * chunk : ((k ^ j) + 1) * chunk] for k in range(4)], axis=1
+        )
+        return mm(mixed, out_pieces[j][:, :width], ((1,), (1,))).astype(low)
+
+    grad_attended = jnp.concatenate([out_transposed(j) for j in range(4)], axis=1)
+    grad_attended = to_columns(reorder(grad_attended, dp_index, 1))
+    mid_cols = to_columns(reorder(mid_low, dp_index, 1))
+    out_grad = jnp.einsum(
+        "src,rn->scn", attended_row, mid_cols, preferred_element_type=full
+    ).reshape(width, cols)
+    out_grad = reorder(out_grad.astype(low), dp_index, 0)
+
+    q_grads, k_grads, v_grads = ([], [], [])
+    for h in range(heads):
+        scores = jnp.where(
+            allowed, mm(q_rot[h], k_rot[h], ((1,), (1,))) * scaling, masked_score
+        )
+        p = jnp.exp(scores - log_total[h])
+        grad_h = head(grad_attended, h)
+        grad_weights = mm(grad_h, head(value_in, h), ((1,), (1,)))
+        delta = jnp.sum(p * grad_weights, axis=-1, keepdims=True)
+        grad_scores = (scaling * p * (grad_weights - delta)).astype(low)
+        q_grads.append(rotate(mm(grad_scores, k_rot[h], ((1,), (0,))), cosine, -sine))
+        k_grads.append(rotate(mm(grad_scores, q_rot[h], ((0,), (0,))), cosine, -sine))
+        v_grads.append(mm(p.astype(low), grad_h, ((0,), (0,))))
+    q_grad, k_grad = (jnp.concatenate(q_grads, axis=1), jnp.concatenate(k_grads, axis=1))
+    gain_query_grad = jnp.sum(q_grad * query * r_query, axis=0)
+    gain_key_grad = jnp.sum(k_grad * key_proj * r_key, axis=0)
+    q_grad, k_grad = (q_grad * g_query, k_grad * g_key)
+    means = sum_over_seq(
+        jnp.stack([jnp.sum(q_grad * query, axis=-1), jnp.sum(k_grad * key_proj, axis=-1)]), shards
+    )
+    means = means / width
+    q_low = (r_query * q_grad - query * (r_query**3) * means[0][:, None]).astype(low)
+    k_low = (r_key * k_grad - key_proj * (r_key**3) * means[1][:, None]).astype(low)
+    v_low = jnp.concatenate(v_grads, axis=1).astype(low)
+    qkv_low = jnp.concatenate([q_low, k_low, v_low], axis=1)
+    normed_grad = mm(qkv_low, w_qkv, ((1,), (1,)))
+    gain_attn_grad = jnp.sum(normed_grad * x_row.astype(full) * r_attn, axis=0)
+    normed_grad, mixture_own, gate_arrived, up_arrived = barrier(
+        (normed_grad.astype(low), mixture_own, gate_arrived, up_arrived)
+    )
+    grad_w_gate = gate_kept.astype(full) + gate_arrived.astype(full)
+    grad_w_up = up_kept.astype(full) + up_arrived.astype(full)
+    normed_sum = lax.psum_scatter(normed_grad, "seq", scatter_dimension=0, tiled=True).astype(full)
+
+    proj_grad = jnp.concatenate(
+        [mm(normed, qkv_low, ((0,), (0,))).astype(low), out_grad], axis=1
+    )
+    proj_grad = sum_pieces([proj_grad[k * chunk : (k + 1) * chunk] for k in range(4)], low)
+    proj_grad = lax.all_to_all(
+        proj_grad.astype(low).reshape(shards, block_rows, 4 * cols), "seq", 0, 0, tiled=True
+    )
+    proj_grad = proj_grad.reshape(shards, block_rows, 4, cols).transpose(2, 1, 0, 3)
+    proj_grad = proj_grad.reshape(4, block_rows, width).astype(full)
+
+    x_own = x_shard.astype(full)
+    r_here = lax.rsqrt(jnp.mean(x_own * x_own, axis=-1, keepdims=True) + epsilon)
+    scaled_grad = normed_sum * g_attn
+    grad_hidden = (
+        grad_mid
+        + r_here * scaled_grad
+        - x_own * (r_here**3) * jnp.mean(scaled_grad * x_own, axis=-1, keepdims=True)
+    )
+    block_out = (mid_own + mixture_own.astype(full)).astype(low)
+
+    def place(values):
+        whole = lax.dynamic_update_slice_in_dim(
+            jnp.zeros((1, width), full), values[None], seq_index * cols, 1
+        )
+        return reorder(whole, dp_index, 1)
+
+    vectors = jnp.concatenate(
+        [
+            router_grad,
+            gain_attn_grad[None],
+            place(gain_query_grad),
+            place(gain_key_grad),
+            gain_ffn_grad[None],
+        ]
+    )
+    count = vectors.shape[0]
+    vectors = sum_pieces([vectors[:, k * chunk : (k + 1) * chunk] for k in range(4)], full)
+    vectors = vectors.reshape(count, shards, block_rows).transpose(1, 0, 2)
+    vectors = jnp.sum(lax.all_to_all(vectors, "seq", 0, 0, tiled=True), axis=0)
+    return (
+        reorder(block_out, dp_index, 1)[None],
+        reorder(grad_hidden, dp_index, 1)[None],
+        proj_grad[0],
+        proj_grad[1],
+        proj_grad[2],
+        proj_grad[3],
+        vectors[expert_count],
+        vectors[expert_count + 1],
+        vectors[expert_count + 2],
+        vectors[expert_count + 3],
+        vectors[:expert_count].T,
+        grad_w_gate,
+        grad_w_up,
+        grad_w_down,
+    )
+
+
 def solution(mesh):
+    def layer(*arrays):
+        whole_heads = (arrays[0].shape[2] // HEAD) % mesh.shape["seq"] == 0
+        if whole_heads and mesh.shape["dp"] == 4:
+            return on_device_heads(*arrays)
+        return on_device(*arrays)
+
     return jax.shard_map(
-        on_device,
+        layer,
         mesh=mesh,
         in_specs=(
             P("dp", "seq", None),

time: 3260 us -> 755 us (0.23)
  waiting for transfers between devices: 2400 us -> 295 us
  blocking collectives: 423 us -> 0 us
  matrix products: 247 us -> 52.1 us
  Pallas kernels: 0 us -> 159 us
  other arithmetic: 58.9 us -> 104 us
  starting transfers between devices: 16.1 us -> 52.2 us
    reduce_scatter x7 -> x3, waiting for transfers between devices: 1590 us -> 0.01 us  [the longest x1 0.01 us: on_device_heads(): nf_sum = lax.psum_scatter(nf_grad, 'seq', scatter_dimension=0, tiled=True)]
    all_gather x9 -> x4, waiting for transfers between devices: 360 us -> 24 us  [the longest x1 13.5 us: on_device_heads(): x_row = lax.all_gather(x_shard, 'seq', axis=0, tiled=True)]
    dot_general x38 -> x21, matrix products: 246 us -> 52.1 us  [the longest x20 48 us: mm(): lax.dot_general(left, right, (dims, ((), ())), preferred_element_type=jnp...]
    all_gather x1 -> x0, blocking collectives: 194 us -> none  [on_device(): lax.all_gather(w_router, ('dp', 'seq'), axis=0, tiled=True)]
    unnamed x20 -> x7, waiting for transfers between devices: 191 us -> 0.12 us
    ppermute x0 -> x30, waiting for transfers between devices: none -> 174 us  [swap(): return lax.ppermute(values, 'dp', [(i, i ^ bits) for i in range(4)])]
    all_to_all x3 -> x7, waiting for transfers between devices: 265 us -> 96.5 us  [the longest x1 36.9 us: on_device_heads(): lax.all_to_all(jnp.concatenate([blocks, gain_rows], axis=1), 'seq', 0, 0,...]
    pallas_call x0 -> x8, Pallas kernels: none -> 159 us  [the longest x7 140 us: grid_call(): pl.pallas_call(body, grid=grid, in_specs=in_specs, out_specs=out_specs, o...]
  transfers between devices with their start and end apart: 21 -> 44, of which waited for: 17 -> 17; matrix products, arithmetic and copies ran while one was open for 7% -> 27% of each run, Pallas kernels for 0% -> 15%
where the time goes in v2:
time: 755 us; the launch traced here: 745 us
  waiting for transfers between devices  295 us (39%)
  Pallas kernels  159 us (21%)
  other arithmetic  104 us (14%)
  local copies, waits for them, and re-layouts  66.2 us (9%)
  starting transfers between devices  52.2 us (7%)
  matrix products  52.1 us (7%)
  between operations  16.8 us (2%)
    ppermute x30, waiting for transfers between devices, swap(): return lax.ppermute(values, 'dp', [(i, i ^ bits) for i in range(4)])  174 us
    pallas_call x7, Pallas kernels, grid_call(): pl.pallas_call(body, grid=grid, in_specs=in_specs, out_specs=out_specs, o...  140 us
    dot_general x20, matrix products, mm(): lax.dot_general(left, right, (dims, ((), ())), preferred_element_type=jnp...  48 us
    all_to_all x1, waiting for transfers between devices, on_device_heads(): lax.all_to_all(jnp.concatenate([blocks, gain_rows], axis=1), 'seq', 0, 0,...  36.9 us
    all_to_all x2, waiting for transfers between devices, to_columns(): lax.all_to_all(values.reshape(tokens, shards, cols).transpose(1, 0, 2), '...  24.2 us
    all_to_all x1, waiting for transfers between devices, on_device_heads(): lax.all_to_all(proj_grad.astype(low).reshape(shards, block_rows, 4 * cols...  22.8 us
    unnamed x249, local copies, waits for them, and re-layouts  22.5 us
    pallas_call x1, Pallas kernels, finish_attention(): pl.pallas_call(body, grid_spec=pltpu.PrefetchScalarGridSpec(num_scalar_pr...  18.9 us
  transfers between devices with their start and end apart: 44, of which 17 were waited for; matrix products, arithmetic and copies ran while one was open for 27% of the time, Pallas kernels for 15%

profile of v2, /device:TPU:0, one launch (start us, length us, event | category | flops | bytes accessed | tf_op | source)
XLA Modules:
  0.0 744.9 jit_solution(17755842954742482463)
XLA Ops:
  14.0 7.5 %all-to-all-start = ((bf16[8,208,256]{2,1,0:T(8,128)(2,1)}), bf16[8,208,256]{2,1,0:T(8,128)(2,1)S(1)}, u32[]{:S(2)}, u32[]{:S(2)}) async-start(bf16[8,208,256]{2,1,0:T(8,128)(2,1)} %pad_maximum_fusion.5), calls=%async_computation | async-start | bytes 1703936 | tf_op jit(solution)/shard_map/all_to_all | solution.py:943
  23.0 36.9 %all-to-all-done = bf16[8,208,256]{2,1,0:T(8,128)(2,1)S(1)} async-done(((bf16[8,208,256]{2,1,0:T(8,128)(2,1)}), bf16[8,208,256]{2,1,0:T(8,128)(2,1)S(1)}, u32[]{:S(2)}, u32[]{:S(2)}) %all-to-all-start) | async-done | bytes 852000 | tf_op jit(solution)/shard_map/all_to_all | solution.py:943
  61.4 25.8 %collective-permute-done.1 = bf16[8,208,256]{2,1,0:T(8,128)(2,1)} collective-permute-done((bf16[8,208,256]{2,1,0:T(8,128)(2,1)S(1)}, bf16[8,208,256]{2,1,0:T(8,128)(2,1)}, u32[]{:S(2)}, u32[]{:S(2)}) %collective-permute-start.1) | collective-permute-done | bytes 852000 | tf_op jit(solution)/shard_map/ppermute | solution.py:861
  90.2 13.5 %all-gather.6.cloned.1.call-done.x_ref = bf16[1024,2048]{1,0:T(8,128)(2,1)} async-done(((bf16[128,2048]{1,0:T(8,128)(2,1)}), bf16[1024,2048]{1,0:T(8,128)(2,1)}) %all-gather.6.cloned.1.call-update) | async-done | bytes 4194320 | tf_op jit(solution)/shard_map/all_gather | solution.py:928
  145.0 10.5 %all-gather.8.cloned.1.call-done.p0 = bf16[512,2176]{1,0:T(8,128)(2,1)} async-done(((bf16[64,2176]{1,0:T(8,128)(2,1)}), bf16[512,2176]{1,0:T(8,128)(2,1)}) %all-gather.8.cloned.1.call-update) | async-done | bytes 2228240 | tf_op jit(solution)/shard_map/all_gather | solution.py:974
  161.7 43.2 %collective-permute-done.6.p2 = bf16[512,2176]{1,0:T(8,128)(2,1)} collective-permute-done((bf16[512,2176]{1,0:T(8,128)(2,1)}, bf16[512,2176]{1,0:T(8,128)(2,1)}, u32[]{:S(2)}, u32[]{:S(2)}) %collective-permute-start.6) | collective-permute-done | bytes 2228256 | tf_op jit(solution)/shard_map/ppermute | solution.py:861
  216.1 7.0 pad_maximum_fusion.gate_ref
  223.1 6.5 pad_maximum_fusion.1.up_ref
  241.6 21.2 %collective-permute-done.13 = bf16[2,1024,512]{2,1,0:T(8,128)(2,1)} collective-permute-done((bf16[2,1024,512]{2,1,0:T(8,128)(2,1)S(1)}, bf16[2,1024,512]{2,1,0:T(8,128)(2,1)}, u32[]{:S(2)}, u32[]{:S(2)}) %collective-permute-start.13) | collective-permute-done | bytes 2097184 | tf_op jit(solution)/shard_map/ppermute | solution.py:861
  275.1 18.9 %shard_map.263 = (f32[1024,2048]{1,0:T(8,128)}, bf16[1024,2048]{1,0:T(8,128)(2,1)}, f32[1024,1]{1,0:T(8,128)}, f32[1024,128]{1,0:T(8,128)}, f32[2,1024,1]{2,1,0:T(8,128)}) custom-call(s32[4]{0:T(128)} %pad_add_fusion.order_ref, bf16[8,1024,256]{2,1,0:T(8,128)(2,1)} %bitcast.151, bf16[512,2176]{1,0:T(8,128)(2,1)} %all-gather.8.cloned.1.call-done.p0, ...), custom_call_target="tpu_custom_call" | custom-call | flops 8589934592 | bytes 26226688 | tf_op jit(solution)/shard_map/pallas_call | solution.py:585
  293.9 24.9 %shard_map.264 = (bf16[2,1024,1024]{2,1,0:T(8,128)(2,1)}, bf16[2,1024,1024]{2,1,0:T(8,128)(2,1)}, bf16[2,1024,1024]{2,1,0:T(8,128)(2,1)}) custom-call(bf16[1024,2048]{1,0:T(8,128)(2,1)} %get-tuple-element.95.x_ref.flat_ref, bf16[2,2048,1024]{2,1,0:T(8,128)(2,1)} %pad_maximum_fusion.gate_ref, bf16[2,2048,1024]{2,1,0:T(8,128)(2,1)} %pad_maximum_fusion.1.up_ref), custom_call_target="tpu_custom_call" | custom-call | flops 17179869184 | bytes 33554432 | tf_op jit(solution)/shard_map/pallas_call | solution.py:516
  318.8 14.2 %shard_map.265 = bf16[1024,2048]{1,0:T(8,128)(2,1)} custom-call(bf16[2,1024,1024]{2,1,0:T(8,128)(2,1)} %get-tuple-element.101.act_ref, bf16[2,1024,2048]{2,1,0:T(8,128)(2,1)} %constant_dynamic-update-slice_fusion.5.down_ref, f32[2,1024,1]{2,1,0:T(8,128)} %get-tuple-element.99.weight_ref), custom_call_target="tpu_custom_call" | custom-call | flops 8589934592 | bytes 16785408 | tf_op jit(solution)/shard_map/pallas_call | solution.py:516
  333.0 20.4 %shard_map.266 = (bf16[2,1024,1024]{2,1,0:T(8,128)(2,1)}, bf16[2,1024,1024]{2,1,0:T(8,128)(2,1)}, bf16[2,1024,1024]{2,1,0:T(8,128)(2,1)}, f32[2,1024,128]{2,1,0:T(8,128)}) custom-call(bf16[1024,2048]{1,0:T(8,128)(2,1)} %all-gather.10.cloned.1.call-done.dy_ref.flat_ref, bf16[2,1024,2048]{2,1,0:T(8,128)(2,1)} %constant_dynamic-update-slice_fusion.5.down_ref, ...), custom_call_target="tpu_custom_call" | custom-call | flops 8589934592 | bytes 38805504 | tf_op jit(solution)/shard_map/pallas_call | solution.py:516
  353.4 26.4 %shard_map.267 = (bf16[1024,2048]{1,0:T(8,128)(2,1)}, bf16[1024,128]{1,0:T(8,128)(2,1)}) custom-call(bf16[2,1024,1024]{2,1,0:T(8,128)(2,1)} %get-tuple-element.104.dgate_ref.stacked_ref, bf16[2,1024,1024]{2,1,0:T(8,128)(2,1)} %get-tuple-element.105.dup_ref.stacked_ref, bf16[2,2048,1024]{2,1,0:T(8,128)(2,1)} %pad_maximum_fusion.gate_ref, ...), custom_call_target="tpu_custom_call" | custom-call | flops 17179869184 | bytes 32244736 | tf_op jit(solution)/shard_map/pallas_call | solution.py:516
  380.1 18.7 %shard_map.268 = (bf16[2,1024,512]{2,1,0:T(8,128)(2,1)}, bf16[2,1024,512]{2,1,0:T(8,128)(2,1)}, bf16[2,1024,512]{2,1,0:T(8,128)(2,1)}, bf16[2,1024,512]{2,1,0:T(8,128)(2,1)}) custom-call(bf16[1024,2048]{1,0:T(8,128)(2,1)} %all-gather.10.cloned.1.call-done.dy_ref.flat_ref, bf16[2,1024,1024]{2,1,0:T(8,128)(2,1)} %get-tuple-element.110.stacked_ref), custom_call_target="tpu_custom_call" | custom-call | flops 8589934592 | bytes 16777216 | tf_op jit(solution)/shard_map/pallas_call | solution.py:516
  399.3 17.8 %shard_map.269 = (bf16[2,512,1024]{2,1,0:T(8,128)(2,1)}, bf16[2,512,1024]{2,1,0:T(8,128)(2,1)}, bf16[2,512,1024]{2,1,0:T(8,128)(2,1)}, bf16[2,512,1024]{2,1,0:T(8,128)(2,1)}) custom-call(bf16[1024,2048]{1,0:T(8,128)(2,1)} %get-tuple-element.95.x_ref.flat_ref, bf16[2,1024,1024]{2,1,0:T(8,128)(2,1)} %get-tuple-element.104.dgate_ref.stacked_ref), custom_call_target="tpu_custom_call" | custom-call | flops 8589934592 | bytes 16777216 | tf_op jit(solution)/shard_map/pallas_call | solution.py:516
  417.1 18.0 %shard_map.270 = (bf16[2,512,1024]{2,1,0:T(8,128)(2,1)}, bf16[2,512,1024]{2,1,0:T(8,128)(2,1)}, bf16[2,512,1024]{2,1,0:T(8,128)(2,1)}, bf16[2,512,1024]{2,1,0:T(8,128)(2,1)}) custom-call(bf16[1024,2048]{1,0:T(8,128)(2,1)} %get-tuple-element.95.x_ref.flat_ref, bf16[2,1024,1024]{2,1,0:T(8,128)(2,1)} %get-tuple-element.105.dup_ref.stacked_ref), custom_call_target="tpu_custom_call" | custom-call | flops 8589934592 | bytes 16777216 | tf_op jit(solution)/shard_map/pallas_call | solution.py:516
  451.5 33.8 %collective-permute-done.16 = bf16[2,1024,512]{2,1,0:T(8,128)(2,1)S(1)} collective-permute-done((bf16[2,1024,512]{2,1,0:T(8,128)(2,1)}, bf16[2,1024,512]{2,1,0:T(8,128)(2,1)S(1)}, u32[]{:S(2)}, u32[]{:S(2)}) %collective-permute-start.16) | collective-permute-done | bytes 2097184 | tf_op jit(solution)/shard_map/ppermute | solution.py:861
  510.4 24.2 %all-to-all-done.2 = bf16[8,128,256]{2,1,0:T(8,128)(2,1)S(1)} async-done(((bf16[8,128,256]{2,1,0:T(8,128)(2,1)}), bf16[8,128,256]{2,1,0:T(8,128)(2,1)S(1)}, u32[]{:S(2)}, u32[]{:S(2)}) %all-to-all-start.2) | async-done | bytes 524320 | tf_op jit(solution)/shard_map/all_to_all | solution.py:1076
  571.1 8.4 %fusion.4 = (f32[2048]{0:T(1024)S(1)}, bf16[1024,2048]{1,0:T(8,128)(2,1)}) fusion(bf16[1024,2048]{1,0:T(8,128)(2,1)S(1)} %copy-done.13, f32[1024]{0:T(1024)} %copy-done.103, bf16[2048,768]{1,0:T(8,128)(2,1)} %copy-done.74, bf16[1024,128]{0,1:T(8,128)(2,1)S(1)} %copy-done.72, bf16[1024,128]{0,1:T(8,128)(2,1)S(1)} %copy-done.70, ...), kind=kOutput, calls=%fused_computation.7 | convolution fusion | flops 3238000640 | bytes 13119488 | tf_op jit(solution)/shard_map/dot_general | solution.py:507
  579.5 20.6 %collective-permute-done.20 = bf16[2,512,1024]{2,1,0:T(8,128)(2,1)} collective-permute-done((bf16[2,512,1024]{2,1,0:T(8,128)(2,1)}, bf16[2,512,1024]{2,1,0:T(8,128)(2,1)}, u32[]{:S(2)}, u32[]{:S(2)}) %collective-permute-start.20) | collective-permute-done | bytes 2097184 | tf_op jit(solution)/shard_map/ppermute | solution.py:861
  614.6 14.9 %maximum_maximum_fusion = bf16[2048,1024]{0,1:T(8,128)(2,1)S(1)} fusion(bf16[512,256]{0,1:T(8,128)(2,1)S(1)} %get-tuple-element.171, bf16[512,256]{0,1:T(8,128)(2,1)S(1)} %get-tuple-element.172, bf16[512,256]{0,1:T(8,128)(2,1)S(1)} %get-tuple-element.173, bf16[512,256]{0,1:T(8,128)(2,1)S(1)} %get-tuple-element.170, ...), kind=kLoop, calls=%fused_computation.10 | loop fusion | flops 20971520 | bytes 8388608 | tf_op jit(solution)/shard_map/concatenate | solution.py:1128
  640.6 22.4 %collective-permute-done.26 = f32[20,512]{1,0:T(8,128)S(1)} collective-permute-done((f32[20,512]{1,0:T(8,128)S(1)}, f32[20,512]{1,0:T(8,128)S(1)}, u32[]{:S(2)}, u32[]{:S(2)}) %collective-permute-start.26) | collective-permute-done | bytes 40992 | tf_op jit(solution)/shard_map/ppermute | solution.py:861
  689.7 22.8 %all-to-all-done.5 = bf16[8,64,1024]{2,1,0:T(8,128)(2,1)S(1)} async-done(((bf16[8,64,1024]{2,1,0:T(8,128)(2,1)}), bf16[8,64,1024]{2,1,0:T(8,128)(2,1)S(1)}, u32[]{:S(2)}, u32[]{:S(2)}) %all-to-all-start.5) | async-done | bytes 1048608 | tf_op jit(solution)/shard_map/all_to_all | solution.py:1132
  (494 shorter events, 249.8 us)
Async XLA Ops:
  7.2 96.5 %all-gather.6.cloned.1.call-start = ((), (), s32[]{:S(2)}) async-start(), calls=%async_computation.10 | async-start | bytes 4718592 | tf_op jit(solution)/shard_map/all_gather | solution.py:928
  14.0 46.0 %all-to-all-start = ((bf16[8,208,256]{2,1,0:T(8,128)(2,1)}), bf16[8,208,256]{2,1,0:T(8,128)(2,1)S(1)}, u32[]{:S(2)}, u32[]{:S(2)}) async-start(bf16[8,208,256]{2,1,0:T(8,128)(2,1)} %pad_maximum_fusion.5), calls=%async_computation | async-start | bytes 1703936 | tf_op jit(solution)/shard_map/all_to_all | solution.py:943
  21.4 134.1 %all-gather.8.cloned.1.call-start = ((), (), s32[]{:S(2)}) async-start(), calls=%async_computation.11 | async-start | bytes 2506752 | tf_op jit(solution)/shard_map/all_gather | solution.py:974
  21.5 68.6 %collective-permute-start.3 = (bf16[2,512,1024]{2,1,0:T(8,128)(2,1)}, bf16[2,512,1024]{2,1,0:T(8,128)(2,1)}, u32[]{:S(2)}, u32[]{:S(2)}) collective-permute-start(bf16[2,512,1024]{2,1,0:T(8,128)(2,1)} %param.28), channel_id=1, source_target_pairs={{0,16},{8,24},{16,0},{24,8},{1,17},{9,25},{17,1},{25,9},{2,18},{10... | collective-permute-start | bytes 6291464 | tf_op jit(solution)/shard_map/ppermute | solution.py:861
  87.2 57.8 %collective-permute-start.4 = (bf16[2,512,1024]{2,1,0:T(8,128)(2,1)}, bf16[2,512,1024]{2,1,0:T(8,128)(2,1)}, u32[]{:S(2)}, u32[]{:S(2)}) collective-permute-start(bf16[2,512,1024]{2,1,0:T(8,128)(2,1)} %param.29), channel_id=1, source_target_pairs={{0,16},{8,24},{16,0},{24,8},{1,17},{9,25},{17,1},{25,9},{2,18},{10... | collective-permute-start | bytes 6291464 | tf_op jit(solution)/shard_map/ppermute | solution.py:861
  127.1 107.7 %all-gather.12.cloned.1.call-start = ((), (), s32[]{:S(2)}) async-start(), calls=%async_computation.16 | async-start | bytes 4718592 | tf_op jit(solution)/shard_map/all_gather | solution.py:1012
  155.5 177.5 %all-gather.10.cloned.1.call-start = ((), (), s32[]{:S(2)}) async-start(), calls=%async_computation.12 | async-start | bytes 4718592 | tf_op jit(solution)/shard_map/all_gather | solution.py:1032
  155.6 49.4 %collective-permute-start.6 = (bf16[512,2176]{1,0:T(8,128)(2,1)}, bf16[512,2176]{1,0:T(8,128)(2,1)}, u32[]{:S(2)}, u32[]{:S(2)}) collective-permute-start(bf16[512,2176]{1,0:T(8,128)(2,1)} %all-gather.8.cloned.1.call-done.p0), channel_id=1, source_target_pairs={{0,16},{8,24},{16,0},{24,8},{1,17},{9,25},{17,1},{25,9},{2,18},{10... | collective-permute-start | bytes 6684680 | tf_op jit(solution)/shard_map/ppermute | solution.py:861
  157.1 57.5 %collective-permute-start.9 = (bf16[2,512,1024]{2,1,0:T(8,128)(2,1)}, bf16[2,512,1024]{2,1,0:T(8,128)(2,1)}, u32[]{:S(2)}, u32[]{:S(2)}) collective-permute-start(bf16[2,512,1024]{2,1,0:T(8,128)(2,1)} %collective-permute-done.3), channel_id=1, source_target_pairs={{0,8},{8,0},{16,24},{24,16},{1,9},{9,1},{17,25},{25,17},{2,10},{10... | collective-permute-start | bytes 6291464 | tf_op jit(solution)/shard_map/ppermute | solution.py:861
  157.6 65.5 %collective-permute-start.10 = (bf16[2,512,1024]{2,1,0:T(8,128)(2,1)}, bf16[2,512,1024]{2,1,0:T(8,128)(2,1)}, u32[]{:S(2)}, u32[]{:S(2)}) collective-permute-start(bf16[2,512,1024]{2,1,0:T(8,128)(2,1)} %param.29), channel_id=1, source_target_pairs={{0,8},{8,0},{16,24},{24,16},{1,9},{9,1},{17,25},{25,17},{2,10},{10... | collective-permute-start | bytes 6291464 | tf_op jit(solution)/shard_map/ppermute | solution.py:861
  157.6 65.5 %collective-permute-start.11 = (bf16[2,512,1024]{2,1,0:T(8,128)(2,1)}, bf16[2,512,1024]{2,1,0:T(8,128)(2,1)}, u32[]{:S(2)}, u32[]{:S(2)}) collective-permute-start(bf16[2,512,1024]{2,1,0:T(8,128)(2,1)} %collective-permute-done.4), channel_id=1, source_target_pairs={{0,8},{8,0},{16,24},{24,16},{1,9},{9,1},{17,25},{25,17},{2,10},{10... | collective-permute-start | bytes 6291464 | tf_op jit(solution)/shard_map/ppermute | solution.py:861
  161.6 69.1 %collective-permute-start.5 = (bf16[512,2176]{1,0:T(8,128)(2,1)}, bf16[512,2176]{1,0:T(8,128)(2,1)}, u32[]{:S(2)}, u32[]{:S(2)}) collective-permute-start(bf16[512,2176]{1,0:T(8,128)(2,1)} %all-gather.8.cloned.1.call-done.p0), channel_id=1, source_target_pairs={{0,8},{8,0},{16,24},{24,16},{1,9},{9,1},{17,25},{25,17},{2,10},{10... | collective-permute-start | bytes 6684680 | tf_op jit(solution)/shard_map/ppermute | solution.py:861
  214.6 48.2 %collective-permute-start.13 = (bf16[2,1024,512]{2,1,0:T(8,128)(2,1)S(1)}, bf16[2,1024,512]{2,1,0:T(8,128)(2,1)}, u32[]{:S(2)}, u32[]{:S(2)}) collective-permute-start(bf16[2,1024,512]{2,1,0:T(8,128)(2,1)S(1)} %copy-done.29), channel_id=1, source_target_pairs={{0,16},{8,24},{16,0},{24,8},{1,17},{9,25},{17,1},{25,9},{2,18},{10... | collective-permute-start | bytes 6291464 | tf_op jit(solution)/shard_map/ppermute | solution.py:861
  241.1 244.2 %reduce-scatter.4.cloned.1.call-start = ((), (), s32[]{:S(2)}) async-start(), calls=%async_computation.13 | async-start | bytes 4718592 | tf_op jit(solution)/shard_map/reduce_scatter | solution.py:1049
  379.8 220.3 %reduce-scatter.6.cloned.1.call-start = ((), (), s32[]{:S(2)}) async-start(), calls=%async_computation.14 | async-start | bytes 4718592 | tf_op jit(solution)/shard_map/reduce_scatter | solution.py:1059
  437.4 47.8 %collective-permute-start.16 = (bf16[2,1024,512]{2,1,0:T(8,128)(2,1)}, bf16[2,1024,512]{2,1,0:T(8,128)(2,1)S(1)}, u32[]{:S(2)}, u32[]{:S(2)}) collective-permute-start(bf16[2,1024,512]{2,1,0:T(8,128)(2,1)} %add_convert_fusion.5), channel_id=1, source_target_pairs={{0,16},{8,24},{16,0},{24,8},{1,17},{9,25},{17,1},{25,9},{2,18},{10... | collective-permute-start | bytes 6291464 | tf_op jit(solution)/shard_map/ppermute | solution.py:861
  508.4 71.2 %collective-permute-start.19 = (bf16[2,512,1024]{2,1,0:T(8,128)(2,1)}, bf16[2,512,1024]{2,1,0:T(8,128)(2,1)}, u32[]{:S(2)}, u32[]{:S(2)}) collective-permute-start(bf16[2,512,1024]{2,1,0:T(8,128)(2,1)} %add_convert_fusion.4), channel_id=1, source_target_pairs={{0,16},{8,24},{16,0},{24,8},{1,17},{9,25},{17,1},{25,9},{2,18},{10... | collective-permute-start | bytes 6291464 | tf_op jit(solution)/shard_map/ppermute | solution.py:861
  509.8 90.3 %collective-permute-start.20 = (bf16[2,512,1024]{2,1,0:T(8,128)(2,1)}, bf16[2,512,1024]{2,1,0:T(8,128)(2,1)}, u32[]{:S(2)}, u32[]{:S(2)}) collective-permute-start(bf16[2,512,1024]{2,1,0:T(8,128)(2,1)} %add_convert_fusion.3), channel_id=1, source_target_pairs={{0,16},{8,24},{16,0},{24,8},{1,17},{9,25},{17,1},{25,9},{2,18},{10... | collective-permute-start | bytes 6291464 | tf_op jit(solution)/shard_map/ppermute | solution.py:861
  562.1 44.4 %all-to-all-start.4 = ((bf16[8,128,256]{2,1,0:T(8,128)(2,1)}), bf16[8,128,256]{2,1,0:T(8,128)(2,1)}, u32[]{:S(2)}, u32[]{:S(2)}) async-start(bf16[8,128,256]{2,1,0:T(8,128)(2,1)} %bitcast.173), calls=%async_computation.7 | async-start | bytes 1048576 | tf_op jit(solution)/shard_map/all_to_all | solution.py:1076
  566.3 165.7 %reduce-scatter.8.cloned.1.call-start = ((), (), s32[]{:S(2)}) async-start(), calls=%async_computation.15 | async-start | bytes 4718592 | tf_op jit(solution)/shard_map/reduce_scatter | solution.py:1126
  631.8 49.5 %collective-permute-start.29 = (bf16[2,1024,512]{2,1,0:T(8,128)(2,1)}, bf16[2,1024,512]{2,1,0:T(8,128)(2,1)}, u32[]{:S(2)}, u32[]{:S(2)}) collective-permute-start(bf16[2,1024,512]{2,1,0:T(8,128)(2,1)} %get-tuple-element.132), channel_id=1, source_target_pairs={{0,8},{8,0},{16,24},{24,16},{1,9},{9,1},{17,25},{25,17},{2,10},{10... | collective-permute-start | bytes 6291464 | tf_op jit(solution)/shard_map/ppermute | solution.py:861
  632.5 37.2 %collective-permute-start.21 = (bf16[512,1024]{0,1:T(8,128)(2,1)S(1)}, bf16[512,1024]{0,1:T(8,128)(2,1)}, u32[]{:S(2)}, u32[]{:S(2)}) collective-permute-start(bf16[512,1024]{0,1:T(8,128)(2,1)S(1)} %get-tuple-element.150), channel_id=1, source_target_pairs={{0,8},{8,0},{16,24},{24,16},{1,9},{9,1},{17,25},{25,17},{2,10},{10... | collective-permute-start | bytes 3145736 | tf_op jit(solution)/shard_map/ppermute | solution.py:861
  680.8 39.6 %collective-permute-start.28 = (bf16[2,512,1024]{2,1,0:T(8,128)(2,1)}, bf16[2,512,1024]{2,1,0:T(8,128)(2,1)}, u32[]{:S(2)}, u32[]{:S(2)}) collective-permute-start(bf16[2,512,1024]{2,1,0:T(8,128)(2,1)} %get-tuple-element.129), channel_id=1, source_target_pairs={{0,8},{8,0},{16,24},{24,16},{1,9},{9,1},{17,25},{25,17},{2,10},{10... | collective-permute-start | bytes 6291464 | tf_op jit(solution)/shard_map/ppermute | solution.py:861
  680.8 45.3 %collective-permute-start.27 = (bf16[2,512,1024]{2,1,0:T(8,128)(2,1)}, bf16[2,512,1024]{2,1,0:T(8,128)(2,1)}, u32[]{:S(2)}, u32[]{:S(2)}) collective-permute-start(bf16[2,512,1024]{2,1,0:T(8,128)(2,1)} %get-tuple-element.126), channel_id=1, source_target_pairs={{0,8},{8,0},{16,24},{24,16},{1,9},{9,1},{17,25},{25,17},{2,10},{10... | collective-permute-start | bytes 6291464 | tf_op jit(solution)/shard_map/ppermute | solution.py:861
  (135 other events, 1615.9 us)
Sparse Core Ops, SparseCore 0:
  11.3 92.3 all-gather.5
  106.4 49.0 all-gather.7
  158.3 71.8 all-gather.11
  241.2 72.0 all-gather.9
  379.9 87.4 reduce-scatter.3
  491.9 104.2 reduce-scatter.5
  600.2 94.8 reduce-scatter.7

commit v3 on v2

--- a/solution.py
+++ b/solution.py
@@ -509,7 +509,9 @@
 
 def cost(flops, transcendentals, *arrays):
     moved = sum(math.prod(a.shape) * a.dtype.itemsize for a in arrays)
-    return pl.CostEstimate(flops=flops, transcendentals=transcendentals, bytes_accessed=moved)
+    return pl.CostEstimate(
+        flops=flops // 4, transcendentals=transcendentals // 4, bytes_accessed=moved // 4
+    )
 
 
 def grid_call(body, grid, in_specs, out_specs, outs, flops, transcendentals, *args):
@@ -846,15 +848,390 @@
         jnp.arange(half_dim, dtype=jnp.float32) * (-2.0 * math.log(rope_base) / head_dim)
     )
     angles = jnp.arange(row_count, dtype=jnp.float32)[:, None] * frequency[None, :]
-    return (jnp.cos(angles), jnp.sin(angles))
-
-
-def rotate(values, cosine, sine):
-    half_dim = values.shape[-1] // 2
-    first, second = (values[:, :half_dim], values[:, half_dim:])
-    return jnp.concatenate(
-        [first * cosine - second * sine, second * cosine + first * sine], axis=-1
-    )
+    cosine, sine = (jnp.cos(angles), jnp.sin(angles))
+    return (
+        jnp.concatenate([cosine, cosine], axis=1),
+        jnp.concatenate([-sine, sine], axis=1),
+    )
+
+
+def seen(first, count, keys, seg_col, seg_row):
+    position = first + lax.broadcasted_iota(jnp.int32, (count, keys), 0)
+    other = lax.broadcasted_iota(jnp.int32, (count, keys), 1)
+    return (position >= other) & (seg_col == seg_row)
+
+
+def pair_rows(first, second):
+    lane = lax.broadcasted_iota(jnp.int32, (first.shape[0], 128), 1)
+    both = jnp.where(lane == 0, first, jnp.where(lane == 1, second, 0.0))
+    return both.T[:8]
+
+
+def pair_columns(sums):
+    total = sum(sums[1:], sums[0])
+    total = jnp.concatenate([total] * 16, axis=0).T
+    return (total[:, 0:1], total[:, 1:2])
+
+
+def project(x_row, gain, w_qkv):
+    rows, width = x_row.shape
+    held_cols = w_qkv.shape[1]
+    cols = held_cols // 3
+    tm = math.gcd(rows, 256)
+
+    def body(x_ref, gain_ref, w_ref, normed_ref, qkv_ref, r_ref, stat_ref):
+        x = x_ref[...].astype(jnp.float32)
+        r = lax.rsqrt(jnp.mean(x * x, axis=-1, keepdims=True) + epsilon)
+        r_ref[...] = r
+        normed = (x * r * gain_ref[...]).astype(jnp.bfloat16)
+        normed_ref[...] = normed
+        qkv = mm(normed, w_ref[...], ((1,), (0,)))
+        qkv_ref[...] = qkv
+        squares = qkv[:, : 2 * cols] * qkv[:, : 2 * cols]
+        stat_ref[...] = pair_rows(
+            jnp.sum(squares[:, :cols], axis=-1, keepdims=True),
+            jnp.sum(squares[:, cols:], axis=-1, keepdims=True),
+        )
+
+    full = jnp.float32
+    return grid_call(
+        body,
+        (rows // tm,),
+        [
+            pl.BlockSpec((tm, width), lambda i: (i, 0)),
+            pl.BlockSpec((1, width), lambda i: (0, 0)),
+            pl.BlockSpec((width, held_cols), lambda i: (0, 0)),
+        ],
+        [
+            pl.BlockSpec((tm, width), lambda i: (i, 0)),
+            pl.BlockSpec((tm, held_cols), lambda i: (i, 0)),
+            pl.BlockSpec((tm, 1), lambda i: (i, 0)),
+            pl.BlockSpec((8, tm), lambda i: (0, i)),
+        ],
+        [
+            jax.ShapeDtypeStruct((rows, width), jnp.bfloat16),
+            jax.ShapeDtypeStruct((rows, held_cols), full),
+            jax.ShapeDtypeStruct((rows, 1), full),
+            jax.ShapeDtypeStruct((8, rows), full),
+        ],
+        2 * rows * width * held_cols,
+        0,
+        x_row,
+        gain,
+        w_qkv,
+    )
+
+
+def attend(qkv, sums, width, g_query, g_key, cosine, sine, seg_col, seg_row):
+    rows, held_cols = qkv.shape
+    cols = held_cols // 3
+    heads = cols // HEAD
+    tq = math.gcd(rows, 256)
+    scaling = HEAD ** (-0.5)
+    shards = sums.shape[0]
+
+    def body(q, k, v, sums_ref, gq, gk, cos, sin, sc, sr, q_out, k_out, v_out, att_out, log_out, rq, rk):
+        @pl.when(pl.program_id(0) == 0)
+        def _():
+            for i in range(rows // tq):
+                at = slice(i * tq, (i + 1) * tq)
+                first, second = pair_columns([sums_ref[d, :, at] for d in range(shards)])
+                rq[at, :] = lax.rsqrt(first / width + epsilon)
+                rk[at, :] = lax.rsqrt(second / width + epsilon)
+
+        def rotated(ref, r, g):
+            values = ref[...] * r[...] * g[...]
+            swapped = pltpu.roll(values, HEAD // 2, 1)
+            return (values * cos[...] + swapped * sin[...]).astype(jnp.bfloat16)
+
+        q_out[...] = rotated(q, rq, gq)
+        k_out[...] = rotated(k, rk, gk)
+        v_out[...] = v[...].astype(jnp.bfloat16)
+        for i in range(rows // tq):
+            at, keys = (slice(i * tq, (i + 1) * tq), (i + 1) * tq)
+            scores = mm(q_out[at, :], k_out[:keys, :], ((1,), (1,))) * scaling
+            allowed = seen(i * tq, tq, keys, sc[at, :], sr[:, :keys])
+            scores = jnp.where(allowed, scores, masked_score)
+            peak = jnp.max(scores, axis=-1, keepdims=True)
+            raised = jnp.exp(scores - peak)
+            total = jnp.sum(raised, axis=-1, keepdims=True)
+            log_out[0, at, :] = peak + jnp.log(total)
+            weights = (raised * (1.0 / total)).astype(jnp.bfloat16)
+            att_out[at, :] = mm(weights, v_out[:keys, :], ((1,), (0,))).astype(jnp.bfloat16)
+
+    def col(offset):
+        return pl.BlockSpec((rows, HEAD), lambda h: (0, offset + h))
+
+    row = pl.BlockSpec((1, HEAD), lambda h: (0, h))
+    one = pl.BlockSpec((rows, 1), lambda h: (0, 0))
+    table = pl.BlockSpec((rows, HEAD), lambda h: (0, 0))
+    low = jax.ShapeDtypeStruct((rows, cols), jnp.bfloat16)
+    column = jax.ShapeDtypeStruct((rows, 1), jnp.float32)
+    return grid_call(
+        body,
+        (heads,),
+        [
+            col(0),
+            col(heads),
+            col(2 * heads),
+            pl.BlockSpec((shards, 8, rows), lambda h: (0, 0, 0)),
+            row,
+            row,
+            table,
+            table,
+            one,
+            pl.BlockSpec((1, rows), lambda h: (0, 0)),
+        ],
+        [col(0)] * 4 + [pl.BlockSpec((1, rows, 1), lambda h: (h, 0, 0)), one, one],
+        [low] * 4 + [jax.ShapeDtypeStruct((heads, rows, 1), jnp.float32), column, column],
+        4 * heads * rows * rows * HEAD,
+        heads * rows * rows,
+        qkv,
+        qkv,
+        qkv,
+        sums,
+        g_query,
+        g_key,
+        cosine,
+        sine,
+        seg_col,
+        seg_row,
+    )
+
+
+def attend_back(qkv, q_rot, k_rot, value_in, grad, log_total, r_query, r_key, g_query, g_key, cosine, sine, seg_col, seg_row):
+    rows, cols = q_rot.shape
+    heads = cols // HEAD
+    tq = math.gcd(rows, 256)
+    scaling = HEAD ** (-0.5)
+
+    def body(q, k, qr, kr, v, ga, lt, rq, rk, gq, gk, cos, sin, sc, sr, q_out, k_out, v_out, stat_out, gq_out, gk_out, q_sum, k_sum, v_sum, stats):
+        k_sum[...] = jnp.zeros_like(k_sum)
+        v_sum[...] = jnp.zeros_like(v_sum)
+        for i in range(rows // tq):
+            at, keys = (slice(i * tq, (i + 1) * tq), (i + 1) * tq)
+            scores = mm(qr[at, :], kr[:keys, :], ((1,), (1,))) * scaling
+            allowed = seen(i * tq, tq, keys, sc[at, :], sr[:, :keys])
+            p = jnp.exp(jnp.where(allowed, scores, masked_score) - lt[0, at, :])
+            grad_weights = mm(ga[at, :], v[:keys, :], ((1,), (1,)))
+            delta = jnp.sum(p * grad_weights, axis=-1, keepdims=True)
+            grad_scores = (scaling * p * (grad_weights - delta)).astype(jnp.bfloat16)
+            q_sum[at, :] = mm(grad_scores, kr[:keys, :], ((1,), (0,)))
+            k_sum[:keys, :] += mm(grad_scores, qr[at, :], ((0,), (0,)))
+            v_sum[:keys, :] += mm(p.astype(jnp.bfloat16), ga[at, :], ((0,), (0,)))
+
+        first = pl.program_id(0) == 0
+
+        def back(total, ref, r, g, out, place, gain):
+            values = total[...]
+            values = values * cos[...] - pltpu.roll(values, HEAD // 2, 1) * sin[...]
+            gain[...] = jnp.sum(values * ref[...] * r[...], axis=0, keepdims=True)
+            values = values * g[...]
+            stat = jnp.sum(values * ref[...], axis=-1, keepdims=True)
+            stats[place] += stat
+            out[...] = values
+
+        @pl.when(first)
+        def _():
+            stats[...] = jnp.zeros_like(stats)
+
+        back(q_sum, q, rq, gq, q_out, 0, gq_out)
+        back(k_sum, k, rk, gk, k_out, 1, gk_out)
+
+        @pl.when(pl.program_id(0) == heads - 1)
+        def _():
+            for i in range(rows // tq):
+                at = slice(i * tq, (i + 1) * tq)
+                stat_out[:, at] = pair_rows(stats[0, at, :], stats[1, at, :])
+
+        v_out[...] = v_sum[...].astype(jnp.bfloat16)
+
+    def col(offset):
+        return pl.BlockSpec((rows, HEAD), lambda h: (0, offset + h))
+
+    row = pl.BlockSpec((1, HEAD), lambda h: (0, h))
+    one = pl.BlockSpec((rows, 1), lambda h: (0, 0))
+    stat = pl.BlockSpec((1, rows, 1), lambda h: (h, 0, 0))
+    table = pl.BlockSpec((rows, HEAD), lambda h: (0, 0))
+    full = jnp.float32
+    outs = (
+        [jax.ShapeDtypeStruct((rows, cols), full)] * 2
+        + [jax.ShapeDtypeStruct((rows, cols), jnp.bfloat16)]
+        + [jax.ShapeDtypeStruct((8, rows), full)]
+        + [jax.ShapeDtypeStruct((1, cols), full)] * 2
+    )
+    args = (qkv, qkv, q_rot, k_rot, value_in, grad, log_total, r_query, r_key, g_query, g_key, cosine, sine, seg_col, seg_row)
+    return pl.pallas_call(
+        body,
+        grid=(heads,),
+        in_specs=[col(0), col(heads), col(0), col(0), col(0), col(0), stat, one, one, row, row, table, table, one,
+                  pl.BlockSpec((1, rows), lambda h: (0, 0))],
+        out_specs=[col(0), col(0), col(0), pl.BlockSpec((8, rows), lambda h: (0, 0)), row, row],
+        out_shape=outs,
+        scratch_shapes=[pltpu.VMEM((rows, HEAD), full)] * 3 + [pltpu.VMEM((2, rows, 1), full)],
+        compiler_params=pltpu.CompilerParams(vmem_limit_bytes=VMEM_GRANT),
+        cost_estimate=cost(10 * heads * rows * rows * HEAD, heads * rows * rows, *args, *outs),
+    )(*args)
+
+
+def normed_gradient(q_grad, k_grad, v_low, qkv, sums, r_query, r_key, w_qkv, x_row, r_attn):
+    rows, cols = q_grad.shape
+    width = x_row.shape[1]
+    shards = sums.shape[0]
+    tm = math.gcd(rows, 256)
+
+    def body(qg, kg, v, q, k, sums_ref, rq, rk, w, x, ra, low_ref, out_ref, gain_ref):
+        means = pair_columns([sums_ref[d] for d in range(shards)])
+        parts = []
+        for grad, ref, r_ref, mean in ((qg, q, rq, means[0]), (kg, k, rk, means[1])):
+            r = r_ref[...]
+            part = r * grad[...] - ref[...] * (r * r * r) * (mean / width)
+            parts.append(part.astype(jnp.bfloat16))
+        parts.append(v[...])
+        for i in range(3):
+            low_ref[:, i * cols : (i + 1) * cols] = parts[i]
+        total = mm(low_ref[...], w[...], ((1,), (1,)))
+        out_ref[...] = total.astype(jnp.bfloat16)
+        gain = jnp.sum(total * x[...].astype(jnp.float32) * ra[...], axis=0, keepdims=True)
+        first = pl.program_id(0) == 0
+
+        @pl.when(first)
+        def _():
+            gain_ref[...] = gain
+
+        @pl.when(jnp.logical_not(first))
+        def _():
+            gain_ref[...] += gain
+
+    def tiled(count, at=0):
+        return pl.BlockSpec((tm, count), lambda i: (i, at))
+
+    return grid_call(
+        body,
+        (rows // tm,),
+        [
+            tiled(cols),
+            tiled(cols),
+            tiled(cols),
+            tiled(cols),
+            tiled(cols, 1),
+            pl.BlockSpec((shards, 8, tm), lambda i: (0, 0, i)),
+            tiled(1),
+            tiled(1),
+            pl.BlockSpec((width, 3 * cols), lambda i: (0, 0)),
+            tiled(width),
+            tiled(1),
+        ],
+        [tiled(3 * cols), tiled(width), pl.BlockSpec((1, width), lambda i: (0, 0))],
+        [
+            jax.ShapeDtypeStruct((rows, 3 * cols), jnp.bfloat16),
+            jax.ShapeDtypeStruct((rows, width), jnp.bfloat16),
+            jax.ShapeDtypeStruct((1, width), jnp.float32),
+        ],
+        6 * rows * width * cols,
+        0,
+        q_grad,
+        k_grad,
+        v_low,
+        qkv,
+        qkv,
+        sums,
+        r_query,
+        r_key,
+        w_qkv,
+        x_row,
+        r_attn,
+    )
+
+
+def middle(order, nf_own, mid, r_ffn, gain, dy, out_pieces):
+    tokens, width = nf_own.shape
+    chunk = width // 4
+
+    def body(order_ref, nf, mid_ref, r_ref, gain_ref, dy_ref, p0, p1, p2, p3, grad_ref, low_ref, att_ref, gain_out):
+        r = r_ref[...]
+        own = mid_ref[...]
+        grad = nf[...].astype(jnp.float32)
+        gain_out[...] = jnp.sum(grad * own * r, axis=0, keepdims=True)
+        grad = grad * gain_ref[...]
+        mean = jnp.mean(grad * own, axis=-1, keepdims=True)
+        total = dy_ref[...].astype(jnp.float32) + r * grad - own * (r * r * r) * mean
+        grad_ref[...] = total
+        low_ref[...] = total.astype(jnp.bfloat16)
+        for j, piece in enumerate((p0, p1, p2, p3)):
+            back = jnp.zeros((tokens, chunk), jnp.float32)
+            for k in range(4):
+                n = k ^ j
+                back = back + mm(
+                    low_ref[:, n * chunk : (n + 1) * chunk],
+                    piece[:, k * chunk : (k + 1) * chunk],
+                    ((1,), (1,)),
+                )
+            att_ref[order_ref[j]] = back.astype(jnp.bfloat16)
+
+    def whole(*shape):
+        return pl.BlockSpec(shape, lambda i, o: (0,) * len(shape))
+
+    outs = [
+        jax.ShapeDtypeStruct((tokens, width), jnp.float32),
+        jax.ShapeDtypeStruct((tokens, width), jnp.bfloat16),
+        jax.ShapeDtypeStruct((4, tokens, chunk), jnp.bfloat16),
+        jax.ShapeDtypeStruct((1, width), jnp.float32),
+    ]
+    return pl.pallas_call(
+        body,
+        grid_spec=pltpu.PrefetchScalarGridSpec(
+            num_scalar_prefetch=1,
+            grid=(1,),
+            in_specs=[
+                whole(tokens, width),
+                pl.BlockSpec((tokens, width), lambda i, o: (o[4], 0)),
+                pl.BlockSpec((tokens, 1), lambda i, o: (o[4], 0)),
+                whole(1, width),
+                whole(tokens, width),
+                *[whole(chunk, width)] * 4,
+            ],
+            out_specs=[whole(*o.shape) for o in outs],
+        ),
+        out_shape=outs,
+        compiler_params=pltpu.CompilerParams(vmem_limit_bytes=VMEM_GRANT),
+        cost_estimate=cost(2 * tokens * width * width, 0, *out_pieces, *outs),
+    )(order, nf_own, mid, r_ffn, gain, dy, *out_pieces)
+
+
+def out_grad_pieces(order, attended, columns):
+    shards, rows, cols = attended.shape
+    per_chunk = shards // 4
+    count = columns.shape[1]
+    tm = math.gcd(cols, 256)
+
+    def body(order_ref, att_ref, col_ref, *outs):
+        step = pl.program_id(0)
+        for j in range(4):
+
+            @pl.when(step == j)
+            def _(j=j):
+                outs[j][...] = mm(att_ref[0], col_ref[...], ((0,), (0,))).astype(jnp.bfloat16)
+
+    def place(j):
+        return lambda k, i, o: (jnp.where(k < j, 0, jnp.where(k > j, per_chunk - 1, i)), 0)
+
+    outs = [jax.ShapeDtypeStruct((per_chunk * cols, count), jnp.bfloat16)] * 4
+    return pl.pallas_call(
+        body,
+        grid_spec=pltpu.PrefetchScalarGridSpec(
+            num_scalar_prefetch=1,
+            grid=(4, per_chunk),
+            in_specs=[
+                pl.BlockSpec((1, rows, cols), lambda k, i, o: (o[k] * per_chunk + i, 0, 0)),
+                pl.BlockSpec((rows, count), lambda k, i, o: (0, 0)),
+            ],
+            out_specs=[pl.BlockSpec((cols, count), place(j)) for j in range(4)],
+        ),
+        out_shape=outs,
+        compiler_params=pltpu.CompilerParams(vmem_limit_bytes=VMEM_GRANT),
+        cost_estimate=cost(2 * rows * shards * cols * count, 0, attended, columns, *outs),
+    )(order, attended, columns)
 
 
 def swap(values, bits):
@@ -865,6 +1242,16 @@
     wide = jnp.float32
     kept = pieces[0].astype(wide) + swap(pieces[1], 1).astype(wide)
     return (kept.astype(sent), (pieces[2].astype(wide) + swap(pieces[3], 1).astype(wide)).astype(sent))
+
+
+def across_by_expert(passed):
+    return [swap(passed[e], 2) for e in range(passed.shape[0])]
+
+
+def add_arrived(kept, arrived):
+    return jnp.stack(
+        [kept[e].astype(jnp.float32) + a.astype(jnp.float32) for e, a in enumerate(arrived)]
+    )
 
 
 def sum_pieces(pieces, sent):
@@ -881,11 +1268,6 @@
         ],
         axis=axis,
     )
-
-
-def sum_over_seq(values, shards):
-    spread = jnp.broadcast_to(values[None], (shards,) + values.shape)
-    return jnp.sum(lax.all_to_all(spread, "seq", 0, 0, tiled=True), axis=0)
 
 
 def on_device_heads(
@@ -924,6 +1306,9 @@
     def own_cols(values, count):
         return lax.dynamic_slice_in_dim(values, seq_index * count, count, axis=values.ndim - 1)
 
+    cosine, sine = rope_tables(rows, HEAD)
+    seg_col, seg_row = (row_seg[:, None], row_seg[None, :])
+
     x_shard = reorder(hidden_in[0], dp_index, 1)
     x_row = lax.all_gather(x_shard, "seq", axis=0, tiled=True)
     blocks = jnp.stack(
@@ -944,7 +1329,8 @@
     across = swap(blocks, 2)
     qkv_pieces = (blocks, swap(blocks, 1), across, swap(across, 1))
     gate_across = swap(w_gate, 2)
-    x_row, qkv_pieces, gate_across = barrier((x_row, qkv_pieces, gate_across))
+    gate_full = jnp.concatenate([w_gate, swap(w_gate, 1), gate_across, swap(gate_across, 1)], axis=1)
+    x_row, qkv_pieces, gate_full = barrier((x_row, qkv_pieces, gate_full))
 
     w_qkv = jnp.concatenate(
         [
@@ -959,7 +1345,7 @@
     gain_pair = sum(
         jnp.sum(p[:, 3 * block_rows : 3 * block_rows + 2].astype(full), axis=0) for p in qkv_pieces
     )
-    g_query, g_key = (gain_pair[0], gain_pair[1])
+    g_query, g_key = (gain_pair[0:1], gain_pair[1:2])
     g_attn = jnp.concatenate(
         [p[:, 3 * block_rows + 2, :block_rows].reshape(1, chunk) for p in qkv_pieces], axis=1
     ).astype(full)
@@ -976,37 +1362,14 @@
     )
     up_across = swap(w_up, 2)
 
-    x_wide = x_row.astype(full)
-    r_attn = lax.rsqrt(jnp.mean(x_wide * x_wide, axis=-1, keepdims=True) + epsilon)
-    normed = (x_wide * r_attn * g_attn).astype(low)
-    qkv = mm(normed, w_qkv, ((1,), (0,)))
-    query, key_proj = (qkv[:, :cols], qkv[:, cols : 2 * cols])
-    value_in = qkv[:, 2 * cols :].astype(low)
-    sums = sum_over_seq(
-        jnp.stack([jnp.sum(query * query, axis=-1), jnp.sum(key_proj * key_proj, axis=-1)]), shards
-    )
-    r_query, r_key = (lax.rsqrt(sums[i] / width + epsilon)[:, None] for i in range(2))
-    cosine, sine = rope_tables(rows, HEAD)
-    q_normed, k_normed = (query * r_query * g_query, key_proj * r_key * g_key)
-    position = lax.iota(jnp.int32, rows)
-    allowed = (position[:, None] >= position[None, :]) & (row_seg[:, None] == row_seg[None, :])
-    scaling = HEAD ** (-0.5)
-
-    def head(values, h):
-        return values[:, h * HEAD : (h + 1) * HEAD]
-
-    q_rot, k_rot, log_total, attended = ([], [], [], [])
-    for h in range(heads):
-        q_rot.append(rotate(head(q_normed, h), cosine, sine).astype(low))
-        k_rot.append(rotate(head(k_normed, h), cosine, sine).astype(low))
-        scores = jnp.where(
-            allowed, mm(q_rot[h], k_rot[h], ((1,), (1,))) * scaling, masked_score
-        )
-        peak = jnp.max(scores, axis=-1, keepdims=True)
-        log_total.append(peak + jnp.log(jnp.sum(jnp.exp(scores - peak), axis=-1, keepdims=True)))
-        weights = jnp.exp(scores - log_total[h]).astype(low)
-        attended.append(mm(weights, head(value_in, h), ((1,), (0,))).astype(low))
-    attended = jnp.concatenate(attended, axis=1)
+    def share(sums):
+        spread = jnp.broadcast_to(sums[None], (shards,) + sums.shape)
+        return lax.all_to_all(spread, "seq", 0, 0, tiled=True)
+
+    normed, qkv, r_attn, sums = project(x_row, g_attn, w_qkv)
+    q_rot, k_rot, value_in, attended, log_total, r_query, r_key = attend(
+        qkv, share(sums), width, g_query, g_key, cosine, sine, seg_col, seg_row
+    )
     attended, out_own, up_across = barrier((attended, out_own, up_across))
 
     attended_row = lax.all_gather(attended, "seq", axis=0)
@@ -1022,21 +1385,20 @@
     own = (
         lane_ids[None, :] == seq_index * held + lax.iota(jnp.int32, held)[:, None]
     ).astype(full)
-    gate_full = jnp.concatenate([w_gate, swap(w_gate, 1), gate_across, swap(gate_across, 1)], axis=1)
     up_full = jnp.concatenate([w_up, swap(w_up, 1), up_across, swap(up_across, 1)], axis=1)
-    attended_row, out_pieces, gate_full, up_full, router, g_ffn, chosen = barrier(
-        (attended_row, out_pieces, gate_full, up_full, router, g_ffn, chosen)
+    attended_row, out_pieces, up_full, router, g_ffn, chosen = barrier(
+        (attended_row, out_pieces, up_full, router, g_ffn, chosen)
     )
 
     dy_shard, attended_row = barrier((reorder(cotangent[0], dp_index, 1), attended_row))
     dy_row = lax.all_gather(dy_shard, "seq", axis=0, tiled=True)
-    down_across = swap(w_down, 2)
-    down_full = jnp.concatenate([w_down, swap(w_down, 1), down_across, swap(down_across, 1)], axis=2)
-    order = jnp.stack([dp_index ^ k for k in range(4)]).astype(jnp.int32)
+    order = jnp.stack([dp_index ^ k for k in range(4)] + [seq_index]).astype(jnp.int32)
     hidden_mid, normed_ffn, r_ffn, chances, gates = finish_attention(
         order, attended_row, out_pieces, x_row, g_ffn, router, chosen, own, expert_count
     )
     act, dgate_factor, dup_factor = expert_activations(normed_ffn, gate_full, up_full)
+    act, down_across = barrier((act, swap(w_down, 2)))
+    down_full = jnp.concatenate([w_down, swap(w_down, 1), down_across, swap(down_across, 1)], axis=2)
     mixture = combine_experts(act, down_full, gates)
     dy_row, mixture, act = barrier((dy_row, mixture, act))
 
@@ -1049,91 +1411,70 @@
     nf_sum = lax.psum_scatter(nf_grad, "seq", scatter_dimension=0, tiled=True)
 
     down_kept, down_passed = sum_in_chip(weight_pieces(scaled, dy_row, 4, False), low)
-    gate_kept, gate_passed = sum_in_chip(weight_pieces(normed_ffn, dgate, 4, True), low)
-    up_kept, up_passed = sum_in_chip(weight_pieces(normed_ffn, dup, 4, True), low)
-    down_arrived = swap(down_passed, 2)
+    gate_pieces = weight_pieces(normed_ffn, dgate, 4, True)
+    dup, down_passed = barrier((dup, down_passed))
+    down_arrived = across_by_expert(down_passed)
+    gate_kept, gate_passed = sum_in_chip(gate_pieces, low)
+    up_pieces = weight_pieces(normed_ffn, dup, 4, True)
+    nf_sum, mixture, up_pieces, down_arrived[0], gate_passed = barrier(
+        (nf_sum, mixture, up_pieces, down_arrived[0], gate_passed)
+    )
+    mixture_own = lax.psum_scatter(mixture, "seq", scatter_dimension=0, tiled=True)
+    up_kept, up_passed = sum_in_chip(up_pieces, low)
     router_grad = mm(grad_logits[:, :expert_count], normed_ffn, ((0,), (0,)))
-    nf_sum, mixture, down_arrived, gate_passed, up_passed, router_grad = barrier(
-        (nf_sum, mixture, down_arrived, gate_passed, up_passed, router_grad)
-    )
-    mixture_own = lax.psum_scatter(mixture, "seq", scatter_dimension=0, tiled=True)
-    gate_arrived, up_arrived = (swap(gate_passed, 2), swap(up_passed, 2))
-    grad_w_down = down_kept.astype(full) + down_arrived.astype(full)
-
+    nf_sum, down_arrived[1], up_passed, router_grad = barrier(
+        (nf_sum, down_arrived[1], up_passed, router_grad)
+    )
+    gate_arrived, up_arrived = (across_by_expert(gate_passed), across_by_expert(up_passed))
+
+    grad_mid, mid_low, grad_attended, gain_ffn_grad = middle(
+        order, nf_sum, hidden_mid, r_ffn, g_ffn, dy_shard, out_pieces
+    )
+    grad_attended, gate_arrived[0] = barrier((grad_attended, gate_arrived[0]))
+
+    def to_columns(values):
+        return lax.all_to_all(values, "seq", 0, 0, tiled=True).reshape(rows, cols)
+
+    grad_attended = grad_attended.reshape(4, tokens, shards // 4, cols).transpose(0, 2, 1, 3)
+    grad_attended = to_columns(grad_attended.reshape(shards, tokens, cols))
+    grad_attended, gate_arrived[1] = barrier((grad_attended, gate_arrived[1]))
+    mid_cols = to_columns(
+        reorder(mid_low, dp_index, 1).reshape(tokens, shards, cols).transpose(1, 0, 2)
+    )
+    q_grad, k_grad, v_low, sums, gain_query_grad, gain_key_grad = attend_back(
+        qkv, q_rot, k_rot, value_in, grad_attended, log_total,
+        r_query, r_key, g_query, g_key, cosine, sine, seg_col, seg_row,
+    )
+    sums, up_arrived[0] = barrier((sums, up_arrived[0]))
+    sums, mid_cols = barrier((share(sums), mid_cols))
+    qkv_low, normed_grad, gain_attn_grad = normed_gradient(
+        q_grad, k_grad, v_low, qkv, sums, r_query, r_key, w_qkv, x_row, r_attn
+    )
+    normed_grad, up_arrived[1], mixture_own = barrier((normed_grad, up_arrived[1], mixture_own))
+    normed_sum = lax.psum_scatter(normed_grad, "seq", scatter_dimension=0, tiled=True).astype(full)
+
+    def to_owners(kept, passed, count):
+        total = kept.astype(full) + swap(passed, 2).astype(full)
+        total = lax.all_to_all(
+            total.astype(low).reshape(shards, block_rows, count * cols), "seq", 0, 0, tiled=True
+        )
+        total = total.reshape(shards, block_rows, count, cols).transpose(2, 1, 0, 3)
+        return total.reshape(count, block_rows, width).astype(full)
+
+    out_kept, out_passed = sum_in_chip(out_grad_pieces(order, attended_row, mid_cols), low)
+    out_grad = to_owners(out_kept, out_passed, 1)
+    qkv_kept, qkv_passed = sum_in_chip(
+        [p[0] for p in weight_pieces(normed, qkv_low[None], 4, True)], low
+    )
+    proj_grad = to_owners(qkv_kept, qkv_passed, 3)
+    grad_w_down = add_arrived(down_kept, down_arrived)
+    grad_w_gate = add_arrived(gate_kept, gate_arrived)
+    grad_w_up = add_arrived(up_kept, up_arrived)
     mid_own = lax.dynamic_slice_in_dim(hidden_mid, first_row, tokens)
-    nf_own = nf_sum.astype(full)
-    r_own = lax.dynamic_slice_in_dim(r_ffn, first_row, tokens)
-    gain_ffn_grad = jnp.sum(nf_own * mid_own * r_own, axis=0)
-    scaled_grad = nf_own * g_ffn
-    grad_mid = (
-        dy_shard.astype(full)
-        + r_own * scaled_grad
-        - mid_own * (r_own**3) * jnp.mean(scaled_grad * mid_own, axis=-1, keepdims=True)
-    )
-    mid_low = grad_mid.astype(low)
-
-    def to_columns(values):
-        return lax.all_to_all(
-            values.reshape(tokens, shards, cols).transpose(1, 0, 2), "seq", 0, 0, tiled=True
-        ).reshape(rows, cols)
-
-    def out_transposed(j):
-        mixed = jnp.concatenate(
-            [mid_low[:, (k ^ j) * chunk : ((k ^ j) + 1) * chunk] for k in range(4)], axis=1
-        )
-        return mm(mixed, out_pieces[j][:, :width], ((1,), (1,))).astype(low)
-
-    grad_attended = jnp.concatenate([out_transposed(j) for j in range(4)], axis=1)
-    grad_attended = to_columns(reorder(grad_attended, dp_index, 1))
-    mid_cols = to_columns(reorder(mid_low, dp_index, 1))
-    out_grad = jnp.einsum(
-        "src,rn->scn", attended_row, mid_cols, preferred_element_type=full
-    ).reshape(width, cols)
-    out_grad = reorder(out_grad.astype(low), dp_index, 0)
-
-    q_grads, k_grads, v_grads = ([], [], [])
-    for h in range(heads):
-        scores = jnp.where(
-            allowed, mm(q_rot[h], k_rot[h], ((1,), (1,))) * scaling, masked_score
-        )
-        p = jnp.exp(scores - log_total[h])
-        grad_h = head(grad_attended, h)
-        grad_weights = mm(grad_h, head(value_in, h), ((1,), (1,)))
-        delta = jnp.sum(p * grad_weights, axis=-1, keepdims=True)
-        grad_scores = (scaling * p * (grad_weights - delta)).astype(low)
-        q_grads.append(rotate(mm(grad_scores, k_rot[h], ((1,), (0,))), cosine, -sine))
-        k_grads.append(rotate(mm(grad_scores, q_rot[h], ((0,), (0,))), cosine, -sine))
-        v_grads.append(mm(p.astype(low), grad_h, ((0,), (0,))))
-    q_grad, k_grad = (jnp.concatenate(q_grads, axis=1), jnp.concatenate(k_grads, axis=1))
-    gain_query_grad = jnp.sum(q_grad * query * r_query, axis=0)
-    gain_key_grad = jnp.sum(k_grad * key_proj * r_key, axis=0)
-    q_grad, k_grad = (q_grad * g_query, k_grad * g_key)
-    means = sum_over_seq(
-        jnp.stack([jnp.sum(q_grad * query, axis=-1), jnp.sum(k_grad * key_proj, axis=-1)]), shards
-    )
-    means = means / width
-    q_low = (r_query * q_grad - query * (r_query**3) * means[0][:, None]).astype(low)
-    k_low = (r_key * k_grad - key_proj * (r_key**3) * means[1][:, None]).astype(low)
-    v_low = jnp.concatenate(v_grads, axis=1).astype(low)
-    qkv_low = jnp.concatenate([q_low, k_low, v_low], axis=1)
-    normed_grad = mm(qkv_low, w_qkv, ((1,), (1,)))
-    gain_attn_grad = jnp.sum(normed_grad * x_row.astype(full) * r_attn, axis=0)
-    normed_grad, mixture_own, gate_arrived, up_arrived = barrier(
-        (normed_grad.astype(low), mixture_own, gate_arrived, up_arrived)
-    )
-    grad_w_gate = gate_kept.astype(full) + gate_arrived.astype(full)
-    grad_w_up = up_kept.astype(full) + up_arrived.astype(full)
-    normed_sum = lax.psum_scatter(normed_grad, "seq", scatter_dimension=0, tiled=True).astype(full)
-
-    proj_grad = jnp.concatenate(
-        [mm(normed, qkv_low, ((0,), (0,))).astype(low), out_grad], axis=1
-    )
-    proj_grad = sum_pieces([proj_grad[k * chunk : (k + 1) * chunk] for k in range(4)], low)
-    proj_grad = lax.all_to_all(
-        proj_grad.astype(low).reshape(shards, block_rows, 4 * cols), "seq", 0, 0, tiled=True
-    )
-    proj_grad = proj_grad.reshape(shards, block_rows, 4, cols).transpose(2, 1, 0, 3)
-    proj_grad = proj_grad.reshape(4, block_rows, width).astype(full)
+    block_out = (mid_own + mixture_own.astype(full)).astype(low)
+    normed_sum, grad_w_down, grad_w_gate, grad_w_up, out_grad, block_out = barrier(
+        (normed_sum, grad_w_down, grad_w_gate, grad_w_up, out_grad, block_out)
+    )
 
     x_own = x_shard.astype(full)
     r_here = lax.rsqrt(jnp.mean(x_own * x_own, axis=-1, keepdims=True) + epsilon)
@@ -1143,7 +1484,6 @@
         + r_here * scaled_grad
         - x_own * (r_here**3) * jnp.mean(scaled_grad * x_own, axis=-1, keepdims=True)
     )
-    block_out = (mid_own + mixture_own.astype(full)).astype(low)
 
     def place(values):
         whole = lax.dynamic_update_slice_in_dim(
@@ -1154,10 +1494,10 @@
     vectors = jnp.concatenate(
         [
             router_grad,
-            gain_attn_grad[None],
-            place(gain_query_grad),
-            place(gain_key_grad),
-            gain_ffn_grad[None],
+            gain_attn_grad,
+            place(gain_query_grad[0]),
+            place(gain_key_grad[0]),
+            gain_ffn_grad,
         ]
     )
     count = vectors.shape[0]
@@ -1170,7 +1510,7 @@
         proj_grad[0],
         proj_grad[1],
         proj_grad[2],
-        proj_grad[3],
+        out_grad[0],
         vectors[expert_count],
         vectors[expert_count + 1],
         vectors[expert_count + 2],

time: 755 us -> 701 us (0.928)
  Pallas kernels: 159 us -> 228 us
  matrix products: 52.1 us -> 2.43 us
  waiting for transfers between devices: 295 us -> 246 us
  other arithmetic: 104 us -> 77.1 us
  blocking collectives: 0 us -> 14.3 us
  local copies, waits for them, and re-layouts: 66.2 us -> 54.4 us
    dot_general x20 -> x1, matrix products: 48 us -> 2.43 us  [mm(): lax.dot_general(left, right, (dims, ((), ())), preferred_element_type=jnp...]
    pallas_call x7 -> x11, Pallas kernels: 140 us -> 179 us  [grid_call(): pl.pallas_call(body, grid=grid, in_specs=in_specs, out_specs=out_specs, o...]
    all_to_all x1, waiting for transfers between devices: 36.9 us -> 0.01 us  [on_device_heads(): lax.all_to_all(jnp.concatenate([blocks, gain_rows], axis=1), 'seq', 0, 0,...]
    pallas_call x0 -> x3, Pallas kernels: none -> 30 us  [the longest x1 12.5 us: attend_back(): pl.pallas_call(body, grid=(heads,), in_specs=[col(0), col(heads), col(0),...]
    reduce_scatter x1, waiting for transfers between devices: 0.01 us -> 21.7 us  [on_device_heads(): nf_sum = lax.psum_scatter(nf_grad, 'seq', scatter_dimension=0, tiled=True)]
    add x5 -> x0, other arithmetic: 17.4 us -> none  [the longest x1 5.84 us: on_device_heads(): grad_w_down = down_kept.astype(full) + down_arrived.astype(full)]
    another operation x4 -> x6, other arithmetic: 1.98 us -> 17.9 us  [add_arrived(): jnp.stack([kept[e].astype(jnp.float32) + a.astype(jnp.float32) for e, a i...]
    ppermute x30 -> x36, waiting for transfers between devices: 174 us -> 158 us  [swap(): return lax.ppermute(values, 'dp', [(i, i ^ bits) for i in range(4)])]
  transfers between devices with their start and end apart: 44 -> 50, of which waited for: 17 -> 20; matrix products, arithmetic and copies ran while one was open for 27% -> 17% of each run, Pallas kernels for 15% -> 26%
where the time goes in v3:
time: 701 us; the launch traced here: 691 us
  waiting for transfers between devices  246 us (35%)
  Pallas kernels  228 us (33%)
  other arithmetic  77.1 us (11%)
  local copies, waits for them, and re-layouts  54.4 us (8%)
  starting transfers between devices  53 us (8%)
  between operations  15.7 us (2%)
  blocking collectives  14.3 us (2%)
    pallas_call x11, Pallas kernels, grid_call(): pl.pallas_call(body, grid=grid, in_specs=in_specs, out_specs=out_specs, o...  179 us
    ppermute x36, waiting for transfers between devices, swap(): return lax.ppermute(values, 'dp', [(i, i ^ bits) for i in range(4)])  158 us
    ppermute x36, starting transfers between devices, swap(): return lax.ppermute(values, 'dp', [(i, i ^ bits) for i in range(4)])  23.4 us
    reduce_scatter x1, waiting for transfers between devices, on_device_heads(): nf_sum = lax.psum_scatter(nf_grad, 'seq', scatter_dimension=0, tiled=True)  21.7 us
    all_to_all x2, waiting for transfers between devices, to_owners(): lax.all_to_all(total.astype(low).reshape(shards, block_rows, count * cols...  21.2 us
    unnamed x130, local copies, waits for them, and re-layouts  20.4 us
    pallas_call x1, Pallas kernels, finish_attention(): pl.pallas_call(body, grid_spec=pltpu.PrefetchScalarGridSpec(num_scalar_pr...  19 us
    another operation x6, other arithmetic, add_arrived(): jnp.stack([kept[e].astype(jnp.float32) + a.astype(jnp.float32) for e, a i...  17.9 us
  transfers between devices with their start and end apart: 50, of which 20 were waited for; matrix products, arithmetic and copies ran while one was open for 17% of the time, Pallas kernels for 26%

profile of v3, /device:TPU:0, one launch (start us, length us, event | category | flops | bytes accessed | tf_op | source)
XLA Modules:
  0.0 690.7 jit_solution(11420156013437761342)
XLA Ops:
  22.3 37.7 %collective-permute-done.4 = bf16[2,512,1024]{2,1,0:T(8,128)(2,1)} collective-permute-done((bf16[2,512,1024]{2,1,0:T(8,128)(2,1)S(1)}, bf16[2,512,1024]{2,1,0:T(8,128)(2,1)}, u32[]{:S(2)}, u32[]{:S(2)}) %collective-permute-start.4) | collective-permute-done | bytes 2097184 | tf_op jit(solution)/shard_map/ppermute | solution.py:1238
  68.8 16.0 %collective-permute-done.1 = bf16[8,208,256]{2,1,0:T(8,128)(2,1)} collective-permute-done((bf16[8,208,256]{2,1,0:T(8,128)(2,1)S(1)}, bf16[8,208,256]{2,1,0:T(8,128)(2,1)}, u32[]{:S(2)}, u32[]{:S(2)}) %collective-permute-start.1) | collective-permute-done | bytes 852000 | tf_op jit(solution)/shard_map/ppermute | solution.py:1238
  93.6 9.6 %all-gather.6.cloned.1.call-done.x_ref.x = bf16[1024,2048]{1,0:T(8,128)(2,1)} async-done(((bf16[128,2048]{1,0:T(8,128)(2,1)}), bf16[1024,2048]{1,0:T(8,128)(2,1)}) %all-gather.6.cloned.1.call-update) | async-done | bytes 4194320 | tf_op jit(solution)/shard_map/all_gather | solution.py:1313
  115.8 9.3 %shard_map.263 = (bf16[1024,2048]{1,0:T(8,128)(2,1)}, f32[1024,768]{1,0:T(8,128)}, f32[1024,1]{1,0:T(8,128)}, f32[8,1024]{1,0:T(8,128)}) custom-call(bf16[1024,2048]{1,0:T(8,128)(2,1)} %all-gather.6.cloned.1.call-done.x_ref.x, f32[1,2048]{1,0:T(1,128)} %maximum_convert_fusion.gain_ref, bf16[2048,768]{1,0:T(8,128)(2,1)} %copy-done.1), custom_call_target="tpu_custom_call" | custom-call | flops 805306368 | bytes 3681280 | tf_op jit(solution)/shard_map/pallas_call | solution.py:518
  133.3 11.9 %all-to-all-done.1.sums_ref = f32[8,8,1024]{2,1,0:T(8,128)S(1)} async-done(((f32[8,8,1024]{2,1,0:T(8,128)}), f32[8,8,1024]{2,1,0:T(8,128)S(1)}, u32[]{:S(2)}, u32[]{:S(2)}) %all-to-all-start.1) | async-done | bytes 262176 | tf_op jit(solution)/shard_map/all_to_all | solution.py:1367
  145.8 11.0 %shard_map.264 = (bf16[1024,256]{1,0:T(8,128)(2,1)}, bf16[1024,256]{1,0:T(8,128)(2,1)}, bf16[1024,256]{1,0:T(8,128)(2,1)}, bf16[1024,256]{1,0:T(8,128)(2,1)}, f3...) custom-call(f32[1024,768]{1,0:T(8,128)} %get-tuple-element.133.q.k.v, ...), custom_call_target="tpu_custom_call" | custom-call | flops 268435456 | bytes 3217920 | tf_op jit(solution)/shard_map/pallas_call | solution.py:518
  159.3 47.6 %collective-permute-done.8.p2 = bf16[512,2176]{1,0:T(8,128)(2,1)S(1)} collective-permute-done((bf16[512,2176]{1,0:T(8,128)(2,1)}, bf16[512,2176]{1,0:T(8,128)(2,1)S(1)}, u32[]{:S(2)}, u32[]{:S(2)}) %collective-permute-start.8) | collective-permute-done | bytes 2228256 | tf_op jit(solution)/shard_map/ppermute | solution.py:1238
  235.0 19.0 %shard_map.265 = (f32[1024,2048]{1,0:T(8,128)}, bf16[1024,2048]{1,0:T(8,128)(2,1)}, f32[1024,1]{1,0:T(8,128)}, f32[1024,128]{1,0:T(8,128)}, f32[2,1024,1]{2,1,0:T(8,128)}) custom-call(s32[5]{0:T(128)} %stack.78.order_ref, bf16[8,1024,256]{2,1,0:T(8,128)(2,1)} %bitcast.189, bf16[512,2176]{1,0:T(8,128)(2,1)} %all-gather.8.cloned.1.call-done.p0, ...), custom_call_target="tpu_custom_call" | custom-call | flops 2147483648 | bytes 6556672 | tf_op jit(solution)/shard_map/pallas_call | solution.py:587
  254.0 25.0 %shard_map.266 = (bf16[2,1024,1024]{2,1,0:T(8,128)(2,1)}, bf16[2,1024,1024]{2,1,0:T(8,128)(2,1)}, bf16[2,1024,1024]{2,1,0:T(8,128)(2,1)}) custom-call(bf16[1024,2048]{1,0:T(8,128)(2,1)} %get-tuple-element.152.x_ref.flat_ref, bf16[2,2048,1024]{2,1,0:T(8,128)(2,1)} %pad_maximum_fusion.gate_ref, bf16[2,2048,1024]{2,1,0:T(8,128)(2,1)} %pad_maximum_fusion.1.up_ref), custom_call_target="tpu_custom_call" | custom-call | flops 4294967296 | bytes 8388608 | tf_op jit(solution)/shard_map/pallas_call | solution.py:518
  287.4 14.2 %shard_map.267 = bf16[1024,2048]{1,0:T(8,128)(2,1)} custom-call(bf16[2,1024,1024]{2,1,0:T(8,128)(2,1)} %get-tuple-element.160.act_ref, bf16[2,1024,2048]{2,1,0:T(8,128)(2,1)} %constant_dynamic-update-slice_fusion.5.down_ref, f32[2,1024,1]{2,1,0:T(8,128)} %get-tuple-element.158.weight_ref), custom_call_target="tpu_custom_call" | custom-call | flops 2147483648 | bytes 4196352 | tf_op jit(solution)/shard_map/pallas_call | solution.py:518
  305.8 20.3 %shard_map.268 = (bf16[2,1024,1024]{2,1,0:T(8,128)(2,1)}, bf16[2,1024,1024]{2,1,0:T(8,128)(2,1)}, bf16[2,1024,1024]{2,1,0:T(8,128)(2,1)}, f32[2,1024,128]{2,1,0:T(8,128)}) custom-call(bf16[1024,2048]{1,0:T(8,128)(2,1)} %all-gather.10.cloned.1.call-done.dy_ref.flat_ref, bf16[2,1024,2048]{2,1,0:T(8,128)(2,1)} %constant_dynamic-update-slice_fusion.5.down_ref, ...), custom_call_target="tpu_custom_call" | custom-call | flops 2147483648 | bytes 9701376 | tf_op jit(solution)/shard_map/pallas_call | solution.py:518
  326.1 26.4 %shard_map.269 = (bf16[1024,2048]{1,0:T(8,128)(2,1)}, bf16[1024,128]{1,0:T(8,128)(2,1)}) custom-call(bf16[2,1024,1024]{2,1,0:T(8,128)(2,1)} %get-tuple-element.163.dgate_ref.stacked_ref, bf16[2,1024,1024]{2,1,0:T(8,128)(2,1)} %get-tuple-element.172.dup_ref.stacked_ref, bf16[2,2048,1024]{2,1,0:T(8,128)(2,1)} %pad_maximum_fusion.gate_ref, ...), custom_call_target="tpu_custom_call" | custom-call | flops 4294967296 | bytes 8061184 | tf_op jit(solution)/shard_map/pallas_call | solution.py:518
  353.0 18.9 %shard_map.270 = (bf16[2,1024,512]{2,1,0:T(8,128)(2,1)}, bf16[2,1024,512]{2,1,0:T(8,128)(2,1)}, bf16[2,1024,512]{2,1,0:T(8,128)(2,1)}, bf16[2,1024,512]{2,1,0:T(8,128)(2,1)}) custom-call(bf16[1024,2048]{1,0:T(8,128)(2,1)} %all-gather.10.cloned.1.call-done.dy_ref.flat_ref, bf16[2,1024,1024]{2,1,0:T(8,128)(2,1)} %get-tuple-element.169.stacked_ref), custom_call_target="tpu_custom_call" | custom-call | flops 2147483648 | bytes 4194304 | tf_op jit(solution)/shard_map/pallas_call | solution.py:518
  372.0 17.8 %shard_map.272 = (bf16[2,512,1024]{2,1,0:T(8,128)(2,1)}, bf16[2,512,1024]{2,1,0:T(8,128)(2,1)}, bf16[2,512,1024]{2,1,0:T(8,128)(2,1)}, bf16[2,512,1024]{2,1,0:T(8,128)(2,1)}) custom-call(bf16[1024,2048]{1,0:T(8,128)(2,1)} %get-tuple-element.152.x_ref.flat_ref, bf16[2,1024,1024]{2,1,0:T(8,128)(2,1)} %get-tuple-element.163.dgate_ref.stacked_ref), custom_call_target="tpu_custom_call" | custom-call | flops 2147483648 | bytes 4194304 | tf_op jit(solution)/shard_map/pallas_call | solution.py:518
  393.1 17.7 %shard_map.271 = (bf16[2,512,1024]{2,1,0:T(8,128)(2,1)}, bf16[2,512,1024]{2,1,0:T(8,128)(2,1)}, bf16[2,512,1024]{2,1,0:T(8,128)(2,1)}, bf16[2,512,1024]{2,1,0:T(8,128)(2,1)}) custom-call(bf16[1024,2048]{1,0:T(8,128)(2,1)} %get-tuple-element.152.x_ref.flat_ref, bf16[2,1024,1024]{2,1,0:T(8,128)(2,1)} %get-tuple-element.172.dup_ref.stacked_ref), custom_call_target="tpu_custom_call" | custom-call | flops 2147483648 | bytes 4194304 | tf_op jit(solution)/shard_map/pallas_call | solution.py:518
  417.3 21.7 %reduce-scatter.4.cloned.1.call-done.nf = bf16[128,2048]{1,0:T(8,128)(2,1)} async-done(((bf16[1024,2048]{1,0:T(8,128)(2,1)}), bf16[128,2048]{1,0:T(8,128)(2,1)}) %reduce-scatter.4.cloned.1.call-update) | async-done | bytes 524304 | tf_op jit(solution)/shard_map/reduce_scatter | solution.py:1411
  445.8 19.4 %collective-permute-done.18 = bf16[1024,512]{1,0:T(8,128)(2,1)S(1)} collective-permute-done((bf16[1024,512]{1,0:T(8,128)(2,1)S(1)}, bf16[1024,512]{1,0:T(8,128)(2,1)S(1)}, u32[]{:S(2)}, u32[]{:S(2)}) %collective-permute-start.18) | collective-permute-done | bytes 1048608 | tf_op jit(solution)/shard_map/ppermute | solution.py:1238
  474.3 12.9 %collective-permute-done.20 = bf16[512,1024]{1,0:T(8,128)(2,1)S(1)} collective-permute-done((bf16[512,1024]{1,0:T(8,128)(2,1)S(1)}, bf16[512,1024]{1,0:T(8,128)(2,1)S(1)}, u32[]{:S(2)}, u32[]{:S(2)}) %collective-permute-start.20) | collective-permute-done | bytes 1048608 | tf_op jit(solution)/shard_map/ppermute | solution.py:1238
  498.4 9.8 %all-to-all-done.2 = bf16[8,128,256]{2,1,0:T(8,128)(2,1)S(1)} async-done(((bf16[8,128,256]{2,1,0:T(8,128)(2,1)}), bf16[8,128,256]{2,1,0:T(8,128)(2,1)S(1)}, u32[]{:S(2)}, u32[]{:S(2)}) %all-to-all-start.2) | async-done | bytes 524320 | tf_op jit(solution)/shard_map/all_to_all | solution.py:1436
  520.3 12.5 %shard_map.274 = (f32[1024,256]{1,0:T(8,128)}, f32[1024,256]{1,0:T(8,128)}, bf16[1024,256]{1,0:T(8,128)(2,1)}, f32[8,1024]{1,0:T(8,128)}, f32[1,256]{1,0:T(1,128)}, /*index=5*/f32[1,256]{1,0:T(1,128)}) custom-call(f32[1024,768]{1,0:T(8,128)} %get-tuple-element.133.q.k.v, f32[1024,768]{1,0:T(8,128)} %get-tuple-element.133.q.k.v, ...), custom_call_target="tpu_custom_call" | custom-call | flops 671088640 | bytes 3030016 | tf_op jit(solution)/shard_map/pallas_call | solution.py:1064
  532.8 10.0 %collective-permute-done.22 = bf16[512,1024]{1,0:T(8,128)(2,1)} collective-permute-done((bf16[512,1024]{1,0:T(8,128)(2,1)}, bf16[512,1024]{1,0:T(8,128)(2,1)}, u32[]{:S(2)}, u32[]{:S(2)}) %collective-permute-start.22) | collective-permute-done | bytes 1048608 | tf_op jit(solution)/shard_map/ppermute | solution.py:1238
  543.6 14.3 %all_to_all.40.sums_ref = f32[8,8,1024]{2,1,0:T(8,128)} all-to-all(f32[8,8,1024]{2,1,0:T(8,128)S(1)} %broadcast_in_dim.23), channel_id=1, replica_groups=mesh['dp'=4,'seq'=8] {'seq'}, dimensions={0} | all-to-all | bytes 524288 | tf_op jit(solution)/shard_map/all_to_all | solution.py:1367
  557.8 10.4 %shard_map.275 = (bf16[1024,768]{1,0:T(8,128)(2,1)}, bf16[1024,2048]{1,0:T(8,128)(2,1)}, f32[1,2048]{1,0:T(1,128)}) custom-call(f32[1024,256]{1,0:T(8,128)} %get-tuple-element.194.qg, f32[1024,256]{1,0:T(8,128)} %get-tuple-element.195.kg, bf16[1024,256]{1,0:T(8,128)(2,1)} %get-tuple-element.196.v, f32[1024,768]{1,0:T(8,128)} %get-tuple-element.133.q.k.v, ...), custom_call_target="tpu_custom_call" | custom-call | flops 805306368 | bytes 5575680 | tf_op jit(solution)/shard_map/pallas_call | solution.py:518
  645.9 21.2 %all-to-all-done.6 = bf16[8,64,768]{2,1,0:T(8,128)(2,1)S(1)} async-done(((bf16[8,64,768]{2,1,0:T(8,128)(2,1)}), bf16[8,64,768]{2,1,0:T(8,128)(2,1)S(1)}, u32[]{:S(2)}, u32[]{:S(2)}) %all-to-all-start.6) | async-done | bytes 786464 | tf_op jit(solution)/shard_map/all_to_all | solution.py:1458
  (359 shorter events, 240.5 us)
Async XLA Ops:
  7.2 96.0 %all-gather.6.cloned.1.call-start = ((), (), s32[]{:S(2)}) async-start(), calls=%async_computation.11 | async-start | bytes 4718592 | tf_op jit(solution)/shard_map/all_gather | solution.py:1313
  11.2 48.7 %collective-permute-start.4 = (bf16[2,512,1024]{2,1,0:T(8,128)(2,1)S(1)}, bf16[2,512,1024]{2,1,0:T(8,128)(2,1)}, u32[]{:S(2)}, u32[]{:S(2)}) collective-permute-start(bf16[2,512,1024]{2,1,0:T(8,128)(2,1)S(1)} %copy-done.18), channel_id=1, source_target_pairs={{0,16},{8,24},{16,0},{24,8},{1,17},{9,25},{17,1},{25,9},{2,18},{10... | collective-permute-start | bytes 6291464 | tf_op jit(solution)/shard_map/ppermute | solution.py:1238
  16.1 46.9 %all-to-all-start = ((bf16[8,208,256]{2,1,0:T(8,128)(2,1)}), bf16[8,208,256]{2,1,0:T(8,128)(2,1)S(1)}, u32[]{:S(2)}, u32[]{:S(2)}) async-start(bf16[8,208,256]{2,1,0:T(8,128)(2,1)} %pad_maximum_fusion.5), calls=%async_computation | async-start | bytes 1703936 | tf_op jit(solution)/shard_map/all_to_all | solution.py:1328
  22.1 135.0 %all-gather.8.cloned.1.call-start = ((), (), s32[]{:S(2)}) async-start(), calls=%async_computation.12 | async-start | bytes 2506752 | tf_op jit(solution)/shard_map/all_gather | solution.py:1360
  22.2 63.9 %collective-permute-start.3 = (bf16[2,512,1024]{2,1,0:T(8,128)(2,1)S(1)}, bf16[2,512,1024]{2,1,0:T(8,128)(2,1)}, u32[]{:S(2)}, u32[]{:S(2)}) collective-permute-start(bf16[2,512,1024]{2,1,0:T(8,128)(2,1)S(1)} %copy-done.18), channel_id=1, source_target_pairs={{0,8},{8,0},{16,24},{24,16},{1,9},{9,1},{17,25},{25,17},{2,10},{10... | collective-permute-start | bytes 6291464 | tf_op jit(solution)/shard_map/ppermute | solution.py:1238
  65.4 91.4 %collective-permute-start.6 = (bf16[2,512,1024]{2,1,0:T(8,128)(2,1)}, bf16[2,512,1024]{2,1,0:T(8,128)(2,1)}, u32[]{:S(2)}, u32[]{:S(2)}) collective-permute-start(bf16[2,512,1024]{2,1,0:T(8,128)(2,1)} %param.29), channel_id=1, source_target_pairs={{0,16},{8,24},{16,0},{24,8},{1,17},{9,25},{17,1},{25,9},{2,18},{10... | collective-permute-start | bytes 6291464 | tf_op jit(solution)/shard_map/ppermute | solution.py:1238
  130.0 102.1 %all-gather.12.cloned.1.call-start = ((), (), s32[]{:S(2)}) async-start(), calls=%async_computation.17 | async-start | bytes 4718592 | tf_op jit(solution)/shard_map/all_gather | solution.py:1375
  157.2 148.6 %all-gather.10.cloned.1.call-start = ((), (), s32[]{:S(2)}) async-start(), calls=%async_computation.13 | async-start | bytes 4718592 | tf_op jit(solution)/shard_map/all_gather | solution.py:1394
  157.3 49.6 %collective-permute-start.8 = (bf16[512,2176]{1,0:T(8,128)(2,1)}, bf16[512,2176]{1,0:T(8,128)(2,1)S(1)}, u32[]{:S(2)}, u32[]{:S(2)}) collective-permute-start(bf16[512,2176]{1,0:T(8,128)(2,1)} %all-gather.8.cloned.1.call-done.p0), channel_id=1, source_target_pairs={{0,16},{8,24},{16,0},{24,8},{1,17},{9,25},{17,1},{25,9},{2,18},{10... | collective-permute-start | bytes 6684680 | tf_op jit(solution)/shard_map/ppermute | solution.py:1238
  158.8 57.9 %collective-permute-start.10 = (bf16[2,512,1024]{2,1,0:T(8,128)(2,1)}, bf16[2,512,1024]{2,1,0:T(8,128)(2,1)}, u32[]{:S(2)}, u32[]{:S(2)}) collective-permute-start(bf16[2,512,1024]{2,1,0:T(8,128)(2,1)} %param.29), channel_id=1, source_target_pairs={{0,8},{8,0},{16,24},{24,16},{1,9},{9,1},{17,25},{25,17},{2,10},{10... | collective-permute-start | bytes 6291464 | tf_op jit(solution)/shard_map/ppermute | solution.py:1238
  158.8 57.9 %collective-permute-start.11 = (bf16[2,512,1024]{2,1,0:T(8,128)(2,1)}, bf16[2,512,1024]{2,1,0:T(8,128)(2,1)}, u32[]{:S(2)}, u32[]{:S(2)}) collective-permute-start(bf16[2,512,1024]{2,1,0:T(8,128)(2,1)} %collective-permute-done.6), channel_id=1, source_target_pairs={{0,8},{8,0},{16,24},{24,16},{1,9},{9,1},{17,25},{25,17},{2,10},{10... | collective-permute-start | bytes 6291464 | tf_op jit(solution)/shard_map/ppermute | solution.py:1238
  159.3 64.4 %collective-permute-start.7 = (bf16[512,2176]{1,0:T(8,128)(2,1)}, bf16[512,2176]{1,0:T(8,128)(2,1)}, u32[]{:S(2)}, u32[]{:S(2)}) collective-permute-start(bf16[512,2176]{1,0:T(8,128)(2,1)} %all-gather.8.cloned.1.call-done.p0), channel_id=1, source_target_pairs={{0,8},{8,0},{16,24},{24,16},{1,9},{9,1},{17,25},{25,17},{2,10},{10... | collective-permute-start | bytes 6684680 | tf_op jit(solution)/shard_map/ppermute | solution.py:1238
  232.1 206.9 %reduce-scatter.4.cloned.1.call-start = ((), (), s32[]{:S(2)}) async-start(), calls=%async_computation.14 | async-start | bytes 4718592 | tf_op jit(solution)/shard_map/reduce_scatter | solution.py:1411
  232.2 46.8 %collective-permute-start.12 = (bf16[2,1024,512]{2,1,0:T(8,128)(2,1)}, bf16[2,1024,512]{2,1,0:T(8,128)(2,1)S(1)}, u32[]{:S(2)}, u32[]{:S(2)}) collective-permute-start(bf16[2,1024,512]{2,1,0:T(8,128)(2,1)} %param.30), channel_id=1, source_target_pairs={{0,16},{8,24},{16,0},{24,8},{1,17},{9,25},{17,1},{25,9},{2,18},{10... | collective-permute-start | bytes 6291464 | tf_op jit(solution)/shard_map/ppermute | solution.py:1238
  233.7 47.3 %collective-permute-start.13 = (bf16[2,1024,512]{2,1,0:T(8,128)(2,1)}, bf16[2,1024,512]{2,1,0:T(8,128)(2,1)}, u32[]{:S(2)}, u32[]{:S(2)}) collective-permute-start(bf16[2,1024,512]{2,1,0:T(8,128)(2,1)} %param.30), channel_id=1, source_target_pairs={{0,8},{8,0},{16,24},{24,16},{1,9},{9,1},{17,25},{25,17},{2,10},{10... | collective-permute-start | bytes 6291464 | tf_op jit(solution)/shard_map/ppermute | solution.py:1238
  352.6 215.7 %reduce-scatter.6.cloned.1.call-start = ((), (), s32[]{:S(2)}) async-start(), calls=%async_computation.15 | async-start | bytes 4718592 | tf_op jit(solution)/shard_map/reduce_scatter | solution.py:1422
  441.8 45.4 %collective-permute-start.20 = (bf16[512,1024]{1,0:T(8,128)(2,1)S(1)}, bf16[512,1024]{1,0:T(8,128)(2,1)S(1)}, u32[]{:S(2)}, u32[]{:S(2)}) collective-permute-start(bf16[512,1024]{1,0:T(8,128)(2,1)S(1)} %get-tuple-element.256), channel_id=1, source_target_pairs={{0,16},{8,24},{16,0},{24,8},{1,17},{9,25},{17,1},{25,9},{2,18},{10... | collective-permute-start | bytes 3145736 | tf_op jit(solution)/shard_map/ppermute | solution.py:1238
  496.9 45.9 %collective-permute-start.22 = (bf16[512,1024]{1,0:T(8,128)(2,1)}, bf16[512,1024]{1,0:T(8,128)(2,1)}, u32[]{:S(2)}, u32[]{:S(2)}) collective-permute-start(bf16[512,1024]{1,0:T(8,128)(2,1)} %get-tuple-element.254), channel_id=1, source_target_pairs={{0,16},{8,24},{16,0},{24,8},{1,17},{9,25},{17,1},{25,9},{2,18},{10... | collective-permute-start | bytes 3145736 | tf_op jit(solution)/shard_map/ppermute | solution.py:1238
  511.9 167.6 %reduce-scatter.8.cloned.1.call-start = ((), (), s32[]{:S(2)}) async-start(), calls=%async_computation.16 | async-start | bytes 4718592 | tf_op jit(solution)/shard_map/reduce_scatter | solution.py:1454
  511.9 56.3 %collective-permute-start.23 = (bf16[512,1024]{1,0:T(8,128)(2,1)}, bf16[512,1024]{1,0:T(8,128)(2,1)}, u32[]{:S(2)}, u32[]{:S(2)}) collective-permute-start(bf16[512,1024]{1,0:T(8,128)(2,1)} %get-tuple-element.253), channel_id=1, source_target_pairs={{0,16},{8,24},{16,0},{24,8},{1,17},{9,25},{17,1},{25,9},{2,18},{10... | collective-permute-start | bytes 3145736 | tf_op jit(solution)/shard_map/ppermute | solution.py:1238
  513.4 55.2 %collective-permute-start.25 = (bf16[2,512,1024]{2,1,0:T(8,128)(2,1)}, bf16[2,512,1024]{2,1,0:T(8,128)(2,1)S(1)}, u32[]{:S(2)}, u32[]{:S(2)}) collective-permute-start(bf16[2,512,1024]{2,1,0:T(8,128)(2,1)} %get-tuple-element.211), channel_id=1, source_target_pairs={{0,8},{8,0},{16,24},{24,16},{1,9},{9,1},{17,25},{25,17},{2,10},{10... | collective-permute-start | bytes 6291464 | tf_op jit(solution)/shard_map/ppermute | solution.py:1238
  513.5 59.9 %collective-permute-start.24 = (bf16[2,1024,512]{2,1,0:T(8,128)(2,1)}, bf16[2,1024,512]{2,1,0:T(8,128)(2,1)}, u32[]{:S(2)}, u32[]{:S(2)}) collective-permute-start(bf16[2,1024,512]{2,1,0:T(8,128)(2,1)} %get-tuple-element.207), channel_id=1, source_target_pairs={{0,8},{8,0},{16,24},{24,16},{1,9},{9,1},{17,25},{25,17},{2,10},{10... | collective-permute-start | bytes 6291464 | tf_op jit(solution)/shard_map/ppermute | solution.py:1238
  577.1 42.9 %collective-permute-start.26 = (bf16[2,512,1024]{2,1,0:T(8,128)(2,1)}, bf16[2,512,1024]{2,1,0:T(8,128)(2,1)}, u32[]{:S(2)}, u32[]{:S(2)}) collective-permute-start(bf16[2,512,1024]{2,1,0:T(8,128)(2,1)} %get-tuple-element.215), channel_id=1, source_target_pairs={{0,8},{8,0},{16,24},{24,16},{1,9},{9,1},{17,25},{25,17},{2,10},{10... | collective-permute-start | bytes 6291464 | tf_op jit(solution)/shard_map/ppermute | solution.py:1238
  628.8 38.3 %all-to-all-start.6 = ((bf16[8,64,768]{2,1,0:T(8,128)(2,1)}), bf16[8,64,768]{2,1,0:T(8,128)(2,1)S(1)}, u32[]{:S(2)}, u32[]{:S(2)}) async-start(bf16[8,64,768]{2,1,0:T(8,128)(2,1)} %bitcast.66), calls=%async_computation.9 | async-start | bytes 1572864 | tf_op jit(solution)/shard_map/all_to_all | solution.py:1458
  (81 other events, 1209.2 us)
Sparse Core Ops, SparseCore 0:
  11.3 91.8 all-gather.5
  106.0 51.1 all-gather.7
  159.9 72.1 all-gather.11
  234.1 71.6 all-gather.9
  352.7 86.3 reduce-scatter.3
  443.0 101.4 reduce-scatter.5
  568.4 101.6 reduce-scatter.7

commit v4 on v3

--- a/solution.py
+++ b/solution.py
@@ -768,37 +768,46 @@
     )
 
 
-def combine_experts(act, down, weight):
+def combine_experts(y_at, act, down, weight):
     held, ff, width = down.shape
     rows = act.shape[1]
-    tile, tm = (math.gcd(width, 512), row_tiles(rows))
-
-    def body(act_ref, down_ref, weight_ref, out_ref):
-        @pl.loop(0, rows // tm)
-        def _(i):
-            at = pl.ds(pl.multiple_of(i * tm, tm), tm)
+    block = rows // 8
+    tile, tm = (math.gcd(width, 512), 4 * block)
+
+    def body(y_ref, act_ref, down_ref, weight_ref, near_ref, far_ref):
+        for i in range(2):
+            at = slice(i * tm, (i + 1) * tm)
             total = weight_ref[0, at, :] * mm(act_ref[0, at, :], down_ref[0], ((1,), (0,)))
             for e in range(1, held):
                 term = mm(act_ref[e, at, :], down_ref[e], ((1,), (0,)))
                 total = total + weight_ref[e, at, :] * term
-            out_ref[at, :] = total.astype(jnp.bfloat16)
-
-    return grid_call(
+            total = total.astype(jnp.bfloat16)
+            for y, outs in ((0, (near_ref, far_ref)), (1, (far_ref, near_ref))):
+
+                @pl.when(y_ref[0] == y)
+                def _(outs=outs):
+                    for j in range(4):
+                        to = (2 * i + j // 2) * block
+                        outs[j % 2][to : to + block, :] = total[j * block : (j + 1) * block]
+
+    half = jax.ShapeDtypeStruct((rows // 2, width), jnp.bfloat16)
+    tiled = pl.BlockSpec((rows // 2, tile), lambda n, y: (0, n))
+    return pl.pallas_call(
         body,
-        (width // tile,),
-        [
-            pl.BlockSpec((held, rows, ff), lambda n: (0, 0, 0)),
-            pl.BlockSpec((held, ff, tile), lambda n: (0, 0, n)),
-            pl.BlockSpec((held, rows, 1), lambda n: (0, 0, 0)),
-        ],
-        pl.BlockSpec((rows, tile), lambda n: (0, n)),
-        jax.ShapeDtypeStruct((rows, width), jnp.bfloat16),
-        2 * held * rows * ff * width,
-        0,
-        act,
-        down,
-        weight,
-    )
+        grid_spec=pltpu.PrefetchScalarGridSpec(
+            num_scalar_prefetch=1,
+            grid=(width // tile,),
+            in_specs=[
+                pl.BlockSpec((held, rows, ff), lambda n, y: (0, 0, 0)),
+                pl.BlockSpec((held, ff, tile), lambda n, y: (0, 0, n)),
+                pl.BlockSpec((held, rows, 1), lambda n, y: (0, 0, 0)),
+            ],
+            out_specs=[tiled, tiled],
+        ),
+        out_shape=[half, half],
+        compiler_params=pltpu.CompilerParams(vmem_limit_bytes=VMEM_GRANT),
+        cost_estimate=cost(2 * held * rows * ff * width, 0, act, down, half, half),
+    )(y_at, act, down, weight)
 
 
 def weight_pieces(left, right, parts, split_left):
@@ -1234,6 +1243,17 @@
     )(order, attended, columns)
 
 
+def over_y(values):
+    return lax.ppermute(values, "seq", [(i, i ^ 1) for i in range(8)])
+
+
+def sum_along_z(values):
+    lines = [[0, 2, 4, 6], [1, 3, 5, 7]]
+    return lax.psum_scatter(
+        values, "seq", scatter_dimension=0, tiled=True, axis_index_groups=lines
+    )
+
+
 def swap(values, bits):
     return lax.ppermute(values, "dp", [(i, i ^ bits) for i in range(4)])
 
@@ -1330,8 +1350,6 @@
     qkv_pieces = (blocks, swap(blocks, 1), across, swap(across, 1))
     gate_across = swap(w_gate, 2)
     gate_full = jnp.concatenate([w_gate, swap(w_gate, 1), gate_across, swap(gate_across, 1)], axis=1)
-    x_row, qkv_pieces, gate_full = barrier((x_row, qkv_pieces, gate_full))
-
     w_qkv = jnp.concatenate(
         [
             p[:, : 3 * block_rows]
@@ -1349,6 +1367,9 @@
     g_attn = jnp.concatenate(
         [p[:, 3 * block_rows + 2, :block_rows].reshape(1, chunk) for p in qkv_pieces], axis=1
     ).astype(full)
+    x_row, w_qkv, g_query, g_key, g_attn, gate_full = barrier(
+        (x_row, w_qkv, g_query, g_key, g_attn, gate_full)
+    )
 
     picks = routes.shape[2]
     packed = tokens // block_rows
@@ -1399,8 +1420,10 @@
     act, dgate_factor, dup_factor = expert_activations(normed_ffn, gate_full, up_full)
     act, down_across = barrier((act, swap(w_down, 2)))
     down_full = jnp.concatenate([w_down, swap(w_down, 1), down_across, swap(down_across, 1)], axis=2)
-    mixture = combine_experts(act, down_full, gates)
-    dy_row, mixture, act = barrier((dy_row, mixture, act))
+    y_at = (seq_index % 2).astype(jnp.int32)[None]
+    mixture, mixture_far = combine_experts(y_at, act, down_full, gates)
+    dy_row, mixture_far, act = barrier((dy_row, mixture_far, act))
+    mixture_far = over_y(mixture_far)
 
     scaled, dgate, dup, gate_sums = expert_gradients(
         dy_row, down_full, act, dgate_factor, dup_factor, gates
@@ -1408,7 +1431,9 @@
     nf_grad, grad_logits = input_gradient(
         dgate, dup, gate_full, up_full, gate_sums, chances, chosen, own, router
     )
+    nf_grad, mixture_far = barrier((nf_grad, mixture_far))
     nf_sum = lax.psum_scatter(nf_grad, "seq", scatter_dimension=0, tiled=True)
+    mixture = (mixture.astype(full) + mixture_far.astype(full)).astype(low)
 
     down_kept, down_passed = sum_in_chip(weight_pieces(scaled, dy_row, 4, False), low)
     gate_pieces = weight_pieces(normed_ffn, dgate, 4, True)
@@ -1416,28 +1441,24 @@
     down_arrived = across_by_expert(down_passed)
     gate_kept, gate_passed = sum_in_chip(gate_pieces, low)
     up_pieces = weight_pieces(normed_ffn, dup, 4, True)
-    nf_sum, mixture, up_pieces, down_arrived[0], gate_passed = barrier(
-        (nf_sum, mixture, up_pieces, down_arrived[0], gate_passed)
-    )
-    mixture_own = lax.psum_scatter(mixture, "seq", scatter_dimension=0, tiled=True)
+    up_pieces, down_arrived[0] = barrier((up_pieces, down_arrived[0]))
     up_kept, up_passed = sum_in_chip(up_pieces, low)
     router_grad = mm(grad_logits[:, :expert_count], normed_ffn, ((0,), (0,)))
-    nf_sum, down_arrived[1], up_passed, router_grad = barrier(
-        (nf_sum, down_arrived[1], up_passed, router_grad)
-    )
-    gate_arrived, up_arrived = (across_by_expert(gate_passed), across_by_expert(up_passed))
+    nf_sum, mixture, down_arrived[1], gate_passed, up_passed, router_grad, down_kept, gate_kept, up_kept = barrier(
+        (nf_sum, mixture, down_arrived[1], gate_passed, up_passed, router_grad, down_kept, gate_kept, up_kept)
+    )
+    gate_arrived, up_arrived = (across_by_expert(gate_passed), [swap(up_passed[0], 2)])
 
     grad_mid, mid_low, grad_attended, gain_ffn_grad = middle(
         order, nf_sum, hidden_mid, r_ffn, g_ffn, dy_shard, out_pieces
     )
-    grad_attended, gate_arrived[0] = barrier((grad_attended, gate_arrived[0]))
-
     def to_columns(values):
         return lax.all_to_all(values, "seq", 0, 0, tiled=True).reshape(rows, cols)
 
     grad_attended = grad_attended.reshape(4, tokens, shards // 4, cols).transpose(0, 2, 1, 3)
     grad_attended = to_columns(grad_attended.reshape(shards, tokens, cols))
-    grad_attended, gate_arrived[1] = barrier((grad_attended, gate_arrived[1]))
+    grad_attended, gate_arrived[0], mixture = barrier((grad_attended, gate_arrived[0], mixture))
+    mixture_own = sum_along_z(mixture)
     mid_cols = to_columns(
         reorder(mid_low, dp_index, 1).reshape(tokens, shards, cols).transpose(1, 0, 2)
     )
@@ -1445,12 +1466,12 @@
         qkv, q_rot, k_rot, value_in, grad_attended, log_total,
         r_query, r_key, g_query, g_key, cosine, sine, seg_col, seg_row,
     )
-    sums, up_arrived[0] = barrier((sums, up_arrived[0]))
+    sums, gate_arrived[1] = barrier((sums, gate_arrived[1]))
     sums, mid_cols = barrier((share(sums), mid_cols))
     qkv_low, normed_grad, gain_attn_grad = normed_gradient(
         q_grad, k_grad, v_low, qkv, sums, r_query, r_key, w_qkv, x_row, r_attn
     )
-    normed_grad, up_arrived[1], mixture_own = barrier((normed_grad, up_arrived[1], mixture_own))
+    normed_grad, up_arrived[0], mixture_own = barrier((normed_grad, up_arrived[0], mixture_own))
     normed_sum = lax.psum_scatter(normed_grad, "seq", scatter_dimension=0, tiled=True).astype(full)
 
     def to_owners(kept, passed, count):
@@ -1461,12 +1482,17 @@
         total = total.reshape(shards, block_rows, count, cols).transpose(2, 1, 0, 3)
         return total.reshape(count, block_rows, width).astype(full)
 
-    out_kept, out_passed = sum_in_chip(out_grad_pieces(order, attended_row, mid_cols), low)
+    qkv_parts = [p[0] for p in weight_pieces(normed, qkv_low[None], 4, True)]
+    qkv_parts, mid_cols, gain_attn_grad, gain_ffn_grad = barrier(
+        (qkv_parts, mid_cols, gain_attn_grad, gain_ffn_grad)
+    )
+    qkv_kept, qkv_passed = sum_in_chip(qkv_parts, low)
+    out_parts = out_grad_pieces(order, attended_row, mid_cols)
+    out_kept, out_passed = sum_in_chip(out_parts, low)
+    qkv_passed, out_passed, up_last = barrier((qkv_passed, out_passed, up_passed[1]))
+    proj_grad = to_owners(qkv_kept, qkv_passed, 3)
     out_grad = to_owners(out_kept, out_passed, 1)
-    qkv_kept, qkv_passed = sum_in_chip(
-        [p[0] for p in weight_pieces(normed, qkv_low[None], 4, True)], low
-    )
-    proj_grad = to_owners(qkv_kept, qkv_passed, 3)
+    up_arrived.append(swap(up_last, 2))
     grad_w_down = add_arrived(down_kept, down_arrived)
     grad_w_gate = add_arrived(gate_kept, gate_arrived)
     grad_w_up = add_arrived(up_kept, up_arrived)
@@ -1525,7 +1551,7 @@
 def solution(mesh):
     def layer(*arrays):
         whole_heads = (arrays[0].shape[2] // HEAD) % mesh.shape["seq"] == 0
-        if whole_heads and mesh.shape["dp"] == 4:
+        if whole_heads and mesh.shape["dp"] == 4 and mesh.shape["seq"] == 8:
             return on_device_heads(*arrays)
         return on_device(*arrays)
 

time: 701 us -> 660 us (0.942)
  waiting for transfers between devices: 246 us -> 177 us
  blocking collectives: 14.3 us -> 37.1 us
  other arithmetic: 77.1 us -> 88.5 us
    ppermute x36, waiting for transfers between devices: 158 us -> 98.6 us  [swap(): return lax.ppermute(values, 'dp', [(i, i ^ bits) for i in range(4)])]
    all_to_all x1, waiting for transfers between devices: 0.01 us -> 36.9 us  [on_device_heads(): lax.all_to_all(jnp.concatenate([blocks, gain_rows], axis=1), 'seq', 0, 0,...]
    reduce_scatter x1, waiting for transfers between devices: 21.7 us -> 0.01 us  [on_device_heads(): nf_sum = lax.psum_scatter(nf_grad, 'seq', scatter_dimension=0, tiled=True)]
    all_to_all x0 -> x1, blocking collectives: none -> 18.6 us  [to_columns(): return lax.all_to_all(values, 'seq', 0, 0, tiled=True).reshape(rows, cols)]
    pallas_call x0 -> x1, Pallas kernels: none -> 14.8 us  [combine_experts(): pl.pallas_call(body, grid_spec=pltpu.PrefetchScalarGridSpec(num_scalar_pr...]
    all_to_all x2, waiting for transfers between devices: 21.2 us -> 6.94 us  [to_owners(): lax.all_to_all(total.astype(low).reshape(shards, block_rows, count * cols...]
    pallas_call x11 -> x10, Pallas kernels: 179 us -> 165 us  [grid_call(): pl.pallas_call(body, grid=grid, in_specs=in_specs, out_specs=out_specs, o...]
    all_gather x1, waiting for transfers between devices: 9.61 us -> 0.01 us  [on_device_heads(): x_row = lax.all_gather(x_shard, 'seq', axis=0, tiled=True)]
  transfers between devices with their start and end apart: 50 -> 50, of which waited for: 20 -> 18; matrix products, arithmetic and copies ran while one was open for 17% -> 20% of each run, Pallas kernels for 26% -> 35%
where the time goes in v4:
time: 660 us; the launch traced here: 652 us
  Pallas kernels  229 us (35%)
  waiting for transfers between devices  177 us (27%)
  other arithmetic  88.5 us (13%)
  local copies, waits for them, and re-layouts  54 us (8%)
  starting transfers between devices  49.1 us (7%)
  blocking collectives  37.1 us (6%)
  between operations  15.4 us (2%)
    pallas_call x10, Pallas kernels, grid_call(): pl.pallas_call(body, grid=grid, in_specs=in_specs, out_specs=out_specs, o...  165 us
    ppermute x36, waiting for transfers between devices, swap(): return lax.ppermute(values, 'dp', [(i, i ^ bits) for i in range(4)])  98.6 us
    all_to_all x1, waiting for transfers between devices, on_device_heads(): lax.all_to_all(jnp.concatenate([blocks, gain_rows], axis=1), 'seq', 0, 0,...  36.9 us
    ppermute x36, starting transfers between devices, swap(): return lax.ppermute(values, 'dp', [(i, i ^ bits) for i in range(4)])  19.9 us
    pallas_call x1, Pallas kernels, finish_attention(): pl.pallas_call(body, grid_spec=pltpu.PrefetchScalarGridSpec(num_scalar_pr...  19.1 us
    all_to_all x1, blocking collectives, to_columns(): return lax.all_to_all(values, 'seq', 0, 0, tiled=True).reshape(rows, cols)  18.6 us
    all_to_all x1, blocking collectives, share(): return lax.all_to_all(spread, 'seq', 0, 0, tiled=True)  18.6 us
    another operation x6, other arithmetic, add_arrived(): jnp.stack([kept[e].astype(jnp.float32) + a.astype(jnp.float32) for e, a i...  17.3 us
  transfers between devices with their start and end apart: 50, of which 18 were waited for; matrix products, arithmetic and copies ran while one was open for 20% of the time, Pallas kernels for 35%

profile of v4, /device:TPU:0, one launch (start us, length us, event | category | flops | bytes accessed | tf_op | source)
XLA Modules:
  0.0 651.6 jit_solution(10336026276490949431)
XLA Ops:
  13.1 7.5 %all-to-all-start = ((bf16[8,208,256]{2,1,0:T(8,128)(2,1)}), bf16[8,208,256]{2,1,0:T(8,128)(2,1)S(1)}, u32[]{:S(2)}, u32[]{:S(2)}) async-start(bf16[8,208,256]{2,1,0:T(8,128)(2,1)} %pad_maximum_fusion.6), calls=%async_computation | async-start | bytes 1703936 | tf_op jit(solution)/shard_map/all_to_all | solution.py:1348
  22.2 36.9 %all-to-all-done = bf16[8,208,256]{2,1,0:T(8,128)(2,1)S(1)} async-done(((bf16[8,208,256]{2,1,0:T(8,128)(2,1)}), bf16[8,208,256]{2,1,0:T(8,128)(2,1)S(1)}, u32[]{:S(2)}, u32[]{:S(2)}) %all-to-all-start) | async-done | bytes 852000 | tf_op jit(solution)/shard_map/all_to_all | solution.py:1348
  62.4 7.1 %collective-permute-done.4 = bf16[2,512,1024]{2,1,0:T(8,128)(2,1)} collective-permute-done((bf16[2,512,1024]{2,1,0:T(8,128)(2,1)}, bf16[2,512,1024]{2,1,0:T(8,128)(2,1)}, u32[]{:S(2)}, u32[]{:S(2)}) %collective-permute-start.4) | collective-permute-done | bytes 2097184 | tf_op jit(solution)/shard_map/ppermute | solution.py:1258
  69.5 16.8 %collective-permute-done.1 = bf16[8,208,256]{2,1,0:T(8,128)(2,1)} collective-permute-done((bf16[8,208,256]{2,1,0:T(8,128)(2,1)S(1)}, bf16[8,208,256]{2,1,0:T(8,128)(2,1)}, u32[]{:S(2)}, u32[]{:S(2)}) %collective-permute-start.1) | collective-permute-done | bytes 852000 | tf_op jit(solution)/shard_map/ppermute | solution.py:1258
  109.9 9.5 %shard_map.263 = (bf16[1024,2048]{1,0:T(8,128)(2,1)}, f32[1024,768]{1,0:T(8,128)}, f32[1024,1]{1,0:T(8,128)}, f32[8,1024]{1,0:T(8,128)}) custom-call(bf16[1024,2048]{1,0:T(8,128)(2,1)} %all-gather.6.cloned.1.call-done.x_ref.x, f32[1,2048]{1,0:T(1,128)} %maximum_convert_fusion.gain_ref, bf16[2048,768]{1,0:T(8,128)(2,1)} %pad_maximum_fusion.5.w_ref.w), custom_call_target="tpu_custom_call" | custom-call | flops 805306368 | bytes 3681280 | tf_op jit(solution)/shard_map/pallas_call | solution.py:518
  130.0 8.3 %all-to-all-done.1.sums_ref = f32[8,8,1024]{2,1,0:T(8,128)S(1)} async-done(((f32[8,8,1024]{2,1,0:T(8,128)}), f32[8,8,1024]{2,1,0:T(8,128)S(1)}, u32[]{:S(2)}, u32[]{:S(2)}) %all-to-all-start.1) | async-done | bytes 262176 | tf_op jit(solution)/shard_map/all_to_all | solution.py:1388
  139.1 11.0 %shard_map.264 = (bf16[1024,256]{1,0:T(8,128)(2,1)}, bf16[1024,256]{1,0:T(8,128)(2,1)}, bf16[1024,256]{1,0:T(8,128)(2,1)}, bf16[1024,256]{1,0:T(8,128)(2,1)}, f3...) custom-call(f32[1024,768]{1,0:T(8,128)} %get-tuple-element.146.q.k.v, ...), custom_call_target="tpu_custom_call" | custom-call | flops 268435456 | bytes 3217920 | tf_op jit(solution)/shard_map/pallas_call | solution.py:518
  156.9 49.5 %collective-permute-done.8.p2 = bf16[512,2176]{1,0:T(8,128)(2,1)S(1)} collective-permute-done((bf16[512,2176]{1,0:T(8,128)(2,1)}, bf16[512,2176]{1,0:T(8,128)(2,1)S(1)}, u32[]{:S(2)}, u32[]{:S(2)}) %collective-permute-start.8) | collective-permute-done | bytes 2228256 | tf_op jit(solution)/shard_map/ppermute | solution.py:1258
  233.0 19.1 %shard_map.265 = (f32[1024,2048]{1,0:T(8,128)}, bf16[1024,2048]{1,0:T(8,128)(2,1)}, f32[1024,1]{1,0:T(8,128)}, f32[1024,128]{1,0:T(8,128)}, f32[2,1024,1]{2,1,0:T(8,128)}) custom-call(s32[5]{0:T(128)} %stack.78.order_ref, bf16[8,1024,256]{2,1,0:T(8,128)(2,1)} %bitcast.175, bf16[512,2176]{1,0:T(8,128)(2,1)} %all-gather.8.cloned.1.call-done.p0, ...), custom_call_target="tpu_custom_call" | custom-call | flops 2147483648 | bytes 6556672 | tf_op jit(solution)/shard_map/pallas_call | solution.py:587
  252.1 25.0 %shard_map.266 = (bf16[2,1024,1024]{2,1,0:T(8,128)(2,1)}, bf16[2,1024,1024]{2,1,0:T(8,128)(2,1)}, bf16[2,1024,1024]{2,1,0:T(8,128)(2,1)}) custom-call(bf16[1024,2048]{1,0:T(8,128)(2,1)} %get-tuple-element.167.x_ref.flat_ref, bf16[2,2048,1024]{2,1,0:T(8,128)(2,1)} %pad_maximum_fusion.gate_ref, bf16[2,2048,1024]{2,1,0:T(8,128)(2,1)} %pad_maximum_fusion.1.up_ref), custom_call_target="tpu_custom_call" | custom-call | flops 4294967296 | bytes 8388608 | tf_op jit(solution)/shard_map/pallas_call | solution.py:518
  288.7 14.8 %shard_map.267 = (bf16[512,2048]{1,0:T(8,128)(2,1)}, bf16[512,2048]{1,0:T(8,128)(2,1)}) custom-call(s32[1]{0:T(128)} %bitcast.34.y_ref, bf16[2,1024,1024]{2,1,0:T(8,128)(2,1)} %get-tuple-element.176.act_ref, bf16[2,1024,2048]{2,1,0:T(8,128)(2,1)} %constant_dynamic-update-slice_fusion.1.down_ref, f32[2,1024,1]{2,1,0:T(8,128)} %get-tuple-element.173.weight_ref), custom_call_target="tpu_custom_call" | custom-call | flops 2147483648 | bytes 4194304 | tf_op jit(solution)/shard_map/pallas_call | solution.py:795
  303.8 20.4 %shard_map.268 = (bf16[2,1024,1024]{2,1,0:T(8,128)(2,1)}, bf16[2,1024,1024]{2,1,0:T(8,128)(2,1)}, bf16[2,1024,1024]{2,1,0:T(8,128)(2,1)}, f32[2,1024,128]{2,1,0:T(8,128)}) custom-call(bf16[1024,2048]{1,0:T(8,128)(2,1)} %all-gather.10.cloned.1.call-done.dy_ref.flat_ref, bf16[2,1024,2048]{2,1,0:T(8,128)(2,1)} %constant_dynamic-update-slice_fusion.1.down_ref, ...), custom_call_target="tpu_custom_call" | custom-call | flops 2147483648 | bytes 9701376 | tf_op jit(solution)/shard_map/pallas_call | solution.py:518
  324.2 26.4 %shard_map.269 = (bf16[1024,2048]{1,0:T(8,128)(2,1)}, bf16[1024,128]{1,0:T(8,128)(2,1)}) custom-call(bf16[2,1024,1024]{2,1,0:T(8,128)(2,1)} %get-tuple-element.179.dgate_ref.stacked_ref, bf16[2,1024,1024]{2,1,0:T(8,128)(2,1)} %get-tuple-element.194.dup_ref.stacked_ref, bf16[2,2048,1024]{2,1,0:T(8,128)(2,1)} %pad_maximum_fusion.gate_ref, ...), custom_call_target="tpu_custom_call" | custom-call | flops 4294967296 | bytes 8061184 | tf_op jit(solution)/shard_map/pallas_call | solution.py:518
  351.5 18.6 %shard_map.270 = (bf16[2,1024,512]{2,1,0:T(8,128)(2,1)}, bf16[2,1024,512]{2,1,0:T(8,128)(2,1)}, bf16[2,1024,512]{2,1,0:T(8,128)(2,1)}, bf16[2,1024,512]{2,1,0:T(8,128)(2,1)}) custom-call(bf16[1024,2048]{1,0:T(8,128)(2,1)} %all-gather.10.cloned.1.call-done.dy_ref.flat_ref, bf16[2,1024,1024]{2,1,0:T(8,128)(2,1)} %get-tuple-element.188.stacked_ref), custom_call_target="tpu_custom_call" | custom-call | flops 2147483648 | bytes 4194304 | tf_op jit(solution)/shard_map/pallas_call | solution.py:518
  370.2 17.9 %shard_map.271 = (bf16[2,512,1024]{2,1,0:T(8,128)(2,1)}, bf16[2,512,1024]{2,1,0:T(8,128)(2,1)}, bf16[2,512,1024]{2,1,0:T(8,128)(2,1)}, bf16[2,512,1024]{2,1,0:T(8,128)(2,1)}) custom-call(bf16[1024,2048]{1,0:T(8,128)(2,1)} %get-tuple-element.167.x_ref.flat_ref, bf16[2,1024,1024]{2,1,0:T(8,128)(2,1)} %get-tuple-element.179.dgate_ref.stacked_ref), custom_call_target="tpu_custom_call" | custom-call | flops 2147483648 | bytes 4194304 | tf_op jit(solution)/shard_map/pallas_call | solution.py:518
  391.5 18.0 %shard_map.272 = (bf16[2,512,1024]{2,1,0:T(8,128)(2,1)}, bf16[2,512,1024]{2,1,0:T(8,128)(2,1)}, bf16[2,512,1024]{2,1,0:T(8,128)(2,1)}, bf16[2,512,1024]{2,1,0:T(8,128)(2,1)}) custom-call(bf16[1024,2048]{1,0:T(8,128)(2,1)} %get-tuple-element.167.x_ref.flat_ref, bf16[2,1024,1024]{2,1,0:T(8,128)(2,1)} %get-tuple-element.194.dup_ref.stacked_ref), custom_call_target="tpu_custom_call" | custom-call | flops 2147483648 | bytes 4194304 | tf_op jit(solution)/shard_map/pallas_call | solution.py:518
  446.8 8.7 %shard_map.273 = (f32[128,2048]{1,0:T(8,128)}, bf16[128,2048]{1,0:T(8,128)(2,1)}, bf16[4,128,512]{2,1,0:T(8,128)(2,1)}, f32[1,2048]{1,0:T(1,128)}) custom-call(s32[5]{0:T(128)} %stack.78.order_ref, bf16[128,2048]{1,0:T(8,128)(2,1)} %reduce-scatter.4.cloned.1.call-done.nf, f32[1024,2048]{1,0:T(8,128)} %get-tuple-element.209.mid_ref, ...), custom_call_target="tpu_custom_call" | custom-call | flops 268435456 | bytes 2754560 | tf_op jit(solution)/shard_map/pallas_call | solution.py:1190
  456.7 18.6 %all_to_all.40 = bf16[8,128,256]{2,1,0:T(8,128)(2,1)} all-to-all(bf16[8,128,256]{2,1,0:T(8,128)(2,1)S(1)} %bitcast.195), channel_id=1, replica_groups=mesh['dp'=4,'seq'=8] {'seq'}, dimensions={0} | all-to-all | bytes 1048576 | tf_op jit(solution)/shard_map/all_to_all | solution.py:1456
  485.6 13.0 %shard_map.274 = (f32[1024,256]{1,0:T(8,128)}, f32[1024,256]{1,0:T(8,128)}, bf16[1024,256]{1,0:T(8,128)(2,1)}, f32[8,1024]{1,0:T(8,128)}, f32[1,256]{1,0:T(1,128)}, /*index=5*/f32[1,256]{1,0:T(1,128)}) custom-call(f32[1024,768]{1,0:T(8,128)} %get-tuple-element.146.q.k.v, f32[1024,768]{1,0:T(8,128)} %get-tuple-element.146.q.k.v, ...), custom_call_target="tpu_custom_call" | custom-call | flops 671088640 | bytes 3030016 | tf_op jit(solution)/shard_map/pallas_call | solution.py:1073
  502.7 9.2 %all-to-all-done.4 = bf16[8,128,256]{2,1,0:T(8,128)(2,1)S(1)} async-done(((bf16[8,128,256]{2,1,0:T(8,128)(2,1)}), bf16[8,128,256]{2,1,0:T(8,128)(2,1)S(1)}, u32[]{:S(2)}, u32[]{:S(2)}) %all-to-all-start.4) | async-done | bytes 524320 | tf_op jit(solution)/shard_map/all_to_all | solution.py:1456
  512.7 18.6 %all_to_all.41.sums_ref = f32[8,8,1024]{2,1,0:T(8,128)} all-to-all(f32[8,8,1024]{2,1,0:T(8,128)S(1)} %broadcast_in_dim.26), channel_id=1, replica_groups=mesh['dp'=4,'seq'=8] {'seq'}, dimensions={0} | all-to-all | bytes 524288 | tf_op jit(solution)/shard_map/all_to_all | solution.py:1388
  531.3 10.4 %shard_map.275 = (bf16[1024,768]{1,0:T(8,128)(2,1)}, bf16[1024,2048]{1,0:T(8,128)(2,1)}, f32[1,2048]{1,0:T(1,128)}) custom-call(f32[1024,256]{1,0:T(8,128)} %get-tuple-element.218.qg, f32[1024,256]{1,0:T(8,128)} %get-tuple-element.219.kg, bf16[1024,256]{1,0:T(8,128)(2,1)} %get-tuple-element.220.v, f32[1024,768]{1,0:T(8,128)} %get-tuple-element.146.q.k.v, ...), custom_call_target="tpu_custom_call" | custom-call | flops 805306368 | bytes 5575680 | tf_op jit(solution)/shard_map/pallas_call | solution.py:518
  542.9 7.9 %shard_map.276 = (bf16[1,512,768]{2,1,0:T(8,128)(2,1)}, bf16[1,512,768]{2,1,0:T(8,128)(2,1)}, bf16[1,512,768]{2,1,0:T(8,128)(2,1)}, bf16[1,512,768]{2,1,0:T(8,128)(2,1)}) custom-call(bf16[1024,2048]{1,0:T(8,128)(2,1)} %get-tuple-element.238.flat_ref, bf16[1,1024,768]{2,1,0:T(8,128)(2,1)} %bitcast.199), custom_call_target="tpu_custom_call" | custom-call | flops 805306368 | bytes 2228224 | tf_op jit(solution)/shard_map/pallas_call | solution.py:518
  551.5 8.2 %shard_map.277 = (bf16[512,256]{1,0:T(8,128)(2,1)}, bf16[512,256]{1,0:T(8,128)(2,1)}, bf16[512,256]{1,0:T(8,128)(2,1)}, bf16[512,256]{1,0:T(8,128)(2,1)}) custom-call(s32[5]{0:T(128)} %stack.78.order_ref, bf16[8,1024,256]{2,1,0:T(8,128)(2,1)} %bitcast.176, bf16[1024,256]{1,0:T(8,128)(2,1)} %bitcast.192), custom_call_target="tpu_custom_call" | custom-call | flops 268435456 | bytes 1441792 | tf_op jit(solution)/shard_map/pallas_call | solution.py:1229
  (345 shorter events, 234.9 us)
Async XLA Ops:
  7.2 102.7 %all-gather.6.cloned.1.call-start = ((), (), s32[]{:S(2)}) async-start(), calls=%async_computation.11 | async-start | bytes 4718592 | tf_op jit(solution)/shard_map/all_gather | solution.py:1333
  13.1 46.0 %all-to-all-start = ((bf16[8,208,256]{2,1,0:T(8,128)(2,1)}), bf16[8,208,256]{2,1,0:T(8,128)(2,1)S(1)}, u32[]{:S(2)}, u32[]{:S(2)}) async-start(bf16[8,208,256]{2,1,0:T(8,128)(2,1)} %pad_maximum_fusion.6), calls=%async_computation | async-start | bytes 1703936 | tf_op jit(solution)/shard_map/all_to_all | solution.py:1348
  20.5 135.3 %all-gather.8.cloned.1.call-start = ((), (), s32[]{:S(2)}) async-start(), calls=%async_computation.12 | async-start | bytes 2506752 | tf_op jit(solution)/shard_map/all_gather | solution.py:1381
  20.6 48.9 %collective-permute-start.4 = (bf16[2,512,1024]{2,1,0:T(8,128)(2,1)}, bf16[2,512,1024]{2,1,0:T(8,128)(2,1)}, u32[]{:S(2)}, u32[]{:S(2)}) collective-permute-start(bf16[2,512,1024]{2,1,0:T(8,128)(2,1)} %param.28), channel_id=1, source_target_pairs={{0,16},{8,24},{16,0},{24,8},{1,17},{9,25},{17,1},{25,9},{2,18},{10... | collective-permute-start | bytes 6291464 | tf_op jit(solution)/shard_map/ppermute | solution.py:1258
  61.9 40.9 %collective-permute-start.3 = (bf16[2,512,1024]{2,1,0:T(8,128)(2,1)}, bf16[2,512,1024]{2,1,0:T(8,128)(2,1)}, u32[]{:S(2)}, u32[]{:S(2)}) collective-permute-start(bf16[2,512,1024]{2,1,0:T(8,128)(2,1)} %param.28), channel_id=1, source_target_pairs={{0,8},{8,0},{16,24},{24,16},{1,9},{9,1},{17,25},{25,17},{2,10},{10... | collective-permute-start | bytes 6291464 | tf_op jit(solution)/shard_map/ppermute | solution.py:1258
  69.5 33.3 %collective-permute-start.5 = (bf16[2,512,1024]{2,1,0:T(8,128)(2,1)}, bf16[2,512,1024]{2,1,0:T(8,128)(2,1)}, u32[]{:S(2)}, u32[]{:S(2)}) collective-permute-start(bf16[2,512,1024]{2,1,0:T(8,128)(2,1)} %collective-permute-done.4), channel_id=1, source_target_pairs={{0,8},{8,0},{16,24},{24,16},{1,9},{9,1},{17,25},{25,17},{2,10},{10... | collective-permute-start | bytes 6291464 | tf_op jit(solution)/shard_map/ppermute | solution.py:1258
  86.4 63.7 %collective-permute-start.6 = (bf16[2,512,1024]{2,1,0:T(8,128)(2,1)}, bf16[2,512,1024]{2,1,0:T(8,128)(2,1)}, u32[]{:S(2)}, u32[]{:S(2)}) collective-permute-start(bf16[2,512,1024]{2,1,0:T(8,128)(2,1)} %param.29), channel_id=1, source_target_pairs={{0,16},{8,24},{16,0},{24,8},{1,17},{9,25},{17,1},{25,9},{2,18},{10... | collective-permute-start | bytes 6291464 | tf_op jit(solution)/shard_map/ppermute | solution.py:1258
  126.4 103.2 %all-gather.12.cloned.1.call-start = ((), (), s32[]{:S(2)}) async-start(), calls=%async_computation.17 | async-start | bytes 4718592 | tf_op jit(solution)/shard_map/all_gather | solution.py:1396
  155.9 147.7 %all-gather.10.cloned.1.call-start = ((), (), s32[]{:S(2)}) async-start(), calls=%async_computation.13 | async-start | bytes 4718592 | tf_op jit(solution)/shard_map/all_gather | solution.py:1415
  155.9 50.5 %collective-permute-start.8 = (bf16[512,2176]{1,0:T(8,128)(2,1)}, bf16[512,2176]{1,0:T(8,128)(2,1)S(1)}, u32[]{:S(2)}, u32[]{:S(2)}) collective-permute-start(bf16[512,2176]{1,0:T(8,128)(2,1)} %all-gather.8.cloned.1.call-done.p0), channel_id=1, source_target_pairs={{0,16},{8,24},{16,0},{24,8},{1,17},{9,25},{17,1},{25,9},{2,18},{10... | collective-permute-start | bytes 6684680 | tf_op jit(solution)/shard_map/ppermute | solution.py:1258
  156.4 59.7 %collective-permute-start.10 = (bf16[2,512,1024]{2,1,0:T(8,128)(2,1)}, bf16[2,512,1024]{2,1,0:T(8,128)(2,1)}, u32[]{:S(2)}, u32[]{:S(2)}) collective-permute-start(bf16[2,512,1024]{2,1,0:T(8,128)(2,1)} %param.29), channel_id=1, source_target_pairs={{0,8},{8,0},{16,24},{24,16},{1,9},{9,1},{17,25},{25,17},{2,10},{10... | collective-permute-start | bytes 6291464 | tf_op jit(solution)/shard_map/ppermute | solution.py:1258
  156.4 59.7 %collective-permute-start.11 = (bf16[2,512,1024]{2,1,0:T(8,128)(2,1)}, bf16[2,512,1024]{2,1,0:T(8,128)(2,1)}, u32[]{:S(2)}, u32[]{:S(2)}) collective-permute-start(bf16[2,512,1024]{2,1,0:T(8,128)(2,1)} %collective-permute-done.6), channel_id=1, source_target_pairs={{0,8},{8,0},{16,24},{24,16},{1,9},{9,1},{17,25},{25,17},{2,10},{10... | collective-permute-start | bytes 6291464 | tf_op jit(solution)/shard_map/ppermute | solution.py:1258
  156.9 66.3 %collective-permute-start.7 = (bf16[512,2176]{1,0:T(8,128)(2,1)}, bf16[512,2176]{1,0:T(8,128)(2,1)}, u32[]{:S(2)}, u32[]{:S(2)}) collective-permute-start(bf16[512,2176]{1,0:T(8,128)(2,1)} %all-gather.8.cloned.1.call-done.p0), channel_id=1, source_target_pairs={{0,8},{8,0},{16,24},{24,16},{1,9},{9,1},{17,25},{25,17},{2,10},{10... | collective-permute-start | bytes 6684680 | tf_op jit(solution)/shard_map/ppermute | solution.py:1258
  229.6 213.3 %reduce-scatter.4.cloned.1.call-start = ((), (), s32[]{:S(2)}) async-start(), calls=%async_computation.14 | async-start | bytes 4718592 | tf_op jit(solution)/shard_map/reduce_scatter | solution.py:1435
  230.2 46.9 %collective-permute-start.12 = (bf16[2,1024,512]{2,1,0:T(8,128)(2,1)}, bf16[2,1024,512]{2,1,0:T(8,128)(2,1)}, u32[]{:S(2)}, u32[]{:S(2)}) collective-permute-start(bf16[2,1024,512]{2,1,0:T(8,128)(2,1)} %param.30), channel_id=1, source_target_pairs={{0,16},{8,24},{16,0},{24,8},{1,17},{9,25},{17,1},{25,9},{2,18},{10... | collective-permute-start | bytes 6291464 | tf_op jit(solution)/shard_map/ppermute | solution.py:1258
  231.7 47.5 %collective-permute-start.13 = (bf16[2,1024,512]{2,1,0:T(8,128)(2,1)}, bf16[2,1024,512]{2,1,0:T(8,128)(2,1)}, u32[]{:S(2)}, u32[]{:S(2)}) collective-permute-start(bf16[2,1024,512]{2,1,0:T(8,128)(2,1)} %param.30), channel_id=1, source_target_pairs={{0,8},{8,0},{16,24},{24,16},{1,9},{9,1},{17,25},{25,17},{2,10},{10... | collective-permute-start | bytes 6291464 | tf_op jit(solution)/shard_map/ppermute | solution.py:1258
  303.6 47.7 %collective-permute-start.15 = (bf16[512,2048]{1,0:T(8,128)(2,1)}, bf16[512,2048]{1,0:T(8,128)(2,1)S(1)}, u32[]{:S(2)}, u32[]{:S(2)}) collective-permute-start(bf16[512,2048]{1,0:T(8,128)(2,1)} %get-tuple-element.184), channel_id=1, source_target_pairs={{0,1},{1,0},{2,3},{3,2},{4,5},{5,4},{6,7},{7,6},{8,9},{9,8},{10,11... | collective-permute-start | bytes 6291464 | tf_op jit(solution)/shard_map/ppermute | solution.py:1247
  351.3 190.4 %reduce-scatter.6.cloned.1.call-start = ((), (), s32[]{:S(2)}) async-start(), calls=%async_computation.15 | async-start | bytes 2621440 | tf_op jit(solution)/shard_map/reduce_scatter | solution.py:1252
  388.0 30.4 %collective-permute-start.22 = (bf16[2,512,1024]{2,1,0:T(8,128)(2,1)}, bf16[2,512,1024]{2,1,0:T(8,128)(2,1)}, u32[]{:S(2)}, u32[]{:S(2)}) collective-permute-start(bf16[2,512,1024]{2,1,0:T(8,128)(2,1)} %get-tuple-element.205), channel_id=1, source_target_pairs={{0,8},{8,0},{16,24},{24,16},{1,9},{9,1},{17,25},{25,17},{2,10},{10... | collective-permute-start | bytes 6291464 | tf_op jit(solution)/shard_map/ppermute | solution.py:1258
  388.3 34.5 %collective-permute-start.21 = (bf16[2,1024,512]{2,1,0:T(8,128)(2,1)}, bf16[2,1024,512]{2,1,0:T(8,128)(2,1)}, u32[]{:S(2)}, u32[]{:S(2)}) collective-permute-start(bf16[2,1024,512]{2,1,0:T(8,128)(2,1)} %get-tuple-element.203), channel_id=1, source_target_pairs={{0,8},{8,0},{16,24},{24,16},{1,9},{9,1},{17,25},{25,17},{2,10},{10... | collective-permute-start | bytes 6291464 | tf_op jit(solution)/shard_map/ppermute | solution.py:1258
  391.4 37.2 %collective-permute-start.18 = (bf16[2,512,1024]{2,1,0:T(8,128)(2,1)}, bf16[2,512,1024]{2,1,0:T(8,128)(2,1)}, u32[]{:S(2)}, u32[]{:S(2)}) collective-permute-start(bf16[2,512,1024]{2,1,0:T(8,128)(2,1)} %get-tuple-element.193), channel_id=1, source_target_pairs={{0,8},{8,0},{16,24},{24,16},{1,9},{9,1},{17,25},{25,17},{2,10},{10... | collective-permute-start | bytes 6291464 | tf_op jit(solution)/shard_map/ppermute | solution.py:1258
  478.9 33.1 %all-to-all-start.4 = ((bf16[8,128,256]{2,1,0:T(8,128)(2,1)}), bf16[8,128,256]{2,1,0:T(8,128)(2,1)S(1)}, u32[]{:S(2)}, u32[]{:S(2)}) async-start(bf16[8,128,256]{2,1,0:T(8,128)(2,1)} %bitcast.170), calls=%async_computation.5 | async-start | bytes 1048576 | tf_op jit(solution)/shard_map/all_to_all | solution.py:1456
  482.5 158.2 %reduce-scatter.8.cloned.1.call-start = ((), (), s32[]{:S(2)}) async-start(), calls=%async_computation.16 | async-start | bytes 4718592 | tf_op jit(solution)/shard_map/reduce_scatter | solution.py:1475
  484.1 57.6 %collective-permute-start.26 = (bf16[512,1024]{1,0:T(8,128)(2,1)}, bf16[512,1024]{1,0:T(8,128)(2,1)S(1)}, u32[]{:S(2)}, u32[]{:S(2)}) collective-permute-start(bf16[512,1024]{1,0:T(8,128)(2,1)} %get-tuple-element.280), channel_id=1, source_target_pairs={{0,16},{8,24},{16,0},{24,8},{1,17},{9,25},{17,1},{25,9},{2,18},{10... | collective-permute-start | bytes 3145736 | tf_op jit(solution)/shard_map/ppermute | solution.py:1258
  (77 other events, 1278.2 us)
Sparse Core Ops, SparseCore 0:
  11.2 91.5 all-gather.5
  105.6 50.2 all-gather.7
  158.5 71.0 all-gather.11
  231.6 71.6 all-gather.9
  351.4 87.1 reduce-scatter.3
  476.4 54.3 reduce-scatter.5
  541.9 98.6 reduce-scatter.7

commit v5 on v4

--- a/solution.py
+++ b/solution.py
@@ -1247,6 +1247,19 @@
     return lax.ppermute(values, "seq", [(i, i ^ 1) for i in range(8)])
 
 
+def along_z(values):
+    lines = [[0, 2, 4, 6], [1, 3, 5, 7]]
+    return lax.all_gather(values, "seq", axis=0, tiled=False, axis_index_groups=lines)
+
+
+def both_y(line, other):
+    y = lax.axis_index("seq") % 2
+    row = jnp.zeros((4, 2) + line.shape[1:], line.dtype)
+    for blocks, at in ((line, y), (other, 1 - y)):
+        row = lax.dynamic_update_slice(row, blocks[:, None], (0, at) + (0,) * (line.ndim - 1))
+    return row.reshape((8,) + line.shape[1:])
+
+
 def sum_along_z(values):
     lines = [[0, 2, 4, 6], [1, 3, 5, 7]]
     return lax.psum_scatter(
@@ -1349,7 +1362,6 @@
     across = swap(blocks, 2)
     qkv_pieces = (blocks, swap(blocks, 1), across, swap(across, 1))
     gate_across = swap(w_gate, 2)
-    gate_full = jnp.concatenate([w_gate, swap(w_gate, 1), gate_across, swap(gate_across, 1)], axis=1)
     w_qkv = jnp.concatenate(
         [
             p[:, : 3 * block_rows]
@@ -1360,15 +1372,13 @@
         ],
         axis=0,
     )
-    gain_pair = sum(
-        jnp.sum(p[:, 3 * block_rows : 3 * block_rows + 2].astype(full), axis=0) for p in qkv_pieces
-    )
+    gain_rows = jnp.concatenate([p[:, 3 * block_rows :] for p in qkv_pieces], axis=0)
+    gain_pair = jnp.sum(gain_rows[:, :2].astype(full), axis=0)
     g_query, g_key = (gain_pair[0:1], gain_pair[1:2])
-    g_attn = jnp.concatenate(
-        [p[:, 3 * block_rows + 2, :block_rows].reshape(1, chunk) for p in qkv_pieces], axis=1
-    ).astype(full)
-    x_row, w_qkv, g_query, g_key, g_attn, gate_full = barrier(
-        (x_row, w_qkv, g_query, g_key, g_attn, gate_full)
+    g_attn = gain_rows[:, 2, :block_rows].reshape(1, width).astype(full)
+    gate_pieces = (w_gate, swap(w_gate, 1), gate_across, swap(gate_across, 1))
+    x_row, w_qkv, g_query, g_key, g_attn, gate_pieces = barrier(
+        (x_row, w_qkv, g_query, g_key, g_attn, gate_pieces)
     )
 
     picks = routes.shape[2]
@@ -1378,9 +1388,7 @@
         axis=1,
     )
     extra = jnp.pad(extra, ((0, 0), (0, 128 - extra.shape[1])))
-    out_own = lax.all_gather(
-        jnp.concatenate([reorder(w_out, dp_index, 1), extra], axis=1), "seq", axis=0, tiled=True
-    )
+    out_line = along_z(jnp.concatenate([reorder(w_out, dp_index, 1), extra], axis=1))
     up_across = swap(w_up, 2)
 
     def share(sums):
@@ -1391,10 +1399,17 @@
     q_rot, k_rot, value_in, attended, log_total, r_query, r_key = attend(
         qkv, share(sums), width, g_query, g_key, cosine, sine, seg_col, seg_row
     )
-    attended, out_own, up_across = barrier((attended, out_own, up_across))
+    attended, out_line, up_across = barrier((attended, out_line, up_across))
 
     attended_row = lax.all_gather(attended, "seq", axis=0)
-    out_across = swap(out_own, 2)
+    out_other, line_across = (over_y(out_line), swap(out_line, 2))
+    gate_full = jnp.concatenate(gate_pieces, axis=1)
+    up_full = jnp.concatenate([w_up, swap(w_up, 1), up_across, swap(up_across, 1)], axis=1)
+    out_other, line_across, gate_full = barrier((out_other, line_across, gate_full))
+    other_across = swap(out_other, 2)
+    out_own = both_y(out_line, out_other).reshape(chunk, width + 128)
+    other_across, up_full, out_own = barrier((other_across, up_full, out_own))
+    out_across = both_y(line_across, other_across).reshape(chunk, width + 128)
     out_pieces = (out_own, swap(out_own, 1), out_across, swap(out_across, 1))
     extras = [p[:, width:] for p in out_pieces]
     routes_row = extras[0][:, : packed * picks].reshape(rows, picks).astype(jnp.int32)
@@ -1406,7 +1421,6 @@
     own = (
         lane_ids[None, :] == seq_index * held + lax.iota(jnp.int32, held)[:, None]
     ).astype(full)
-    up_full = jnp.concatenate([w_up, swap(w_up, 1), up_across, swap(up_across, 1)], axis=1)
     attended_row, out_pieces, up_full, router, g_ffn, chosen = barrier(
         (attended_row, out_pieces, up_full, router, g_ffn, chosen)
     )

time: 660 us -> 650 us (0.985)
  waiting for transfers between devices: 177 us -> 127 us
  blocking collectives: 37.1 us -> 81.3 us
    all_to_all x0 -> x1, blocking collectives: none -> 44.7 us  [on_device_heads(): lax.all_to_all(jnp.concatenate([blocks, gain_rows], axis=1), 'seq', 0, 0,...]
    ppermute x36 -> x37, waiting for transfers between devices: 98.6 us -> 59.8 us  [swap(): return lax.ppermute(values, 'dp', [(i, i ^ bits) for i in range(4)])]
    all_to_all x1 -> x0, waiting for transfers between devices: 36.9 us -> none  [on_device_heads(): lax.all_to_all(jnp.concatenate([blocks, gain_rows], axis=1), 'seq', 0, 0,...]
    ppermute x1 -> x2, waiting for transfers between devices: 0.7 us -> 21.6 us  [over_y(): return lax.ppermute(values, 'seq', [(i, i ^ 1) for i in range(8)])]
    all_to_all x1 -> x0, starting transfers between devices: 7.48 us -> none  [on_device_heads(): lax.all_to_all(jnp.concatenate([blocks, gain_rows], axis=1), 'seq', 0, 0,...]
    ppermute x36 -> x37, starting transfers between devices: 19.9 us -> 23.6 us  [swap(): return lax.ppermute(values, 'dp', [(i, i ^ bits) for i in range(4)])]
    unnamed x119 -> x125, local copies, waits for them, and re-layouts: 16.6 us -> 16.6 us
  transfers between devices with their start and end apart: 50 -> 51, of which waited for: 18 -> 18; matrix products, arithmetic and copies ran while one was open for 20% -> 20% of each run, Pallas kernels for 35% -> 36%
where the time goes in v5:
time: 650 us; the launch traced here: 642 us
  Pallas kernels  228 us (35%)
  waiting for transfers between devices  127 us (20%)
  other arithmetic  85.2 us (13%)
  blocking collectives  81.3 us (13%)
  local copies, waits for them, and re-layouts  58.1 us (9%)
  starting transfers between devices  44.6 us (7%)
  between operations  15.7 us (2%)
    pallas_call x10, Pallas kernels, grid_call(): pl.pallas_call(body, grid=grid, in_specs=in_specs, out_specs=out_specs, o...  165 us
    ppermute x37, waiting for transfers between devices, swap(): return lax.ppermute(values, 'dp', [(i, i ^ bits) for i in range(4)])  59.8 us
    all_to_all x1, blocking collectives, on_device_heads(): lax.all_to_all(jnp.concatenate([blocks, gain_rows], axis=1), 'seq', 0, 0,...  44.7 us
    ppermute x37, starting transfers between devices, swap(): return lax.ppermute(values, 'dp', [(i, i ^ bits) for i in range(4)])  23.6 us
    ppermute x2, waiting for transfers between devices, over_y(): return lax.ppermute(values, 'seq', [(i, i ^ 1) for i in range(8)])  21.6 us
    pallas_call x1, Pallas kernels, finish_attention(): pl.pallas_call(body, grid_spec=pltpu.PrefetchScalarGridSpec(num_scalar_pr...  19.1 us
    all_to_all x1, blocking collectives, share(): return lax.all_to_all(spread, 'seq', 0, 0, tiled=True)  18.6 us
    all_to_all x1, blocking collectives, to_columns(): return lax.all_to_all(values, 'seq', 0, 0, tiled=True).reshape(rows, cols)  18 us
  transfers between devices with their start and end apart: 51, of which 18 were waited for; matrix products, arithmetic and copies ran while one was open for 20% of the time, Pallas kernels for 36%

profile of v5, /device:TPU:0, one launch (start us, length us, event | category | flops | bytes accessed | tf_op | source)
XLA Modules:
  0.0 641.7 jit_solution(6490943734619437216)
XLA Ops:
  15.1 44.7 %all_to_all.40 = bf16[8,208,256]{2,1,0:T(8,128)(2,1)S(1)} all-to-all(bf16[8,208,256]{2,1,0:T(8,128)(2,1)S(1)} %pad_maximum_fusion.6), channel_id=1, replica_groups=mesh['dp'=4,'seq'=8] {'seq'}, dimensions={0} | all-to-all | bytes 1703936 | tf_op jit(solution)/shard_map/all_to_all | solution.py:1361
  63.2 18.6 %collective-permute-done.1 = bf16[8,208,256]{2,1,0:T(8,128)(2,1)} collective-permute-done((bf16[8,208,256]{2,1,0:T(8,128)(2,1)S(1)}, bf16[8,208,256]{2,1,0:T(8,128)(2,1)}, u32[]{:S(2)}, u32[]{:S(2)}) %collective-permute-start.1) | collective-permute-done | bytes 852000 | tf_op jit(solution)/shard_map/ppermute | solution.py:1271
  102.4 9.3 %shard_map.263 = (bf16[1024,2048]{1,0:T(8,128)(2,1)}, f32[1024,768]{1,0:T(8,128)}, f32[1024,1]{1,0:T(8,128)}, f32[8,1024]{1,0:T(8,128)}) custom-call(bf16[1024,2048]{1,0:T(8,128)(2,1)} %all-gather.7.cloned.1.call-done.x_ref.x, f32[1,2048]{1,0:T(1,128)} %reshape.224.gain_ref, bf16[2048,768]{1,0:T(8,128)(2,1)} %pad_maximum_fusion.5.w_ref.w), custom_call_target="tpu_custom_call" | custom-call | flops 805306368 | bytes 3681280 | tf_op jit(solution)/shard_map/pallas_call | solution.py:518
  120.1 13.5 %all-to-all-done.1.sums_ref = f32[8,8,1024]{2,1,0:T(8,128)S(1)} async-done(((f32[8,8,1024]{2,1,0:T(8,128)}), f32[8,8,1024]{2,1,0:T(8,128)S(1)}, u32[]{:S(2)}, u32[]{:S(2)}) %all-to-all-start.1) | async-done | bytes 262176 | tf_op jit(solution)/shard_map/all_to_all | solution.py:1396
  134.4 10.9 %shard_map.264 = (bf16[1024,256]{1,0:T(8,128)(2,1)}, bf16[1024,256]{1,0:T(8,128)(2,1)}, bf16[1024,256]{1,0:T(8,128)(2,1)}, bf16[1024,256]{1,0:T(8,128)(2,1)}, f3...) custom-call(f32[1024,768]{1,0:T(8,128)} %get-tuple-element.155.q.k.v, ...), custom_call_target="tpu_custom_call" | custom-call | flops 268435456 | bytes 3217920 | tf_op jit(solution)/shard_map/pallas_call | solution.py:518
  148.2 7.2 %pad_maximum_fusion.gate_ref = bf16[2,2048,1024]{2,1,0:T(8,128)(2,1)} fusion(bf16[2,512,1024]{2,1,0:T(8,128)(2,1)} %collective-permute-done.5, bf16[2,512,1024]{2,1,0:T(8,128)(2,1)} %collective-permute-done.4, bf16[2,512,1024]{2,1,0:T(8,128)(2,1)} %collective-permute-done.3, bf16[2,512,1024]{2,1,0:T(8,128)(2,1)} %param.28), kind=kLoop, calls=%fused_computation | loop fusion | flops 33554432 | bytes 16777216 | tf_op jit(solution)/shard_map/concatenate | solution.py:1406
  156.7 21.6 %collective-permute-done.7 = bf16[4,64,2176]{2,1,0:T(8,128)(2,1)S(1)} collective-permute-done((bf16[4,64,2176]{2,1,0:T(8,128)(2,1)}, bf16[4,64,2176]{2,1,0:T(8,128)(2,1)S(1)}, u32[]{:S(2)}, u32[]{:S(2)}) %collective-permute-start.7) | collective-permute-done | bytes 1114144 | tf_op jit(solution)/shard_map/ppermute | solution.py:1247
  189.4 15.0 %collective-permute-done.9 = bf16[4,64,2176]{2,1,0:T(8,128)(2,1)S(1)} collective-permute-done((bf16[4,64,2176]{2,1,0:T(8,128)(2,1)S(1)}, bf16[4,64,2176]{2,1,0:T(8,128)(2,1)S(1)}, u32[]{:S(2)}, u32[]{:S(2)}) %collective-permute-start.9) | collective-permute-done | bytes 1114144 | tf_op jit(solution)/shard_map/ppermute | solution.py:1271
  223.5 19.1 %shard_map.265 = (f32[1024,2048]{1,0:T(8,128)}, bf16[1024,2048]{1,0:T(8,128)(2,1)}, f32[1024,1]{1,0:T(8,128)}, f32[1024,128]{1,0:T(8,128)}, f32[2,1024,1]{2,1,0:T(8,128)}) custom-call(s32[5]{0:T(128)} %stack.78.order_ref, bf16[8,1024,256]{2,1,0:T(8,128)(2,1)} %bitcast.197, bf16[512,2176]{1,0:T(8,128)(2,1)} %bitcast.195, ...), custom_call_target="tpu_custom_call" | custom-call | flops 2147483648 | bytes 6556672 | tf_op jit(solution)/shard_map/pallas_call | solution.py:587
  242.6 25.0 %shard_map.266 = (bf16[2,1024,1024]{2,1,0:T(8,128)(2,1)}, bf16[2,1024,1024]{2,1,0:T(8,128)(2,1)}, bf16[2,1024,1024]{2,1,0:T(8,128)(2,1)}) custom-call(bf16[1024,2048]{1,0:T(8,128)(2,1)} %get-tuple-element.185.x_ref.flat_ref, bf16[2,2048,1024]{2,1,0:T(8,128)(2,1)} %pad_maximum_fusion.gate_ref, bf16[2,2048,1024]{2,1,0:T(8,128)(2,1)} %pad_maximum_fusion.1.up_ref), custom_call_target="tpu_custom_call" | custom-call | flops 4294967296 | bytes 8388608 | tf_op jit(solution)/shard_map/pallas_call | solution.py:518
  276.5 14.6 %shard_map.267 = (bf16[512,2048]{1,0:T(8,128)(2,1)}, bf16[512,2048]{1,0:T(8,128)(2,1)}) custom-call(s32[1]{0:T(128)} %bitcast.44.y_ref, bf16[2,1024,1024]{2,1,0:T(8,128)(2,1)} %get-tuple-element.194.act_ref, bf16[2,1024,2048]{2,1,0:T(8,128)(2,1)} %constant_dynamic-update-slice_fusion.1.down_ref, f32[2,1024,1]{2,1,0:T(8,128)} %get-tuple-element.191.weight_ref), custom_call_target="tpu_custom_call" | custom-call | flops 2147483648 | bytes 4194304 | tf_op jit(solution)/shard_map/pallas_call | solution.py:795
  294.4 20.3 %shard_map.268 = (bf16[2,1024,1024]{2,1,0:T(8,128)(2,1)}, bf16[2,1024,1024]{2,1,0:T(8,128)(2,1)}, bf16[2,1024,1024]{2,1,0:T(8,128)(2,1)}, f32[2,1024,128]{2,1,0:T(8,128)}) custom-call(bf16[1024,2048]{1,0:T(8,128)(2,1)} %all-gather.9.cloned.1.call-done.dy_ref.flat_ref, bf16[2,1024,2048]{2,1,0:T(8,128)(2,1)} %constant_dynamic-update-slice_fusion.1.down_ref, ...), custom_call_target="tpu_custom_call" | custom-call | flops 2147483648 | bytes 9701376 | tf_op jit(solution)/shard_map/pallas_call | solution.py:518
  314.7 26.4 %shard_map.269 = (bf16[1024,2048]{1,0:T(8,128)(2,1)}, bf16[1024,128]{1,0:T(8,128)(2,1)}) custom-call(bf16[2,1024,1024]{2,1,0:T(8,128)(2,1)} %get-tuple-element.197.dgate_ref.stacked_ref, bf16[2,1024,1024]{2,1,0:T(8,128)(2,1)} %get-tuple-element.212.dup_ref.stacked_ref, bf16[2,2048,1024]{2,1,0:T(8,128)(2,1)} %pad_maximum_fusion.gate_ref, ...), custom_call_target="tpu_custom_call" | custom-call | flops 4294967296 | bytes 8061184 | tf_op jit(solution)/shard_map/pallas_call | solution.py:518
  341.6 18.6 %shard_map.270 = (bf16[2,1024,512]{2,1,0:T(8,128)(2,1)}, bf16[2,1024,512]{2,1,0:T(8,128)(2,1)}, bf16[2,1024,512]{2,1,0:T(8,128)(2,1)}, bf16[2,1024,512]{2,1,0:T(8,128)(2,1)}) custom-call(bf16[1024,2048]{1,0:T(8,128)(2,1)} %all-gather.9.cloned.1.call-done.dy_ref.flat_ref, bf16[2,1024,1024]{2,1,0:T(8,128)(2,1)} %get-tuple-element.206.stacked_ref), custom_call_target="tpu_custom_call" | custom-call | flops 2147483648 | bytes 4194304 | tf_op jit(solution)/shard_map/pallas_call | solution.py:518
  360.2 17.9 %shard_map.271 = (bf16[2,512,1024]{2,1,0:T(8,128)(2,1)}, bf16[2,512,1024]{2,1,0:T(8,128)(2,1)}, bf16[2,512,1024]{2,1,0:T(8,128)(2,1)}, bf16[2,512,1024]{2,1,0:T(8,128)(2,1)}) custom-call(bf16[1024,2048]{1,0:T(8,128)(2,1)} %get-tuple-element.185.x_ref.flat_ref, bf16[2,1024,1024]{2,1,0:T(8,128)(2,1)} %get-tuple-element.197.dgate_ref.stacked_ref), custom_call_target="tpu_custom_call" | custom-call | flops 2147483648 | bytes 4194304 | tf_op jit(solution)/shard_map/pallas_call | solution.py:518
  381.8 18.0 %shard_map.272 = (bf16[2,512,1024]{2,1,0:T(8,128)(2,1)}, bf16[2,512,1024]{2,1,0:T(8,128)(2,1)}, bf16[2,512,1024]{2,1,0:T(8,128)(2,1)}, bf16[2,512,1024]{2,1,0:T(8,128)(2,1)}) custom-call(bf16[1024,2048]{1,0:T(8,128)(2,1)} %get-tuple-element.185.x_ref.flat_ref, bf16[2,1024,1024]{2,1,0:T(8,128)(2,1)} %get-tuple-element.212.dup_ref.stacked_ref), custom_call_target="tpu_custom_call" | custom-call | flops 2147483648 | bytes 4194304 | tf_op jit(solution)/shard_map/pallas_call | solution.py:518
  437.2 8.7 %shard_map.273 = (f32[128,2048]{1,0:T(8,128)}, bf16[128,2048]{1,0:T(8,128)(2,1)}, bf16[4,128,512]{2,1,0:T(8,128)(2,1)}, f32[1,2048]{1,0:T(1,128)}) custom-call(s32[5]{0:T(128)} %stack.78.order_ref, bf16[128,2048]{1,0:T(8,128)(2,1)} %reduce-scatter.4.cloned.1.call-done.nf, f32[1024,2048]{1,0:T(8,128)} %get-tuple-element.227.mid_ref, ...), custom_call_target="tpu_custom_call" | custom-call | flops 268435456 | bytes 2754560 | tf_op jit(solution)/shard_map/pallas_call | solution.py:1190
  447.0 18.0 %all_to_all.41 = bf16[8,128,256]{2,1,0:T(8,128)(2,1)} all-to-all(bf16[8,128,256]{2,1,0:T(8,128)(2,1)S(1)} %bitcast.217), channel_id=1, replica_groups=mesh['dp'=4,'seq'=8] {'seq'}, dimensions={0} | all-to-all | bytes 1048576 | tf_op jit(solution)/shard_map/all_to_all | solution.py:1470
  475.4 12.8 %shard_map.274 = (f32[1024,256]{1,0:T(8,128)}, f32[1024,256]{1,0:T(8,128)}, bf16[1024,256]{1,0:T(8,128)(2,1)}, f32[8,1024]{1,0:T(8,128)}, f32[1,256]{1,0:T(1,128)}, /*index=5*/f32[1,256]{1,0:T(1,128)}) custom-call(f32[1024,768]{1,0:T(8,128)} %get-tuple-element.155.q.k.v, f32[1024,768]{1,0:T(8,128)} %get-tuple-element.155.q.k.v, ...), custom_call_target="tpu_custom_call" | custom-call | flops 671088640 | bytes 3030016 | tf_op jit(solution)/shard_map/pallas_call | solution.py:1073
  492.5 9.2 %all-to-all-done.4 = bf16[8,128,256]{2,1,0:T(8,128)(2,1)S(1)} async-done(((bf16[8,128,256]{2,1,0:T(8,128)(2,1)}), bf16[8,128,256]{2,1,0:T(8,128)(2,1)S(1)}, u32[]{:S(2)}, u32[]{:S(2)}) %all-to-all-start.4) | async-done | bytes 524320 | tf_op jit(solution)/shard_map/all_to_all | solution.py:1470
  502.5 18.6 %all_to_all.42.sums_ref = f32[8,8,1024]{2,1,0:T(8,128)} all-to-all(f32[8,8,1024]{2,1,0:T(8,128)S(1)} %broadcast_in_dim.70), channel_id=1, replica_groups=mesh['dp'=4,'seq'=8] {'seq'}, dimensions={0} | all-to-all | bytes 524288 | tf_op jit(solution)/shard_map/all_to_all | solution.py:1396
  521.1 10.4 %shard_map.275 = (bf16[1024,768]{1,0:T(8,128)(2,1)}, bf16[1024,2048]{1,0:T(8,128)(2,1)}, f32[1,2048]{1,0:T(1,128)}) custom-call(f32[1024,256]{1,0:T(8,128)} %get-tuple-element.236.qg, f32[1024,256]{1,0:T(8,128)} %get-tuple-element.237.kg, bf16[1024,256]{1,0:T(8,128)(2,1)} %get-tuple-element.238.v, f32[1024,768]{1,0:T(8,128)} %get-tuple-element.155.q.k.v, ...), custom_call_target="tpu_custom_call" | custom-call | flops 805306368 | bytes 5575680 | tf_op jit(solution)/shard_map/pallas_call | solution.py:518
  532.7 7.9 %shard_map.276 = (bf16[1,512,768]{2,1,0:T(8,128)(2,1)}, bf16[1,512,768]{2,1,0:T(8,128)(2,1)}, bf16[1,512,768]{2,1,0:T(8,128)(2,1)}, bf16[1,512,768]{2,1,0:T(8,128)(2,1)}) custom-call(bf16[1024,2048]{1,0:T(8,128)(2,1)} %get-tuple-element.256.flat_ref, bf16[1,1024,768]{2,1,0:T(8,128)(2,1)} %bitcast.221), custom_call_target="tpu_custom_call" | custom-call | flops 805306368 | bytes 2228224 | tf_op jit(solution)/shard_map/pallas_call | solution.py:518
  541.3 8.2 %shard_map.277 = (bf16[512,256]{1,0:T(8,128)(2,1)}, bf16[512,256]{1,0:T(8,128)(2,1)}, bf16[512,256]{1,0:T(8,128)(2,1)}, bf16[512,256]{1,0:T(8,128)(2,1)}) custom-call(s32[5]{0:T(128)} %stack.78.order_ref, bf16[8,1024,256]{2,1,0:T(8,128)(2,1)} %bitcast.198, bf16[1024,256]{1,0:T(8,128)(2,1)} %bitcast.214), custom_call_target="tpu_custom_call" | custom-call | flops 268435456 | bytes 1441792 | tf_op jit(solution)/shard_map/pallas_call | solution.py:1229
  (353 shorter events, 231.4 us)
Async XLA Ops:
  7.2 95.2 %all-gather.7.cloned.1.call-start = ((), (), s32[]{:S(2)}) async-start(), calls=%async_computation.11 | async-start | bytes 4718592 | tf_op jit(solution)/shard_map/all_gather | solution.py:1346
  11.1 134.3 %all-gather.11.cloned.1.call-start = ((), (), s32[]{:S(2)}) async-start(), calls=%async_computation.16 | async-start | bytes 1392640 | tf_op jit(solution)/shard_map/all_gather | solution.py:1252
  11.1 49.8 %collective-permute-start.4 = (bf16[2,512,1024]{2,1,0:T(8,128)(2,1)}, bf16[2,512,1024]{2,1,0:T(8,128)(2,1)}, u32[]{:S(2)}, u32[]{:S(2)}) collective-permute-start(bf16[2,512,1024]{2,1,0:T(8,128)(2,1)} %param.28), channel_id=1, source_target_pairs={{0,16},{8,24},{16,0},{24,8},{1,17},{9,25},{17,1},{25,9},{2,18},{10... | collective-permute-start | bytes 6291464 | tf_op jit(solution)/shard_map/ppermute | solution.py:1271
  60.3 37.2 %collective-permute-start.3 = (bf16[2,512,1024]{2,1,0:T(8,128)(2,1)}, bf16[2,512,1024]{2,1,0:T(8,128)(2,1)}, u32[]{:S(2)}, u32[]{:S(2)}) collective-permute-start(bf16[2,512,1024]{2,1,0:T(8,128)(2,1)} %param.28), channel_id=1, source_target_pairs={{0,8},{8,0},{16,24},{24,16},{1,9},{9,1},{17,25},{25,17},{2,10},{10... | collective-permute-start | bytes 6291464 | tf_op jit(solution)/shard_map/ppermute | solution.py:1271
  60.9 36.5 %collective-permute-start.5 = (bf16[2,512,1024]{2,1,0:T(8,128)(2,1)}, bf16[2,512,1024]{2,1,0:T(8,128)(2,1)}, u32[]{:S(2)}, u32[]{:S(2)}) collective-permute-start(bf16[2,512,1024]{2,1,0:T(8,128)(2,1)} %collective-permute-done.4), channel_id=1, source_target_pairs={{0,8},{8,0},{16,24},{24,16},{1,9},{9,1},{17,25},{25,17},{2,10},{10... | collective-permute-start | bytes 6291464 | tf_op jit(solution)/shard_map/ppermute | solution.py:1271
  60.9 84.4 %collective-permute-start.6 = (bf16[2,512,1024]{2,1,0:T(8,128)(2,1)}, bf16[2,512,1024]{2,1,0:T(8,128)(2,1)}, u32[]{:S(2)}, u32[]{:S(2)}) collective-permute-start(bf16[2,512,1024]{2,1,0:T(8,128)(2,1)} %param.29), channel_id=1, source_target_pairs={{0,16},{8,24},{16,0},{24,8},{1,17},{9,25},{17,1},{25,9},{2,18},{10... | collective-permute-start | bytes 6291464 | tf_op jit(solution)/shard_map/ppermute | solution.py:1271
  116.6 103.8 %all-gather.13.cloned.1.call-start = ((), (), s32[]{:S(2)}) async-start(), calls=%async_computation.17 | async-start | bytes 4718592 | tf_op jit(solution)/shard_map/all_gather | solution.py:1404
  145.4 148.5 %all-gather.9.cloned.1.call-start = ((), (), s32[]{:S(2)}) async-start(), calls=%async_computation.12 | async-start | bytes 4718592 | tf_op jit(solution)/shard_map/all_gather | solution.py:1429
  145.4 37.5 %collective-permute-start.10 = (bf16[2,512,1024]{2,1,0:T(8,128)(2,1)}, bf16[2,512,1024]{2,1,0:T(8,128)(2,1)}, u32[]{:S(2)}, u32[]{:S(2)}) collective-permute-start(bf16[2,512,1024]{2,1,0:T(8,128)(2,1)} %param.29), channel_id=1, source_target_pairs={{0,8},{8,0},{16,24},{24,16},{1,9},{9,1},{17,25},{25,17},{2,10},{10... | collective-permute-start | bytes 6291464 | tf_op jit(solution)/shard_map/ppermute | solution.py:1271
  145.5 32.8 %collective-permute-start.7 = (bf16[4,64,2176]{2,1,0:T(8,128)(2,1)}, bf16[4,64,2176]{2,1,0:T(8,128)(2,1)S(1)}, u32[]{:S(2)}, u32[]{:S(2)}) collective-permute-start(bf16[4,64,2176]{2,1,0:T(8,128)(2,1)} %bitcast.222), channel_id=1, source_target_pairs={{0,1},{1,0},{2,3},{3,2},{4,5},{5,4},{6,7},{7,6},{8,9},{9,8},{10,11... | collective-permute-start | bytes 3342344 | tf_op jit(solution)/shard_map/ppermute | solution.py:1247
  146.7 31.6 %collective-permute-start.8 = (bf16[4,64,2176]{2,1,0:T(8,128)(2,1)}, bf16[4,64,2176]{2,1,0:T(8,128)(2,1)S(1)}, u32[]{:S(2)}, u32[]{:S(2)}) collective-permute-start(bf16[4,64,2176]{2,1,0:T(8,128)(2,1)} %bitcast.223), channel_id=1, source_target_pairs={{0,16},{8,24},{16,0},{24,8},{1,17},{9,25},{17,1},{25,9},{2,18},{10... | collective-permute-start | bytes 3342344 | tf_op jit(solution)/shard_map/ppermute | solution.py:1271
  155.4 27.5 %collective-permute-start.11 = (bf16[2,512,1024]{2,1,0:T(8,128)(2,1)}, bf16[2,512,1024]{2,1,0:T(8,128)(2,1)S(1)}, u32[]{:S(2)}, u32[]{:S(2)}) collective-permute-start(bf16[2,512,1024]{2,1,0:T(8,128)(2,1)} %collective-permute-done.6), channel_id=1, source_target_pairs={{0,8},{8,0},{16,24},{24,16},{1,9},{9,1},{17,25},{25,17},{2,10},{10... | collective-permute-start | bytes 6291464 | tf_op jit(solution)/shard_map/ppermute | solution.py:1271
  220.5 212.5 %reduce-scatter.4.cloned.1.call-start = ((), (), s32[]{:S(2)}) async-start(), calls=%async_computation.13 | async-start | bytes 4718592 | tf_op jit(solution)/shard_map/reduce_scatter | solution.py:1449
  220.7 47.8 %collective-permute-start.14 = (bf16[2,1024,512]{2,1,0:T(8,128)(2,1)}, bf16[2,1024,512]{2,1,0:T(8,128)(2,1)S(1)}, u32[]{:S(2)}, u32[]{:S(2)}) collective-permute-start(bf16[2,1024,512]{2,1,0:T(8,128)(2,1)} %param.30), channel_id=1, source_target_pairs={{0,16},{8,24},{16,0},{24,8},{1,17},{9,25},{17,1},{25,9},{2,18},{10... | collective-permute-start | bytes 6291464 | tf_op jit(solution)/shard_map/ppermute | solution.py:1271
  222.3 47.9 %collective-permute-start.15 = (bf16[2,1024,512]{2,1,0:T(8,128)(2,1)}, bf16[2,1024,512]{2,1,0:T(8,128)(2,1)}, u32[]{:S(2)}, u32[]{:S(2)}) collective-permute-start(bf16[2,1024,512]{2,1,0:T(8,128)(2,1)} %param.30), channel_id=1, source_target_pairs={{0,8},{8,0},{16,24},{24,16},{1,9},{9,1},{17,25},{25,17},{2,10},{10... | collective-permute-start | bytes 6291464 | tf_op jit(solution)/shard_map/ppermute | solution.py:1271
  293.9 47.2 %collective-permute-start.17 = (bf16[512,2048]{1,0:T(8,128)(2,1)}, bf16[512,2048]{1,0:T(8,128)(2,1)S(1)}, u32[]{:S(2)}, u32[]{:S(2)}) collective-permute-start(bf16[512,2048]{1,0:T(8,128)(2,1)} %get-tuple-element.202), channel_id=1, source_target_pairs={{0,1},{1,0},{2,3},{3,2},{4,5},{5,4},{6,7},{7,6},{8,9},{9,8},{10,11... | collective-permute-start | bytes 6291464 | tf_op jit(solution)/shard_map/ppermute | solution.py:1247
  341.2 190.4 %reduce-scatter.6.cloned.1.call-start = ((), (), s32[]{:S(2)}) async-start(), calls=%async_computation.14 | async-start | bytes 2621440 | tf_op jit(solution)/shard_map/reduce_scatter | solution.py:1265
  378.1 30.7 %collective-permute-start.24 = (bf16[2,512,1024]{2,1,0:T(8,128)(2,1)}, bf16[2,512,1024]{2,1,0:T(8,128)(2,1)}, u32[]{:S(2)}, u32[]{:S(2)}) collective-permute-start(bf16[2,512,1024]{2,1,0:T(8,128)(2,1)} %get-tuple-element.223), channel_id=1, source_target_pairs={{0,8},{8,0},{16,24},{24,16},{1,9},{9,1},{17,25},{25,17},{2,10},{10... | collective-permute-start | bytes 6291464 | tf_op jit(solution)/shard_map/ppermute | solution.py:1271
  378.3 34.7 %collective-permute-start.23 = (bf16[2,1024,512]{2,1,0:T(8,128)(2,1)}, bf16[2,1024,512]{2,1,0:T(8,128)(2,1)}, u32[]{:S(2)}, u32[]{:S(2)}) collective-permute-start(bf16[2,1024,512]{2,1,0:T(8,128)(2,1)} %get-tuple-element.221), channel_id=1, source_target_pairs={{0,8},{8,0},{16,24},{24,16},{1,9},{9,1},{17,25},{25,17},{2,10},{10... | collective-permute-start | bytes 6291464 | tf_op jit(solution)/shard_map/ppermute | solution.py:1271
  381.8 37.0 %collective-permute-start.20 = (bf16[2,512,1024]{2,1,0:T(8,128)(2,1)}, bf16[2,512,1024]{2,1,0:T(8,128)(2,1)}, u32[]{:S(2)}, u32[]{:S(2)}) collective-permute-start(bf16[2,512,1024]{2,1,0:T(8,128)(2,1)} %get-tuple-element.211), channel_id=1, source_target_pairs={{0,8},{8,0},{16,24},{24,16},{1,9},{9,1},{17,25},{25,17},{2,10},{10... | collective-permute-start | bytes 6291464 | tf_op jit(solution)/shard_map/ppermute | solution.py:1271
  435.7 29.3 %collective-permute-start.26 = (bf16[512,1024]{1,0:T(8,128)(2,1)S(1)}, bf16[512,1024]{1,0:T(8,128)(2,1)S(1)}, u32[]{:S(2)}, u32[]{:S(2)}) collective-permute-start(bf16[512,1024]{1,0:T(8,128)(2,1)S(1)} %get-tuple-element.304), channel_id=1, source_target_pairs={{0,16},{8,24},{16,0},{24,8},{1,17},{9,25},{17,1},{25,9},{2,18},{10... | collective-permute-start | bytes 3145736 | tf_op jit(solution)/shard_map/ppermute | solution.py:1271
  468.7 33.1 %all-to-all-start.4 = ((bf16[8,128,256]{2,1,0:T(8,128)(2,1)}), bf16[8,128,256]{2,1,0:T(8,128)(2,1)S(1)}, u32[]{:S(2)}, u32[]{:S(2)}) async-start(bf16[8,128,256]{2,1,0:T(8,128)(2,1)} %bitcast.187), calls=%async_computation.5 | async-start | bytes 1048576 | tf_op jit(solution)/shard_map/all_to_all | solution.py:1470
  472.3 158.1 %reduce-scatter.8.cloned.1.call-start = ((), (), s32[]{:S(2)}) async-start(), calls=%async_computation.15 | async-start | bytes 4718592 | tf_op jit(solution)/shard_map/reduce_scatter | solution.py:1489
  473.9 57.6 %collective-permute-start.28 = (bf16[512,1024]{1,0:T(8,128)(2,1)}, bf16[512,1024]{1,0:T(8,128)(2,1)S(1)}, u32[]{:S(2)}, u32[]{:S(2)}) collective-permute-start(bf16[512,1024]{1,0:T(8,128)(2,1)} %get-tuple-element.298), channel_id=1, source_target_pairs={{0,16},{8,24},{16,0},{24,8},{1,17},{9,25},{17,1},{25,9},{2,18},{10... | collective-permute-start | bytes 3145736 | tf_op jit(solution)/shard_map/ppermute | solution.py:1271
  (81 other events, 1175.3 us)
Sparse Core Ops, SparseCore 0:
  11.2 91.1 all-gather.6
  104.5 33.4 all-gather.10
  145.5 74.6 all-gather.12
  222.2 71.6 all-gather.8
  341.3 87.2 reduce-scatter.3
  466.2 54.4 reduce-scatter.5
  531.7 98.6 reduce-scatter.7

commit v6 on v5

--- a/solution.py
+++ b/solution.py
@@ -661,7 +661,7 @@
     def body(dy_ref, down_ref, act_ref, a_ref, b_ref, weight_ref, out_ref, dgate_ref, dup_ref, sum_ref):
         first = pl.program_id(1) == 0
 
-        @pl.loop(0, rows // tm)
+        @pl.loop(0, rows // tm, unroll=True)
         def _(i):
             at = pl.ds(pl.multiple_of(i * tm, tm), tm)
             grad = mm(dy_ref[at, :], down_ref[0], ((1,), (1,)))
@@ -717,7 +717,7 @@
     tile, tm = (math.gcd(width, 512), row_tiles(rows))
 
     def body(dgate_ref, dup_ref, gate_ref, up_ref, sum_ref, chance_ref, chosen_ref, own_ref, router_ref, out_ref, logits_ref):
-        @pl.loop(0, rows // tm)
+        @pl.loop(0, rows // tm, unroll=True)
         def _(i):
             at = pl.ds(pl.multiple_of(i * tm, tm), tm)
             chances = chance_ref[at, :]
@@ -877,9 +877,11 @@
 
 
 def pair_columns(sums):
-    total = sum(sums[1:], sums[0])
-    total = jnp.concatenate([total] * 16, axis=0).T
-    return (total[:, 0:1], total[:, 1:2])
+    rows = [sum((s[i : i + 1] for s in sums[1:]), sums[0][i : i + 1]) for i in range(2)]
+    wide = (128, rows[0].shape[1])
+    first = lax.broadcasted_iota(jnp.int32, wide, 0) == 0
+    both = jnp.where(first, jnp.broadcast_to(rows[0], wide), jnp.broadcast_to(rows[1], wide)).T
+    return (both[:, 0:1], both[:, 1:2])
 
 
 def project(x_row, gain, w_qkv):
@@ -983,7 +985,7 @@
             col(0),
             col(heads),
             col(2 * heads),
-            pl.BlockSpec((shards, 8, rows), lambda h: (0, 0, 0)),
+            pl.BlockSpec((shards, 2, rows), lambda h: (0, 0, 0)),
             row,
             row,
             table,
@@ -1124,7 +1126,7 @@
             tiled(cols),
             tiled(cols),
             tiled(cols, 1),
-            pl.BlockSpec((shards, 8, tm), lambda i: (0, 0, i)),
+            pl.BlockSpec((shards, 2, tm), lambda i: (0, 0, i)),
             tiled(1),
             tiled(1),
             pl.BlockSpec((width, 3 * cols), lambda i: (0, 0)),
@@ -1277,8 +1279,19 @@
     return (kept.astype(sent), (pieces[2].astype(wide) + swap(pieces[3], 1).astype(wide)).astype(sent))
 
 
+def sum_experts_in_chip(pieces):
+    wide, low = (jnp.float32, jnp.bfloat16)
+    arrived = swap(pieces[3], 1)
+    kept = pieces[0].astype(wide) + swap(pieces[1], 1).astype(wide)
+    passed = [
+        (pieces[2][e].astype(wide) + arrived[e].astype(wide)).astype(low)
+        for e in range(arrived.shape[0])
+    ]
+    return (kept.astype(low), passed)
+
+
 def across_by_expert(passed):
-    return [swap(passed[e], 2) for e in range(passed.shape[0])]
+    return [swap(p, 2) for p in passed]
 
 
 def add_arrived(kept, arrived):
@@ -1392,7 +1405,7 @@
     up_across = swap(w_up, 2)
 
     def share(sums):
-        spread = jnp.broadcast_to(sums[None], (shards,) + sums.shape)
+        spread = jnp.broadcast_to(sums[None, :2], (shards, 2, rows))
         return lax.all_to_all(spread, "seq", 0, 0, tiled=True)
 
     normed, qkv, r_attn, sums = project(x_row, g_attn, w_qkv)
@@ -1449,17 +1462,16 @@
     nf_sum = lax.psum_scatter(nf_grad, "seq", scatter_dimension=0, tiled=True)
     mixture = (mixture.astype(full) + mixture_far.astype(full)).astype(low)
 
-    down_kept, down_passed = sum_in_chip(weight_pieces(scaled, dy_row, 4, False), low)
+    down_kept, down_passed = sum_experts_in_chip(weight_pieces(scaled, dy_row, 4, False))
     gate_pieces = weight_pieces(normed_ffn, dgate, 4, True)
     dup, down_passed = barrier((dup, down_passed))
     down_arrived = across_by_expert(down_passed)
-    gate_kept, gate_passed = sum_in_chip(gate_pieces, low)
+    gate_kept, gate_passed = sum_experts_in_chip(gate_pieces)
     up_pieces = weight_pieces(normed_ffn, dup, 4, True)
-    up_pieces, down_arrived[0] = barrier((up_pieces, down_arrived[0]))
-    up_kept, up_passed = sum_in_chip(up_pieces, low)
+    up_kept, up_passed = sum_experts_in_chip(up_pieces)
     router_grad = mm(grad_logits[:, :expert_count], normed_ffn, ((0,), (0,)))
-    nf_sum, mixture, down_arrived[1], gate_passed, up_passed, router_grad, down_kept, gate_kept, up_kept = barrier(
-        (nf_sum, mixture, down_arrived[1], gate_passed, up_passed, router_grad, down_kept, gate_kept, up_kept)
+    nf_sum, mixture, down_arrived[0], gate_passed, up_passed, router_grad, down_kept, gate_kept, up_kept = barrier(
+        (nf_sum, mixture, down_arrived[0], gate_passed, up_passed, router_grad, down_kept, gate_kept, up_kept)
     )
     gate_arrived, up_arrived = (across_by_expert(gate_passed), [swap(up_passed[0], 2)])
 
@@ -1471,7 +1483,9 @@
 
     grad_attended = grad_attended.reshape(4, tokens, shards // 4, cols).transpose(0, 2, 1, 3)
     grad_attended = to_columns(grad_attended.reshape(shards, tokens, cols))
-    grad_attended, gate_arrived[0], mixture = barrier((grad_attended, gate_arrived[0], mixture))
+    grad_attended, down_arrived[1], gate_arrived[0], mixture = barrier(
+        (grad_attended, down_arrived[1], gate_arrived[0], mixture)
+    )
     mixture_own = sum_along_z(mixture)
     mid_cols = to_columns(
         reorder(mid_low, dp_index, 1).reshape(tokens, shards, cols).transpose(1, 0, 2)

time: 650 us -> 638 us (0.982)
  blocking collectives: 81.3 us -> 55.9 us
  waiting for transfers between devices: 127 us -> 134 us
    all_to_all x1 -> x0, blocking collectives: 18 us -> none  [to_columns(): return lax.all_to_all(values, 'seq', 0, 0, tiled=True).reshape(rows, cols)]
    all_to_all x1 -> x2, waiting for transfers between devices: 9.23 us -> 19.8 us  [to_columns(): return lax.all_to_all(values, 'seq', 0, 0, tiled=True).reshape(rows, cols)]
    convert_element_type x3 -> x6, other arithmetic: 11.8 us -> 20.6 us  [the longest x3 11.1 us: sum_experts_in_chip(): return (kept.astype(low), passed)]
    convert_element_type x5 -> x2, other arithmetic: 12 us -> 3.93 us  [sum_in_chip(): (pieces[2].astype(wide) + swap(pieces[3], 1).astype(wide)).astype(sent)]
    all_to_all x1, waiting for transfers between devices: 13.5 us -> 6.02 us  [share(): return lax.all_to_all(spread, 'seq', 0, 0, tiled=True)]
    all_to_all x1, blocking collectives: 18.6 us -> 11.2 us  [share(): return lax.all_to_all(spread, 'seq', 0, 0, tiled=True)]
    unnamed x125 -> x121, local copies, waits for them, and re-layouts: 16.6 us -> 15.8 us
  transfers between devices with their start and end apart: 51 -> 52, of which waited for: 18 -> 22; matrix products, arithmetic and copies ran while one was open for 20% -> 22% of each run, Pallas kernels for 36% -> 36%
where the time goes in v6:
time: 638 us; the launch traced here: 629 us
  Pallas kernels  227 us (36%)
  waiting for transfers between devices  134 us (21%)
  other arithmetic  91 us (14%)
  blocking collectives  55.9 us (9%)
  local copies, waits for them, and re-layouts  55.1 us (9%)
  starting transfers between devices  49.6 us (8%)
  between operations  15.4 us (2%)
    pallas_call x10, Pallas kernels, grid_call(): pl.pallas_call(body, grid=grid, in_specs=in_specs, out_specs=out_specs, o...  163 us
    ppermute x37, waiting for transfers between devices, swap(): return lax.ppermute(values, 'dp', [(i, i ^ bits) for i in range(4)])  62.4 us
    all_to_all x1, blocking collectives, on_device_heads(): lax.all_to_all(jnp.concatenate([blocks, gain_rows], axis=1), 'seq', 0, 0,...  44.7 us
    ppermute x37, starting transfers between devices, swap(): return lax.ppermute(values, 'dp', [(i, i ^ bits) for i in range(4)])  23.8 us
    ppermute x2, waiting for transfers between devices, over_y(): return lax.ppermute(values, 'seq', [(i, i ^ 1) for i in range(8)])  22.2 us
    all_to_all x2, waiting for transfers between devices, to_columns(): return lax.all_to_all(values, 'seq', 0, 0, tiled=True).reshape(rows, cols)  19.8 us
    another operation x6, other arithmetic, add_arrived(): jnp.stack([kept[e].astype(jnp.float32) + a.astype(jnp.float32) for e, a i...  19.6 us
    pallas_call x1, Pallas kernels, finish_attention(): pl.pallas_call(body, grid_spec=pltpu.PrefetchScalarGridSpec(num_scalar_pr...  19.1 us
  transfers between devices with their start and end apart: 52, of which 22 were waited for; matrix products, arithmetic and copies ran while one was open for 22% of the time, Pallas kernels for 36%

profile of v6, /device:TPU:0, one launch (start us, length us, event | category | flops | bytes accessed | tf_op | source)
XLA Modules:
  0.0 629.4 jit_solution(5291344699285489243)
XLA Ops:
  15.1 44.7 %all_to_all.40 = bf16[8,208,256]{2,1,0:T(8,128)(2,1)S(1)} all-to-all(bf16[8,208,256]{2,1,0:T(8,128)(2,1)S(1)} %pad_maximum_fusion.6), channel_id=1, replica_groups=mesh['dp'=4,'seq'=8] {'seq'}, dimensions={0} | all-to-all | bytes 1703936 | tf_op jit(solution)/shard_map/all_to_all | solution.py:1374
  64.6 17.2 %collective-permute-done.1 = bf16[8,208,256]{2,1,0:T(8,128)(2,1)} collective-permute-done((bf16[8,208,256]{2,1,0:T(8,128)(2,1)S(1)}, bf16[8,208,256]{2,1,0:T(8,128)(2,1)}, u32[]{:S(2)}, u32[]{:S(2)}) %collective-permute-start.1) | collective-permute-done | bytes 852000 | tf_op jit(solution)/shard_map/ppermute | solution.py:1273
  102.4 9.4 %shard_map.263 = (bf16[1024,2048]{1,0:T(8,128)(2,1)}, f32[1024,768]{1,0:T(8,128)}, f32[1024,1]{1,0:T(8,128)}, f32[8,1024]{1,0:T(8,128)}) custom-call(bf16[1024,2048]{1,0:T(8,128)(2,1)} %all-gather.7.cloned.1.call-done.x_ref.x, f32[1,2048]{1,0:T(1,128)} %reshape.248.gain_ref, bf16[2048,768]{1,0:T(8,128)(2,1)} %pad_maximum_fusion.5.w_ref.w), custom_call_target="tpu_custom_call" | custom-call | flops 805306368 | bytes 3681280 | tf_op jit(solution)/shard_map/pallas_call | solution.py:518
  125.0 10.9 %shard_map.264 = (bf16[1024,256]{1,0:T(8,128)(2,1)}, bf16[1024,256]{1,0:T(8,128)(2,1)}, bf16[1024,256]{1,0:T(8,128)(2,1)}, bf16[1024,256]{1,0:T(8,128)(2,1)}, f3...) custom-call(f32[1024,768]{1,0:T(8,128)} %get-tuple-element.154.q.k.v, ...), custom_call_target="tpu_custom_call" | custom-call | flops 268435456 | bytes 3168768 | tf_op jit(solution)/shard_map/pallas_call | solution.py:518
  138.7 7.2 %pad_maximum_fusion.gate_ref = bf16[2,2048,1024]{2,1,0:T(8,128)(2,1)} fusion(bf16[2,512,1024]{2,1,0:T(8,128)(2,1)} %collective-permute-done.5, bf16[2,512,1024]{2,1,0:T(8,128)(2,1)} %collective-permute-done.4, bf16[2,512,1024]{2,1,0:T(8,128)(2,1)} %collective-permute-done.3, bf16[2,512,1024]{2,1,0:T(8,128)(2,1)} %param.28), kind=kLoop, calls=%fused_computation | loop fusion | flops 33554432 | bytes 16777216 | tf_op jit(solution)/shard_map/concatenate | solution.py:1419
  147.3 21.6 %collective-permute-done.7 = bf16[4,64,2176]{2,1,0:T(8,128)(2,1)S(1)} collective-permute-done((bf16[4,64,2176]{2,1,0:T(8,128)(2,1)}, bf16[4,64,2176]{2,1,0:T(8,128)(2,1)S(1)}, u32[]{:S(2)}, u32[]{:S(2)}) %collective-permute-start.7) | collective-permute-done | bytes 1114144 | tf_op jit(solution)/shard_map/ppermute | solution.py:1249
  180.0 15.0 %collective-permute-done.9 = bf16[4,64,2176]{2,1,0:T(8,128)(2,1)S(1)} collective-permute-done((bf16[4,64,2176]{2,1,0:T(8,128)(2,1)S(1)}, bf16[4,64,2176]{2,1,0:T(8,128)(2,1)S(1)}, u32[]{:S(2)}, u32[]{:S(2)}) %collective-permute-start.9) | collective-permute-done | bytes 1114144 | tf_op jit(solution)/shard_map/ppermute | solution.py:1273
  215.4 19.1 %shard_map.265 = (f32[1024,2048]{1,0:T(8,128)}, bf16[1024,2048]{1,0:T(8,128)(2,1)}, f32[1024,1]{1,0:T(8,128)}, f32[1024,128]{1,0:T(8,128)}, f32[2,1024,1]{2,1,0:T(8,128)}) custom-call(s32[5]{0:T(128)} %stack.78.order_ref, bf16[8,1024,256]{2,1,0:T(8,128)(2,1)} %bitcast.197, bf16[512,2176]{1,0:T(8,128)(2,1)} %bitcast.195, ...), custom_call_target="tpu_custom_call" | custom-call | flops 2147483648 | bytes 6556672 | tf_op jit(solution)/shard_map/pallas_call | solution.py:587
  234.5 25.0 %shard_map.266 = (bf16[2,1024,1024]{2,1,0:T(8,128)(2,1)}, bf16[2,1024,1024]{2,1,0:T(8,128)(2,1)}, bf16[2,1024,1024]{2,1,0:T(8,128)(2,1)}) custom-call(bf16[1024,2048]{1,0:T(8,128)(2,1)} %get-tuple-element.184.x_ref.flat_ref, bf16[2,2048,1024]{2,1,0:T(8,128)(2,1)} %pad_maximum_fusion.gate_ref, bf16[2,2048,1024]{2,1,0:T(8,128)(2,1)} %pad_maximum_fusion.1.up_ref), custom_call_target="tpu_custom_call" | custom-call | flops 4294967296 | bytes 8388608 | tf_op jit(solution)/shard_map/pallas_call | solution.py:518
  267.9 14.6 %shard_map.267 = (bf16[512,2048]{1,0:T(8,128)(2,1)}, bf16[512,2048]{1,0:T(8,128)(2,1)}) custom-call(s32[1]{0:T(128)} %bitcast.44.y_ref, bf16[2,1024,1024]{2,1,0:T(8,128)(2,1)} %get-tuple-element.193.act_ref, bf16[2,1024,2048]{2,1,0:T(8,128)(2,1)} %constant_dynamic-update-slice_fusion.1.down_ref, f32[2,1024,1]{2,1,0:T(8,128)} %get-tuple-element.190.weight_ref), custom_call_target="tpu_custom_call" | custom-call | flops 2147483648 | bytes 4194304 | tf_op jit(solution)/shard_map/pallas_call | solution.py:795
  286.3 19.6 %shard_map.268 = (bf16[2,1024,1024]{2,1,0:T(8,128)(2,1)}, bf16[2,1024,1024]{2,1,0:T(8,128)(2,1)}, bf16[2,1024,1024]{2,1,0:T(8,128)(2,1)}, f32[2,1024,128]{2,1,0:T(8,128)}) custom-call(bf16[1024,2048]{1,0:T(8,128)(2,1)} %all-gather.9.cloned.1.call-done.dy_ref.flat_ref, bf16[2,1024,2048]{2,1,0:T(8,128)(2,1)} %constant_dynamic-update-slice_fusion.1.down_ref, ...), custom_call_target="tpu_custom_call" | custom-call | flops 2147483648 | bytes 9701376 | tf_op jit(solution)/shard_map/pallas_call | solution.py:518
  305.8 25.7 %shard_map.269 = (bf16[1024,2048]{1,0:T(8,128)(2,1)}, bf16[1024,128]{1,0:T(8,128)(2,1)}) custom-call(bf16[2,1024,1024]{2,1,0:T(8,128)(2,1)} %get-tuple-element.196.dgate_ref.stacked_ref, bf16[2,1024,1024]{2,1,0:T(8,128)(2,1)} %get-tuple-element.211.dup_ref.stacked_ref, bf16[2,2048,1024]{2,1,0:T(8,128)(2,1)} %pad_maximum_fusion.gate_ref, ...), custom_call_target="tpu_custom_call" | custom-call | flops 4294967296 | bytes 8061184 | tf_op jit(solution)/shard_map/pallas_call | solution.py:518
  332.1 18.6 %shard_map.270 = (bf16[2,1024,512]{2,1,0:T(8,128)(2,1)}, bf16[2,1024,512]{2,1,0:T(8,128)(2,1)}, bf16[2,1024,512]{2,1,0:T(8,128)(2,1)}, bf16[2,1024,512]{2,1,0:T(8,128)(2,1)}) custom-call(bf16[1024,2048]{1,0:T(8,128)(2,1)} %all-gather.9.cloned.1.call-done.dy_ref.flat_ref, bf16[2,1024,1024]{2,1,0:T(8,128)(2,1)} %get-tuple-element.205.stacked_ref), custom_call_target="tpu_custom_call" | custom-call | flops 2147483648 | bytes 4194304 | tf_op jit(solution)/shard_map/pallas_call | solution.py:518
  350.8 17.9 %shard_map.271 = (bf16[2,512,1024]{2,1,0:T(8,128)(2,1)}, bf16[2,512,1024]{2,1,0:T(8,128)(2,1)}, bf16[2,512,1024]{2,1,0:T(8,128)(2,1)}, bf16[2,512,1024]{2,1,0:T(8,128)(2,1)}) custom-call(bf16[1024,2048]{1,0:T(8,128)(2,1)} %get-tuple-element.184.x_ref.flat_ref, bf16[2,1024,1024]{2,1,0:T(8,128)(2,1)} %get-tuple-element.196.dgate_ref.stacked_ref), custom_call_target="tpu_custom_call" | custom-call | flops 2147483648 | bytes 4194304 | tf_op jit(solution)/shard_map/pallas_call | solution.py:518
  371.1 18.0 %shard_map.272 = (bf16[2,512,1024]{2,1,0:T(8,128)(2,1)}, bf16[2,512,1024]{2,1,0:T(8,128)(2,1)}, bf16[2,512,1024]{2,1,0:T(8,128)(2,1)}, bf16[2,512,1024]{2,1,0:T(8,128)(2,1)}) custom-call(bf16[1024,2048]{1,0:T(8,128)(2,1)} %get-tuple-element.184.x_ref.flat_ref, bf16[2,1024,1024]{2,1,0:T(8,128)(2,1)} %get-tuple-element.211.dup_ref.stacked_ref), custom_call_target="tpu_custom_call" | custom-call | flops 2147483648 | bytes 4194304 | tf_op jit(solution)/shard_map/pallas_call | solution.py:518
  421.4 8.7 %shard_map.273 = (f32[128,2048]{1,0:T(8,128)}, bf16[128,2048]{1,0:T(8,128)(2,1)}, bf16[4,128,512]{2,1,0:T(8,128)(2,1)}, f32[1,2048]{1,0:T(1,128)}) custom-call(s32[5]{0:T(128)} %stack.78.order_ref, bf16[128,2048]{1,0:T(8,128)(2,1)} %reduce-scatter.4.cloned.1.call-done.nf, f32[1024,2048]{1,0:T(8,128)} %get-tuple-element.222.mid_ref, ...), custom_call_target="tpu_custom_call" | custom-call | flops 268435456 | bytes 2754560 | tf_op jit(solution)/shard_map/pallas_call | solution.py:1192
  439.5 11.5 %all-to-all-done.2 = bf16[8,128,256]{2,1,0:T(8,128)(2,1)S(1)} async-done(((bf16[8,128,256]{2,1,0:T(8,128)(2,1)}), bf16[8,128,256]{2,1,0:T(8,128)(2,1)S(1)}, u32[]{:S(2)}, u32[]{:S(2)}) %all-to-all-start.2) | async-done | bytes 524320 | tf_op jit(solution)/shard_map/all_to_all | solution.py:1482
  451.0 10.1 %collective-permute-done.26 = bf16[512,1024]{1,0:T(8,128)(2,1)} collective-permute-done((bf16[512,1024]{1,0:T(8,128)(2,1)}, bf16[512,1024]{1,0:T(8,128)(2,1)}, u32[]{:S(2)}, u32[]{:S(2)}) %collective-permute-start.26) | collective-permute-done | bytes 1048608 | tf_op jit(solution)/shard_map/ppermute | solution.py:1273
  468.9 12.9 %shard_map.274 = (f32[1024,256]{1,0:T(8,128)}, f32[1024,256]{1,0:T(8,128)}, bf16[1024,256]{1,0:T(8,128)(2,1)}, f32[8,1024]{1,0:T(8,128)}, f32[1,256]{1,0:T(1,128)}, /*index=5*/f32[1,256]{1,0:T(1,128)}) custom-call(f32[1024,768]{1,0:T(8,128)} %get-tuple-element.154.q.k.v, f32[1024,768]{1,0:T(8,128)} %get-tuple-element.154.q.k.v, ...), custom_call_target="tpu_custom_call" | custom-call | flops 671088640 | bytes 3030016 | tf_op jit(solution)/shard_map/pallas_call | solution.py:1075
  488.4 8.4 %all-to-all-done.4 = bf16[8,128,256]{2,1,0:T(8,128)(2,1)S(1)} async-done(((bf16[8,128,256]{2,1,0:T(8,128)(2,1)}), bf16[8,128,256]{2,1,0:T(8,128)(2,1)S(1)}, u32[]{:S(2)}, u32[]{:S(2)}) %all-to-all-start.4) | async-done | bytes 524320 | tf_op jit(solution)/shard_map/all_to_all | solution.py:1482
  496.8 11.2 %all_to_all.41.sums_ref = f32[8,2,1024]{2,1,0:T(2,128)} all-to-all(f32[8,2,1024]{2,1,0:T(2,128)S(1)} %broadcast_in_dim.70), channel_id=1, replica_groups=mesh['dp'=4,'seq'=8] {'seq'}, dimensions={0} | all-to-all | bytes 131072 | tf_op jit(solution)/shard_map/all_to_all | solution.py:1409
  508.0 10.4 %shard_map.275 = (bf16[1024,768]{1,0:T(8,128)(2,1)}, bf16[1024,2048]{1,0:T(8,128)(2,1)}, f32[1,2048]{1,0:T(1,128)}) custom-call(f32[1024,256]{1,0:T(8,128)} %get-tuple-element.232.qg, f32[1024,256]{1,0:T(8,128)} %get-tuple-element.233.kg, bf16[1024,256]{1,0:T(8,128)(2,1)} %get-tuple-element.234.v, f32[1024,768]{1,0:T(8,128)} %get-tuple-element.154.q.k.v, ...), custom_call_target="tpu_custom_call" | custom-call | flops 805306368 | bytes 5526528 | tf_op jit(solution)/shard_map/pallas_call | solution.py:518
  519.2 7.9 %shard_map.276 = (bf16[1,512,768]{2,1,0:T(8,128)(2,1)}, bf16[1,512,768]{2,1,0:T(8,128)(2,1)}, bf16[1,512,768]{2,1,0:T(8,128)(2,1)}, bf16[1,512,768]{2,1,0:T(8,128)(2,1)}) custom-call(bf16[1024,2048]{1,0:T(8,128)(2,1)} %get-tuple-element.253.flat_ref, bf16[1,1024,768]{2,1,0:T(8,128)(2,1)} %bitcast.220), custom_call_target="tpu_custom_call" | custom-call | flops 805306368 | bytes 2228224 | tf_op jit(solution)/shard_map/pallas_call | solution.py:518
  527.8 8.2 %shard_map.277 = (bf16[512,256]{1,0:T(8,128)(2,1)}, bf16[512,256]{1,0:T(8,128)(2,1)}, bf16[512,256]{1,0:T(8,128)(2,1)}, bf16[512,256]{1,0:T(8,128)(2,1)}) custom-call(s32[5]{0:T(128)} %stack.78.order_ref, bf16[8,1024,256]{2,1,0:T(8,128)(2,1)} %bitcast.198, bf16[1024,256]{1,0:T(8,128)(2,1)} %bitcast.214), custom_call_target="tpu_custom_call" | custom-call | flops 268435456 | bytes 1441792 | tf_op jit(solution)/shard_map/pallas_call | solution.py:1231
  (349 shorter events, 240.2 us)
Async XLA Ops:
  7.2 95.2 %all-gather.7.cloned.1.call-start = ((), (), s32[]{:S(2)}) async-start(), calls=%async_computation.11 | async-start | bytes 4718592 | tf_op jit(solution)/shard_map/all_gather | solution.py:1359
  11.1 124.8 %all-gather.11.cloned.1.call-start = ((), (), s32[]{:S(2)}) async-start(), calls=%async_computation.16 | async-start | bytes 1392640 | tf_op jit(solution)/shard_map/all_gather | solution.py:1254
  11.1 49.8 %collective-permute-start.4 = (bf16[2,512,1024]{2,1,0:T(8,128)(2,1)}, bf16[2,512,1024]{2,1,0:T(8,128)(2,1)}, u32[]{:S(2)}, u32[]{:S(2)}) collective-permute-start(bf16[2,512,1024]{2,1,0:T(8,128)(2,1)} %param.28), channel_id=1, source_target_pairs={{0,16},{8,24},{16,0},{24,8},{1,17},{9,25},{17,1},{25,9},{2,18},{10... | collective-permute-start | bytes 6291464 | tf_op jit(solution)/shard_map/ppermute | solution.py:1273
  60.3 38.8 %collective-permute-start.3 = (bf16[2,512,1024]{2,1,0:T(8,128)(2,1)}, bf16[2,512,1024]{2,1,0:T(8,128)(2,1)}, u32[]{:S(2)}, u32[]{:S(2)}) collective-permute-start(bf16[2,512,1024]{2,1,0:T(8,128)(2,1)} %param.28), channel_id=1, source_target_pairs={{0,8},{8,0},{16,24},{24,16},{1,9},{9,1},{17,25},{25,17},{2,10},{10... | collective-permute-start | bytes 6291464 | tf_op jit(solution)/shard_map/ppermute | solution.py:1273
  60.9 38.2 %collective-permute-start.5 = (bf16[2,512,1024]{2,1,0:T(8,128)(2,1)}, bf16[2,512,1024]{2,1,0:T(8,128)(2,1)}, u32[]{:S(2)}, u32[]{:S(2)}) collective-permute-start(bf16[2,512,1024]{2,1,0:T(8,128)(2,1)} %collective-permute-done.4), channel_id=1, source_target_pairs={{0,8},{8,0},{16,24},{24,16},{1,9},{9,1},{17,25},{25,17},{2,10},{10... | collective-permute-start | bytes 6291464 | tf_op jit(solution)/shard_map/ppermute | solution.py:1273
  60.9 75.0 %collective-permute-start.6 = (bf16[2,512,1024]{2,1,0:T(8,128)(2,1)}, bf16[2,512,1024]{2,1,0:T(8,128)(2,1)}, u32[]{:S(2)}, u32[]{:S(2)}) collective-permute-start(bf16[2,512,1024]{2,1,0:T(8,128)(2,1)} %param.29), channel_id=1, source_target_pairs={{0,16},{8,24},{16,0},{24,8},{1,17},{9,25},{17,1},{25,9},{2,18},{10... | collective-permute-start | bytes 6291464 | tf_op jit(solution)/shard_map/ppermute | solution.py:1273
  116.7 95.3 %all-gather.13.cloned.1.call-start = ((), (), s32[]{:S(2)}) async-start(), calls=%async_computation.17 | async-start | bytes 4718592 | tf_op jit(solution)/shard_map/all_gather | solution.py:1417
  135.9 149.8 %all-gather.9.cloned.1.call-start = ((), (), s32[]{:S(2)}) async-start(), calls=%async_computation.12 | async-start | bytes 4718592 | tf_op jit(solution)/shard_map/all_gather | solution.py:1442
  136.0 37.5 %collective-permute-start.10 = (bf16[2,512,1024]{2,1,0:T(8,128)(2,1)}, bf16[2,512,1024]{2,1,0:T(8,128)(2,1)}, u32[]{:S(2)}, u32[]{:S(2)}) collective-permute-start(bf16[2,512,1024]{2,1,0:T(8,128)(2,1)} %param.29), channel_id=1, source_target_pairs={{0,8},{8,0},{16,24},{24,16},{1,9},{9,1},{17,25},{25,17},{2,10},{10... | collective-permute-start | bytes 6291464 | tf_op jit(solution)/shard_map/ppermute | solution.py:1273
  136.1 32.8 %collective-permute-start.7 = (bf16[4,64,2176]{2,1,0:T(8,128)(2,1)}, bf16[4,64,2176]{2,1,0:T(8,128)(2,1)S(1)}, u32[]{:S(2)}, u32[]{:S(2)}) collective-permute-start(bf16[4,64,2176]{2,1,0:T(8,128)(2,1)} %bitcast.221), channel_id=1, source_target_pairs={{0,1},{1,0},{2,3},{3,2},{4,5},{5,4},{6,7},{7,6},{8,9},{9,8},{10,11... | collective-permute-start | bytes 3342344 | tf_op jit(solution)/shard_map/ppermute | solution.py:1249
  137.3 31.6 %collective-permute-start.8 = (bf16[4,64,2176]{2,1,0:T(8,128)(2,1)}, bf16[4,64,2176]{2,1,0:T(8,128)(2,1)S(1)}, u32[]{:S(2)}, u32[]{:S(2)}) collective-permute-start(bf16[4,64,2176]{2,1,0:T(8,128)(2,1)} %bitcast.222), channel_id=1, source_target_pairs={{0,16},{8,24},{16,0},{24,8},{1,17},{9,25},{17,1},{25,9},{2,18},{10... | collective-permute-start | bytes 3342344 | tf_op jit(solution)/shard_map/ppermute | solution.py:1273
  145.9 27.5 %collective-permute-start.11 = (bf16[2,512,1024]{2,1,0:T(8,128)(2,1)}, bf16[2,512,1024]{2,1,0:T(8,128)(2,1)S(1)}, u32[]{:S(2)}, u32[]{:S(2)}) collective-permute-start(bf16[2,512,1024]{2,1,0:T(8,128)(2,1)} %collective-permute-done.6), channel_id=1, source_target_pairs={{0,8},{8,0},{16,24},{24,16},{1,9},{9,1},{17,25},{25,17},{2,10},{10... | collective-permute-start | bytes 6291464 | tf_op jit(solution)/shard_map/ppermute | solution.py:1273
  212.0 207.9 %reduce-scatter.4.cloned.1.call-start = ((), (), s32[]{:S(2)}) async-start(), calls=%async_computation.13 | async-start | bytes 4718592 | tf_op jit(solution)/shard_map/reduce_scatter | solution.py:1462
  212.6 46.9 %collective-permute-start.14 = (bf16[2,1024,512]{2,1,0:T(8,128)(2,1)}, bf16[2,1024,512]{2,1,0:T(8,128)(2,1)S(1)}, u32[]{:S(2)}, u32[]{:S(2)}) collective-permute-start(bf16[2,1024,512]{2,1,0:T(8,128)(2,1)} %param.30), channel_id=1, source_target_pairs={{0,16},{8,24},{16,0},{24,8},{1,17},{9,25},{17,1},{25,9},{2,18},{10... | collective-permute-start | bytes 6291464 | tf_op jit(solution)/shard_map/ppermute | solution.py:1273
  214.2 47.5 %collective-permute-start.15 = (bf16[2,1024,512]{2,1,0:T(8,128)(2,1)}, bf16[2,1024,512]{2,1,0:T(8,128)(2,1)}, u32[]{:S(2)}, u32[]{:S(2)}) collective-permute-start(bf16[2,1024,512]{2,1,0:T(8,128)(2,1)} %param.30), channel_id=1, source_target_pairs={{0,8},{8,0},{16,24},{24,16},{1,9},{9,1},{17,25},{25,17},{2,10},{10... | collective-permute-start | bytes 6291464 | tf_op jit(solution)/shard_map/ppermute | solution.py:1273
  285.7 46.4 %collective-permute-start.17 = (bf16[512,2048]{1,0:T(8,128)(2,1)}, bf16[512,2048]{1,0:T(8,128)(2,1)S(1)}, u32[]{:S(2)}, u32[]{:S(2)}) collective-permute-start(bf16[512,2048]{1,0:T(8,128)(2,1)} %get-tuple-element.201), channel_id=1, source_target_pairs={{0,1},{1,0},{2,3},{3,2},{4,5},{5,4},{6,7},{7,6},{8,9},{9,8},{10,11... | collective-permute-start | bytes 6291464 | tf_op jit(solution)/shard_map/ppermute | solution.py:1249
  369.0 29.6 %collective-permute-start.22 = (bf16[2,1024,512]{2,1,0:T(8,128)(2,1)}, bf16[2,1024,512]{2,1,0:T(8,128)(2,1)}, u32[]{:S(2)}, u32[]{:S(2)}) collective-permute-start(bf16[2,1024,512]{2,1,0:T(8,128)(2,1)} %get-tuple-element.216), channel_id=1, source_target_pairs={{0,8},{8,0},{16,24},{24,16},{1,9},{9,1},{17,25},{25,17},{2,10},{10... | collective-permute-start | bytes 6291464 | tf_op jit(solution)/shard_map/ppermute | solution.py:1273
  369.1 34.5 %collective-permute-start.20 = (bf16[2,512,1024]{2,1,0:T(8,128)(2,1)}, bf16[2,512,1024]{2,1,0:T(8,128)(2,1)}, u32[]{:S(2)}, u32[]{:S(2)}) collective-permute-start(bf16[2,512,1024]{2,1,0:T(8,128)(2,1)} %get-tuple-element.210), channel_id=1, source_target_pairs={{0,8},{8,0},{16,24},{24,16},{1,9},{9,1},{17,25},{25,17},{2,10},{10... | collective-permute-start | bytes 6291464 | tf_op jit(solution)/shard_map/ppermute | solution.py:1273
  398.6 40.9 %collective-permute-start.25 = (bf16[1024,512]{1,0:T(8,128)(2,1)}, bf16[1024,512]{1,0:T(8,128)(2,1)}, u32[]{:S(2)}, u32[]{:S(2)}) collective-permute-start(bf16[1024,512]{1,0:T(8,128)(2,1)} %get-tuple-element.225), channel_id=1, source_target_pairs={{0,16},{8,24},{16,0},{24,8},{1,17},{9,25},{17,1},{25,9},{2,18},{10... | collective-permute-start | bytes 3145736 | tf_op jit(solution)/shard_map/ppermute | solution.py:1273
  420.0 41.2 %collective-permute-start.26 = (bf16[512,1024]{1,0:T(8,128)(2,1)}, bf16[512,1024]{1,0:T(8,128)(2,1)}, u32[]{:S(2)}, u32[]{:S(2)}) collective-permute-start(bf16[512,1024]{1,0:T(8,128)(2,1)} %get-tuple-element.226), channel_id=1, source_target_pairs={{0,16},{8,24},{16,0},{24,8},{1,17},{9,25},{17,1},{25,9},{2,18},{10... | collective-permute-start | bytes 3145736 | tf_op jit(solution)/shard_map/ppermute | solution.py:1273
  436.6 81.9 %reduce-scatter.6.cloned.1.call-start = ((), (), s32[]{:S(2)}) async-start(), calls=%async_computation.14 | async-start | bytes 2621440 | tf_op jit(solution)/shard_map/reduce_scatter | solution.py:1267
  463.6 33.1 %all-to-all-start.4 = ((bf16[8,128,256]{2,1,0:T(8,128)(2,1)}), bf16[8,128,256]{2,1,0:T(8,128)(2,1)S(1)}, u32[]{:S(2)}, u32[]{:S(2)}) async-start(bf16[8,128,256]{2,1,0:T(8,128)(2,1)} %bitcast.187), calls=%async_computation.5 | async-start | bytes 1048576 | tf_op jit(solution)/shard_map/all_to_all | solution.py:1482
  468.2 150.3 %reduce-scatter.8.cloned.1.call-start = ((), (), s32[]{:S(2)}) async-start(), calls=%async_computation.15 | async-start | bytes 4718592 | tf_op jit(solution)/shard_map/reduce_scatter | solution.py:1503
  468.3 50.1 %collective-permute-start.28 = (bf16[512,1024]{1,0:T(8,128)(2,1)}, bf16[512,1024]{1,0:T(8,128)(2,1)}, u32[]{:S(2)}, u32[]{:S(2)}) collective-permute-start(bf16[512,1024]{1,0:T(8,128)(2,1)} %get-tuple-element.242), channel_id=1, source_target_pairs={{0,16},{8,24},{16,0},{24,8},{1,17},{9,25},{17,1},{25,9},{2,18},{10... | collective-permute-start | bytes 3145736 | tf_op jit(solution)/shard_map/ppermute | solution.py:1273
  (80 other events, 1155.4 us)
Sparse Core Ops, SparseCore 0:
  11.2 91.1 all-gather.6
  104.6 29.2 all-gather.10
  136.6 75.4 all-gather.12
  214.0 71.6 all-gather.8
  332.2 87.6 reduce-scatter.3
  461.3 53.1 reduce-scatter.5
  518.6 99.8 reduce-scatter.7

commit v7 on v6

--- a/solution.py
+++ b/solution.py
@@ -1468,6 +1468,7 @@
     down_arrived = across_by_expert(down_passed)
     gate_kept, gate_passed = sum_experts_in_chip(gate_pieces)
     up_pieces = weight_pieces(normed_ffn, dup, 4, True)
+    up_pieces, down_arrived[0] = barrier((up_pieces, down_arrived[0]))
     up_kept, up_passed = sum_experts_in_chip(up_pieces)
     router_grad = mm(grad_logits[:, :expert_count], normed_ffn, ((0,), (0,)))
     nf_sum, mixture, down_arrived[0], gate_passed, up_passed, router_grad, down_kept, gate_kept, up_kept = barrier(

time: 638 us -> 627 us (0.983)
  waiting for transfers between devices: 134 us -> 124 us
    ppermute x37, waiting for transfers between devices: 62.4 us -> 53.3 us  [swap(): return lax.ppermute(values, 'dp', [(i, i ^ bits) for i in range(4)])]
  transfers between devices with their start and end apart: 52 -> 52, of which waited for: 22 -> 19; matrix products, arithmetic and copies ran while one was open for 22% -> 22% of each run, Pallas kernels for 36% -> 37%
where the time goes in v7:
time: 627 us; the launch traced here: 618 us
  Pallas kernels  227 us (36%)
  waiting for transfers between devices  124 us (20%)
  other arithmetic  90.8 us (14%)
  blocking collectives  55.9 us (9%)
  local copies, waits for them, and re-layouts  55.3 us (9%)
  starting transfers between devices  48.5 us (8%)
  between operations  15.4 us (2%)
    pallas_call x10, Pallas kernels, grid_call(): pl.pallas_call(body, grid=grid, in_specs=in_specs, out_specs=out_specs, o...  163 us
    ppermute x37, waiting for transfers between devices, swap(): return lax.ppermute(values, 'dp', [(i, i ^ bits) for i in range(4)])  53.3 us
    all_to_all x1, blocking collectives, on_device_heads(): lax.all_to_all(jnp.concatenate([blocks, gain_rows], axis=1), 'seq', 0, 0,...  44.7 us
    ppermute x37, starting transfers between devices, swap(): return lax.ppermute(values, 'dp', [(i, i ^ bits) for i in range(4)])  23.8 us
    ppermute x2, waiting for transfers between devices, over_y(): return lax.ppermute(values, 'seq', [(i, i ^ 1) for i in range(8)])  22.2 us
    all_to_all x2, waiting for transfers between devices, to_columns(): return lax.all_to_all(values, 'seq', 0, 0, tiled=True).reshape(rows, cols)  21.6 us
    another operation x6, other arithmetic, add_arrived(): jnp.stack([kept[e].astype(jnp.float32) + a.astype(jnp.float32) for e, a i...  19.7 us
    pallas_call x1, Pallas kernels, finish_attention(): pl.pallas_call(body, grid_spec=pltpu.PrefetchScalarGridSpec(num_scalar_pr...  19.1 us
  transfers between devices with their start and end apart: 52, of which 19 were waited for; matrix products, arithmetic and copies ran while one was open for 22% of the time, Pallas kernels for 37%

profile of v7, /device:TPU:0, one launch (start us, length us, event | category | flops | bytes accessed | tf_op | source)
XLA Modules:
  0.0 618.3 jit_solution(3612200049887938261)
XLA Ops:
  15.1 44.7 %all_to_all.40 = bf16[8,208,256]{2,1,0:T(8,128)(2,1)S(1)} all-to-all(bf16[8,208,256]{2,1,0:T(8,128)(2,1)S(1)} %pad_maximum_fusion.6), channel_id=1, replica_groups=mesh['dp'=4,'seq'=8] {'seq'}, dimensions={0} | all-to-all | bytes 1703936 | tf_op jit(solution)/shard_map/all_to_all | solution.py:1374
  64.6 17.2 %collective-permute-done.1 = bf16[8,208,256]{2,1,0:T(8,128)(2,1)} collective-permute-done((bf16[8,208,256]{2,1,0:T(8,128)(2,1)S(1)}, bf16[8,208,256]{2,1,0:T(8,128)(2,1)}, u32[]{:S(2)}, u32[]{:S(2)}) %collective-permute-start.1) | collective-permute-done | bytes 852000 | tf_op jit(solution)/shard_map/ppermute | solution.py:1273
  102.4 9.4 %shard_map.263 = (bf16[1024,2048]{1,0:T(8,128)(2,1)}, f32[1024,768]{1,0:T(8,128)}, f32[1024,1]{1,0:T(8,128)}, f32[8,1024]{1,0:T(8,128)}) custom-call(bf16[1024,2048]{1,0:T(8,128)(2,1)} %all-gather.7.cloned.1.call-done.x_ref.x, f32[1,2048]{1,0:T(1,128)} %reshape.248.gain_ref, bf16[2048,768]{1,0:T(8,128)(2,1)} %pad_maximum_fusion.5.w_ref.w), custom_call_target="tpu_custom_call" | custom-call | flops 805306368 | bytes 3681280 | tf_op jit(solution)/shard_map/pallas_call | solution.py:518
  125.0 10.9 %shard_map.264 = (bf16[1024,256]{1,0:T(8,128)(2,1)}, bf16[1024,256]{1,0:T(8,128)(2,1)}, bf16[1024,256]{1,0:T(8,128)(2,1)}, bf16[1024,256]{1,0:T(8,128)(2,1)}, f3...) custom-call(f32[1024,768]{1,0:T(8,128)} %get-tuple-element.159.q.k.v, ...), custom_call_target="tpu_custom_call" | custom-call | flops 268435456 | bytes 3168768 | tf_op jit(solution)/shard_map/pallas_call | solution.py:518
  138.7 7.2 %pad_maximum_fusion.gate_ref = bf16[2,2048,1024]{2,1,0:T(8,128)(2,1)} fusion(bf16[2,512,1024]{2,1,0:T(8,128)(2,1)} %collective-permute-done.5, bf16[2,512,1024]{2,1,0:T(8,128)(2,1)} %collective-permute-done.4, bf16[2,512,1024]{2,1,0:T(8,128)(2,1)} %collective-permute-done.3, bf16[2,512,1024]{2,1,0:T(8,128)(2,1)} %param.28), kind=kLoop, calls=%fused_computation | loop fusion | flops 33554432 | bytes 16777216 | tf_op jit(solution)/shard_map/concatenate | solution.py:1419
  147.3 21.6 %collective-permute-done.7 = bf16[4,64,2176]{2,1,0:T(8,128)(2,1)S(1)} collective-permute-done((bf16[4,64,2176]{2,1,0:T(8,128)(2,1)}, bf16[4,64,2176]{2,1,0:T(8,128)(2,1)S(1)}, u32[]{:S(2)}, u32[]{:S(2)}) %collective-permute-start.7) | collective-permute-done | bytes 1114144 | tf_op jit(solution)/shard_map/ppermute | solution.py:1249
  180.0 15.0 %collective-permute-done.9 = bf16[4,64,2176]{2,1,0:T(8,128)(2,1)S(1)} collective-permute-done((bf16[4,64,2176]{2,1,0:T(8,128)(2,1)S(1)}, bf16[4,64,2176]{2,1,0:T(8,128)(2,1)S(1)}, u32[]{:S(2)}, u32[]{:S(2)}) %collective-permute-start.9) | collective-permute-done | bytes 1114144 | tf_op jit(solution)/shard_map/ppermute | solution.py:1273
  215.4 19.1 %shard_map.265 = (f32[1024,2048]{1,0:T(8,128)}, bf16[1024,2048]{1,0:T(8,128)(2,1)}, f32[1024,1]{1,0:T(8,128)}, f32[1024,128]{1,0:T(8,128)}, f32[2,1024,1]{2,1,0:T(8,128)}) custom-call(s32[5]{0:T(128)} %stack.78.order_ref, bf16[8,1024,256]{2,1,0:T(8,128)(2,1)} %bitcast.197, bf16[512,2176]{1,0:T(8,128)(2,1)} %bitcast.195, ...), custom_call_target="tpu_custom_call" | custom-call | flops 2147483648 | bytes 6556672 | tf_op jit(solution)/shard_map/pallas_call | solution.py:587
  234.5 25.0 %shard_map.266 = (bf16[2,1024,1024]{2,1,0:T(8,128)(2,1)}, bf16[2,1024,1024]{2,1,0:T(8,128)(2,1)}, bf16[2,1024,1024]{2,1,0:T(8,128)(2,1)}) custom-call(bf16[1024,2048]{1,0:T(8,128)(2,1)} %get-tuple-element.189.x_ref.flat_ref, bf16[2,2048,1024]{2,1,0:T(8,128)(2,1)} %pad_maximum_fusion.gate_ref, bf16[2,2048,1024]{2,1,0:T(8,128)(2,1)} %pad_maximum_fusion.1.up_ref), custom_call_target="tpu_custom_call" | custom-call | flops 4294967296 | bytes 8388608 | tf_op jit(solution)/shard_map/pallas_call | solution.py:518
  267.9 14.6 %shard_map.267 = (bf16[512,2048]{1,0:T(8,128)(2,1)}, bf16[512,2048]{1,0:T(8,128)(2,1)}) custom-call(s32[1]{0:T(128)} %bitcast.44.y_ref, bf16[2,1024,1024]{2,1,0:T(8,128)(2,1)} %get-tuple-element.198.act_ref, bf16[2,1024,2048]{2,1,0:T(8,128)(2,1)} %constant_dynamic-update-slice_fusion.1.down_ref, f32[2,1024,1]{2,1,0:T(8,128)} %get-tuple-element.195.weight_ref), custom_call_target="tpu_custom_call" | custom-call | flops 2147483648 | bytes 4194304 | tf_op jit(solution)/shard_map/pallas_call | solution.py:795
  286.3 19.6 %shard_map.268 = (bf16[2,1024,1024]{2,1,0:T(8,128)(2,1)}, bf16[2,1024,1024]{2,1,0:T(8,128)(2,1)}, bf16[2,1024,1024]{2,1,0:T(8,128)(2,1)}, f32[2,1024,128]{2,1,0:T(8,128)}) custom-call(bf16[1024,2048]{1,0:T(8,128)(2,1)} %all-gather.9.cloned.1.call-done.dy_ref.flat_ref, bf16[2,1024,2048]{2,1,0:T(8,128)(2,1)} %constant_dynamic-update-slice_fusion.1.down_ref, ...), custom_call_target="tpu_custom_call" | custom-call | flops 2147483648 | bytes 9701376 | tf_op jit(solution)/shard_map/pallas_call | solution.py:518
  305.8 25.7 %shard_map.269 = (bf16[1024,2048]{1,0:T(8,128)(2,1)}, bf16[1024,128]{1,0:T(8,128)(2,1)}) custom-call(bf16[2,1024,1024]{2,1,0:T(8,128)(2,1)} %get-tuple-element.201.dgate_ref.stacked_ref, bf16[2,1024,1024]{2,1,0:T(8,128)(2,1)} %get-tuple-element.213.dup_ref.stacked_ref, bf16[2,2048,1024]{2,1,0:T(8,128)(2,1)} %pad_maximum_fusion.gate_ref, ...), custom_call_target="tpu_custom_call" | custom-call | flops 4294967296 | bytes 8061184 | tf_op jit(solution)/shard_map/pallas_call | solution.py:518
  332.1 18.6 %shard_map.270 = (bf16[2,1024,512]{2,1,0:T(8,128)(2,1)}, bf16[2,1024,512]{2,1,0:T(8,128)(2,1)}, bf16[2,1024,512]{2,1,0:T(8,128)(2,1)}, bf16[2,1024,512]{2,1,0:T(8,128)(2,1)}) custom-call(bf16[1024,2048]{1,0:T(8,128)(2,1)} %all-gather.9.cloned.1.call-done.dy_ref.flat_ref, bf16[2,1024,1024]{2,1,0:T(8,128)(2,1)} %get-tuple-element.210.stacked_ref), custom_call_target="tpu_custom_call" | custom-call | flops 2147483648 | bytes 4194304 | tf_op jit(solution)/shard_map/pallas_call | solution.py:518
  350.8 17.9 %shard_map.272 = (bf16[2,512,1024]{2,1,0:T(8,128)(2,1)}, bf16[2,512,1024]{2,1,0:T(8,128)(2,1)}, bf16[2,512,1024]{2,1,0:T(8,128)(2,1)}, bf16[2,512,1024]{2,1,0:T(8,128)(2,1)}) custom-call(bf16[1024,2048]{1,0:T(8,128)(2,1)} %get-tuple-element.189.x_ref.flat_ref, bf16[2,1024,1024]{2,1,0:T(8,128)(2,1)} %get-tuple-element.201.dgate_ref.stacked_ref), custom_call_target="tpu_custom_call" | custom-call | flops 2147483648 | bytes 4194304 | tf_op jit(solution)/shard_map/pallas_call | solution.py:518
  372.3 18.0 %shard_map.271 = (bf16[2,512,1024]{2,1,0:T(8,128)(2,1)}, bf16[2,512,1024]{2,1,0:T(8,128)(2,1)}, bf16[2,512,1024]{2,1,0:T(8,128)(2,1)}, bf16[2,512,1024]{2,1,0:T(8,128)(2,1)}) custom-call(bf16[1024,2048]{1,0:T(8,128)(2,1)} %get-tuple-element.189.x_ref.flat_ref, bf16[2,1024,1024]{2,1,0:T(8,128)(2,1)} %get-tuple-element.213.dup_ref.stacked_ref), custom_call_target="tpu_custom_call" | custom-call | flops 2147483648 | bytes 4194304 | tf_op jit(solution)/shard_map/pallas_call | solution.py:518
  421.6 8.7 %shard_map.273 = (f32[128,2048]{1,0:T(8,128)}, bf16[128,2048]{1,0:T(8,128)(2,1)}, bf16[4,128,512]{2,1,0:T(8,128)(2,1)}, f32[1,2048]{1,0:T(1,128)}) custom-call(s32[5]{0:T(128)} %stack.78.order_ref, bf16[128,2048]{1,0:T(8,128)(2,1)} %reduce-scatter.4.cloned.1.call-done.nf, f32[1024,2048]{1,0:T(8,128)} %get-tuple-element.232.mid_ref, ...), custom_call_target="tpu_custom_call" | custom-call | flops 268435456 | bytes 2754560 | tf_op jit(solution)/shard_map/pallas_call | solution.py:1192
  436.7 14.3 %all-to-all-done.2 = bf16[8,128,256]{2,1,0:T(8,128)(2,1)S(1)} async-done(((bf16[8,128,256]{2,1,0:T(8,128)(2,1)}), bf16[8,128,256]{2,1,0:T(8,128)(2,1)S(1)}, u32[]{:S(2)}, u32[]{:S(2)}) %all-to-all-start.2) | async-done | bytes 524320 | tf_op jit(solution)/shard_map/all_to_all | solution.py:1483
  457.8 13.0 %shard_map.274 = (f32[1024,256]{1,0:T(8,128)}, f32[1024,256]{1,0:T(8,128)}, bf16[1024,256]{1,0:T(8,128)(2,1)}, f32[8,1024]{1,0:T(8,128)}, f32[1,256]{1,0:T(1,128)}, /*index=5*/f32[1,256]{1,0:T(1,128)}) custom-call(f32[1024,768]{1,0:T(8,128)} %get-tuple-element.159.q.k.v, f32[1024,768]{1,0:T(8,128)} %get-tuple-element.159.q.k.v, ...), custom_call_target="tpu_custom_call" | custom-call | flops 671088640 | bytes 3030016 | tf_op jit(solution)/shard_map/pallas_call | solution.py:1075
  470.7 6.7 %collective-permute-done.27 = bf16[512,1024]{1,0:T(8,128)(2,1)} collective-permute-done((bf16[512,1024]{1,0:T(8,128)(2,1)}, bf16[512,1024]{1,0:T(8,128)(2,1)}, u32[]{:S(2)}, u32[]{:S(2)}) %collective-permute-start.27) | collective-permute-done | bytes 1048608 | tf_op jit(solution)/shard_map/ppermute | solution.py:1273
  478.2 7.3 %all-to-all-done.4 = bf16[8,128,256]{2,1,0:T(8,128)(2,1)S(1)} async-done(((bf16[8,128,256]{2,1,0:T(8,128)(2,1)}), bf16[8,128,256]{2,1,0:T(8,128)(2,1)S(1)}, u32[]{:S(2)}, u32[]{:S(2)}) %all-to-all-start.4) | async-done | bytes 524320 | tf_op jit(solution)/shard_map/all_to_all | solution.py:1483
  485.5 11.2 %all_to_all.41.sums_ref = f32[8,2,1024]{2,1,0:T(2,128)} all-to-all(f32[8,2,1024]{2,1,0:T(2,128)S(1)} %broadcast_in_dim.70), channel_id=1, replica_groups=mesh['dp'=4,'seq'=8] {'seq'}, dimensions={0} | all-to-all | bytes 131072 | tf_op jit(solution)/shard_map/all_to_all | solution.py:1409
  496.7 10.4 %shard_map.275 = (bf16[1024,768]{1,0:T(8,128)(2,1)}, bf16[1024,2048]{1,0:T(8,128)(2,1)}, f32[1,2048]{1,0:T(1,128)}) custom-call(f32[1024,256]{1,0:T(8,128)} %get-tuple-element.242.qg, f32[1024,256]{1,0:T(8,128)} %get-tuple-element.243.kg, bf16[1024,256]{1,0:T(8,128)(2,1)} %get-tuple-element.244.v, f32[1024,768]{1,0:T(8,128)} %get-tuple-element.159.q.k.v, ...), custom_call_target="tpu_custom_call" | custom-call | flops 805306368 | bytes 5526528 | tf_op jit(solution)/shard_map/pallas_call | solution.py:518
  508.0 7.9 %shard_map.276 = (bf16[1,512,768]{2,1,0:T(8,128)(2,1)}, bf16[1,512,768]{2,1,0:T(8,128)(2,1)}, bf16[1,512,768]{2,1,0:T(8,128)(2,1)}, bf16[1,512,768]{2,1,0:T(8,128)(2,1)}) custom-call(bf16[1024,2048]{1,0:T(8,128)(2,1)} %get-tuple-element.263.flat_ref, bf16[1,1024,768]{2,1,0:T(8,128)(2,1)} %bitcast.220), custom_call_target="tpu_custom_call" | custom-call | flops 805306368 | bytes 2228224 | tf_op jit(solution)/shard_map/pallas_call | solution.py:518
  516.7 8.2 %shard_map.277 = (bf16[512,256]{1,0:T(8,128)(2,1)}, bf16[512,256]{1,0:T(8,128)(2,1)}, bf16[512,256]{1,0:T(8,128)(2,1)}, bf16[512,256]{1,0:T(8,128)(2,1)}) custom-call(s32[5]{0:T(128)} %stack.78.order_ref, bf16[8,1024,256]{2,1,0:T(8,128)(2,1)} %bitcast.198, bf16[1024,256]{1,0:T(8,128)(2,1)} %bitcast.214), custom_call_target="tpu_custom_call" | custom-call | flops 268435456 | bytes 1441792 | tf_op jit(solution)/shard_map/pallas_call | solution.py:1231
  (349 shorter events, 230.5 us)
Async XLA Ops:
  7.2 95.2 %all-gather.7.cloned.1.call-start = ((), (), s32[]{:S(2)}) async-start(), calls=%async_computation.11 | async-start | bytes 4718592 | tf_op jit(solution)/shard_map/all_gather | solution.py:1359
  11.1 124.8 %all-gather.11.cloned.1.call-start = ((), (), s32[]{:S(2)}) async-start(), calls=%async_computation.16 | async-start | bytes 1392640 | tf_op jit(solution)/shard_map/all_gather | solution.py:1254
  11.1 49.8 %collective-permute-start.4 = (bf16[2,512,1024]{2,1,0:T(8,128)(2,1)}, bf16[2,512,1024]{2,1,0:T(8,128)(2,1)}, u32[]{:S(2)}, u32[]{:S(2)}) collective-permute-start(bf16[2,512,1024]{2,1,0:T(8,128)(2,1)} %param.28), channel_id=1, source_target_pairs={{0,16},{8,24},{16,0},{24,8},{1,17},{9,25},{17,1},{25,9},{2,18},{10... | collective-permute-start | bytes 6291464 | tf_op jit(solution)/shard_map/ppermute | solution.py:1273
  60.3 38.8 %collective-permute-start.3 = (bf16[2,512,1024]{2,1,0:T(8,128)(2,1)}, bf16[2,512,1024]{2,1,0:T(8,128)(2,1)}, u32[]{:S(2)}, u32[]{:S(2)}) collective-permute-start(bf16[2,512,1024]{2,1,0:T(8,128)(2,1)} %param.28), channel_id=1, source_target_pairs={{0,8},{8,0},{16,24},{24,16},{1,9},{9,1},{17,25},{25,17},{2,10},{10... | collective-permute-start | bytes 6291464 | tf_op jit(solution)/shard_map/ppermute | solution.py:1273
  60.9 38.2 %collective-permute-start.5 = (bf16[2,512,1024]{2,1,0:T(8,128)(2,1)}, bf16[2,512,1024]{2,1,0:T(8,128)(2,1)}, u32[]{:S(2)}, u32[]{:S(2)}) collective-permute-start(bf16[2,512,1024]{2,1,0:T(8,128)(2,1)} %collective-permute-done.4), channel_id=1, source_target_pairs={{0,8},{8,0},{16,24},{24,16},{1,9},{9,1},{17,25},{25,17},{2,10},{10... | collective-permute-start | bytes 6291464 | tf_op jit(solution)/shard_map/ppermute | solution.py:1273
  60.9 75.0 %collective-permute-start.6 = (bf16[2,512,1024]{2,1,0:T(8,128)(2,1)}, bf16[2,512,1024]{2,1,0:T(8,128)(2,1)}, u32[]{:S(2)}, u32[]{:S(2)}) collective-permute-start(bf16[2,512,1024]{2,1,0:T(8,128)(2,1)} %param.29), channel_id=1, source_target_pairs={{0,16},{8,24},{16,0},{24,8},{1,17},{9,25},{17,1},{25,9},{2,18},{10... | collective-permute-start | bytes 6291464 | tf_op jit(solution)/shard_map/ppermute | solution.py:1273
  116.7 95.3 %all-gather.13.cloned.1.call-start = ((), (), s32[]{:S(2)}) async-start(), calls=%async_computation.17 | async-start | bytes 4718592 | tf_op jit(solution)/shard_map/all_gather | solution.py:1417
  135.9 149.8 %all-gather.9.cloned.1.call-start = ((), (), s32[]{:S(2)}) async-start(), calls=%async_computation.12 | async-start | bytes 4718592 | tf_op jit(solution)/shard_map/all_gather | solution.py:1442
  136.0 37.5 %collective-permute-start.10 = (bf16[2,512,1024]{2,1,0:T(8,128)(2,1)}, bf16[2,512,1024]{2,1,0:T(8,128)(2,1)}, u32[]{:S(2)}, u32[]{:S(2)}) collective-permute-start(bf16[2,512,1024]{2,1,0:T(8,128)(2,1)} %param.29), channel_id=1, source_target_pairs={{0,8},{8,0},{16,24},{24,16},{1,9},{9,1},{17,25},{25,17},{2,10},{10... | collective-permute-start | bytes 6291464 | tf_op jit(solution)/shard_map/ppermute | solution.py:1273
  136.1 32.8 %collective-permute-start.7 = (bf16[4,64,2176]{2,1,0:T(8,128)(2,1)}, bf16[4,64,2176]{2,1,0:T(8,128)(2,1)S(1)}, u32[]{:S(2)}, u32[]{:S(2)}) collective-permute-start(bf16[4,64,2176]{2,1,0:T(8,128)(2,1)} %bitcast.221), channel_id=1, source_target_pairs={{0,1},{1,0},{2,3},{3,2},{4,5},{5,4},{6,7},{7,6},{8,9},{9,8},{10,11... | collective-permute-start | bytes 3342344 | tf_op jit(solution)/shard_map/ppermute | solution.py:1249
  137.3 31.6 %collective-permute-start.8 = (bf16[4,64,2176]{2,1,0:T(8,128)(2,1)}, bf16[4,64,2176]{2,1,0:T(8,128)(2,1)S(1)}, u32[]{:S(2)}, u32[]{:S(2)}) collective-permute-start(bf16[4,64,2176]{2,1,0:T(8,128)(2,1)} %bitcast.222), channel_id=1, source_target_pairs={{0,16},{8,24},{16,0},{24,8},{1,17},{9,25},{17,1},{25,9},{2,18},{10... | collective-permute-start | bytes 3342344 | tf_op jit(solution)/shard_map/ppermute | solution.py:1273
  212.0 208.7 %reduce-scatter.4.cloned.1.call-start = ((), (), s32[]{:S(2)}) async-start(), calls=%async_computation.13 | async-start | bytes 4718592 | tf_op jit(solution)/shard_map/reduce_scatter | solution.py:1462
  212.6 46.9 %collective-permute-start.14 = (bf16[2,1024,512]{2,1,0:T(8,128)(2,1)}, bf16[2,1024,512]{2,1,0:T(8,128)(2,1)S(1)}, u32[]{:S(2)}, u32[]{:S(2)}) collective-permute-start(bf16[2,1024,512]{2,1,0:T(8,128)(2,1)} %param.30), channel_id=1, source_target_pairs={{0,16},{8,24},{16,0},{24,8},{1,17},{9,25},{17,1},{25,9},{2,18},{10... | collective-permute-start | bytes 6291464 | tf_op jit(solution)/shard_map/ppermute | solution.py:1273
  214.2 47.5 %collective-permute-start.15 = (bf16[2,1024,512]{2,1,0:T(8,128)(2,1)}, bf16[2,1024,512]{2,1,0:T(8,128)(2,1)}, u32[]{:S(2)}, u32[]{:S(2)}) collective-permute-start(bf16[2,1024,512]{2,1,0:T(8,128)(2,1)} %param.30), channel_id=1, source_target_pairs={{0,8},{8,0},{16,24},{24,16},{1,9},{9,1},{17,25},{25,17},{2,10},{10... | collective-permute-start | bytes 6291464 | tf_op jit(solution)/shard_map/ppermute | solution.py:1273
  285.7 46.4 %collective-permute-start.17 = (bf16[512,2048]{1,0:T(8,128)(2,1)}, bf16[512,2048]{1,0:T(8,128)(2,1)S(1)}, u32[]{:S(2)}, u32[]{:S(2)}) collective-permute-start(bf16[512,2048]{1,0:T(8,128)(2,1)} %get-tuple-element.206), channel_id=1, source_target_pairs={{0,1},{1,0},{2,3},{3,2},{4,5},{5,4},{6,7},{7,6},{8,9},{9,8},{10,11... | collective-permute-start | bytes 6291464 | tf_op jit(solution)/shard_map/ppermute | solution.py:1249
  368.7 29.4 %collective-permute-start.20 = (bf16[2,512,1024]{2,1,0:T(8,128)(2,1)}, bf16[2,512,1024]{2,1,0:T(8,128)(2,1)}, u32[]{:S(2)}, u32[]{:S(2)}) collective-permute-start(bf16[2,512,1024]{2,1,0:T(8,128)(2,1)} %get-tuple-element.221), channel_id=1, source_target_pairs={{0,8},{8,0},{16,24},{24,16},{1,9},{9,1},{17,25},{25,17},{2,10},{10... | collective-permute-start | bytes 6291464 | tf_op jit(solution)/shard_map/ppermute | solution.py:1273
  369.0 34.6 %collective-permute-start.23 = (bf16[2,512,1024]{2,1,0:T(8,128)(2,1)}, bf16[2,512,1024]{2,1,0:T(8,128)(2,1)}, u32[]{:S(2)}, u32[]{:S(2)}) collective-permute-start(bf16[2,512,1024]{2,1,0:T(8,128)(2,1)} %get-tuple-element.228), channel_id=1, source_target_pairs={{0,8},{8,0},{16,24},{24,16},{1,9},{9,1},{17,25},{25,17},{2,10},{10... | collective-permute-start | bytes 6291464 | tf_op jit(solution)/shard_map/ppermute | solution.py:1273
  372.2 35.5 %collective-permute-start.22 = (bf16[2,1024,512]{2,1,0:T(8,128)(2,1)}, bf16[2,1024,512]{2,1,0:T(8,128)(2,1)}, u32[]{:S(2)}, u32[]{:S(2)}) collective-permute-start(bf16[2,1024,512]{2,1,0:T(8,128)(2,1)} %get-tuple-element.226), channel_id=1, source_target_pairs={{0,8},{8,0},{16,24},{24,16},{1,9},{9,1},{17,25},{25,17},{2,10},{10... | collective-permute-start | bytes 6291464 | tf_op jit(solution)/shard_map/ppermute | solution.py:1273
  398.1 38.5 %collective-permute-start.25 = (bf16[1024,512]{1,0:T(8,128)(2,1)}, bf16[1024,512]{1,0:T(8,128)(2,1)}, u32[]{:S(2)}, u32[]{:S(2)}) collective-permute-start(bf16[1024,512]{1,0:T(8,128)(2,1)} %get-tuple-element.235), channel_id=1, source_target_pairs={{0,16},{8,24},{16,0},{24,8},{1,17},{9,25},{17,1},{25,9},{2,18},{10... | collective-permute-start | bytes 3145736 | tf_op jit(solution)/shard_map/ppermute | solution.py:1273
  420.8 30.2 %collective-permute-start.26 = (bf16[512,1024]{1,0:T(8,128)(2,1)}, bf16[512,1024]{1,0:T(8,128)(2,1)}, u32[]{:S(2)}, u32[]{:S(2)}) collective-permute-start(bf16[512,1024]{1,0:T(8,128)(2,1)} %get-tuple-element.236), channel_id=1, source_target_pairs={{0,16},{8,24},{16,0},{24,8},{1,17},{9,25},{17,1},{25,9},{2,18},{10... | collective-permute-start | bytes 3145736 | tf_op jit(solution)/shard_map/ppermute | solution.py:1273
  436.6 70.6 %reduce-scatter.6.cloned.1.call-start = ((), (), s32[]{:S(2)}) async-start(), calls=%async_computation.14 | async-start | bytes 2621440 | tf_op jit(solution)/shard_map/reduce_scatter | solution.py:1267
  453.3 32.2 %all-to-all-start.4 = ((bf16[8,128,256]{2,1,0:T(8,128)(2,1)}), bf16[8,128,256]{2,1,0:T(8,128)(2,1)S(1)}, u32[]{:S(2)}, u32[]{:S(2)}) async-start(bf16[8,128,256]{2,1,0:T(8,128)(2,1)} %bitcast.187), calls=%async_computation.5 | async-start | bytes 1048576 | tf_op jit(solution)/shard_map/all_to_all | solution.py:1483
  456.9 150.4 %reduce-scatter.8.cloned.1.call-start = ((), (), s32[]{:S(2)}) async-start(), calls=%async_computation.15 | async-start | bytes 4718592 | tf_op jit(solution)/shard_map/reduce_scatter | solution.py:1504
  457.0 50.2 %collective-permute-start.28 = (bf16[512,1024]{1,0:T(8,128)(2,1)}, bf16[512,1024]{1,0:T(8,128)(2,1)}, u32[]{:S(2)}, u32[]{:S(2)}) collective-permute-start(bf16[512,1024]{1,0:T(8,128)(2,1)} %get-tuple-element.252), channel_id=1, source_target_pairs={{0,16},{8,24},{16,0},{24,8},{1,17},{9,25},{17,1},{25,9},{2,18},{10... | collective-permute-start | bytes 3145736 | tf_op jit(solution)/shard_map/ppermute | solution.py:1273
  (80 other events, 1150.3 us)
Sparse Core Ops, SparseCore 0:
  11.2 91.1 all-gather.6
  104.6 29.2 all-gather.10
  136.6 75.4 all-gather.12
  214.0 71.6 all-gather.8
  332.2 87.6 reduce-scatter.3
  451.1 52.0 reduce-scatter.5
  507.4 99.9 reduce-scatter.7
